TPU v7x, 32 devices: a whole 2x2x4 slice. The times are simulated.
32 devices in a mesh: fsdp: 4 (over y, core), ctx: 2 (over x), tp: 4 (over z).
Axes of the slice: x: 2, y: 2, z: 4, core: 2. Of those that a mesh axis runs over, the one named last changes fastest.
Arguments:
- tokens: bfloat16 [1024, 8, 768], P('ctx', 'fsdp'), may hold values from -11 to 11
- cotangent: bfloat16 [1024, 8, 768], P(('ctx', 'tp'), 'fsdp'), may hold values from -6 to 6
- segment_ids: int32 [8, 1024], P('fsdp', 'ctx'), may hold values from 0 to 3, never falling along the last dimension, each value on 1 to 512 neighbouring positions
- valid_mask: int32 [8, 1024], P('fsdp', 'ctx'), may hold values from 0 to 1, as said below
- latent_qkv: float32 [768, 3, 768], P('fsdp', None, 'tp'), may hold values from -1 to 1
- latent_out: float32 [768, 768], P('fsdp', 'tp'), may hold values from -1 to 1
- latent_up: float32 [768, 3072], P('fsdp', 'tp'), may hold values from -1 to 1
- latent_down: float32 [768, 3072], P('fsdp', 'tp'), may hold values from -1 to 1
- qkv_quant: float32 [2, 3, 768], P(None, None, 'tp'), may hold values from -0.3 to 2, as said below
- up_quant: float32 [2, 3072], P(None, 'tp'), may hold values from -0.3 to 2, as said below
- out_quant: float32 [2, 768], P(None, 'fsdp'), may hold values from -0.3 to 2, as said below
- down_quant: float32 [2, 768], P(None, 'fsdp'), may hold values from -0.3 to 2, as said below
- bias_qv: float32 [2, 768], P(None, 'tp'), may hold values from -1.5 to 1.5
- bias_up: float32 [3072], P('tp'), may hold values from -1.5 to 1.5
- row_params: float32 [6, 768], replicated, may hold values from -2 to 2, as said below
- clip_in: float32 [768], replicated, may hold values from 2 to 4
- clip_ctx: float32 [768], P('tp'), may hold values from 0.3 to 1.5
- clip_hidden: float32 [3072], P('tp'), may hold values from 1 to 3
- t_qkv: bfloat16 [768, 3, 768], P('fsdp', None, 'tp'), may hold values from -0.21875 to 0.21875
- t_out: bfloat16 [768, 768], P('fsdp', 'tp'), may hold values from -1.75 to 1.75
- t_up: bfloat16 [768, 3072], P('fsdp', 'tp'), may hold values from -0.21875 to 0.21875
- t_down: bfloat16 [768, 3072], P('fsdp', 'tp'), may hold values from -0.109375 to 0.109375
- t_bias_qv: float32 [2, 768], P(None, 'tp'), may hold values from -1.5 to 1.5
- t_bias_up: float32 [3072], P('tp'), may hold values from -1.5 to 1.5
- t_rows: float32 [6, 768], replicated, may hold values from -2 to 2, as said below
Outputs:
- layer_out: bfloat16 [1024, 8, 768], P(('ctx', 'tp'), 'fsdp')
- input_grad: float32 [1024, 8, 768], P(('ctx', 'tp'), 'fsdp')
- grad_qkv: float32 [768, 3, 768], P('fsdp', None, 'tp')
- grad_out: float32 [768, 768], P('fsdp', 'tp')
- grad_up: float32 [768, 3072], P('fsdp', 'tp')
- grad_down: float32 [768, 3072], P('fsdp', 'tp')
- grad_rows: float32 [6, 768], P(None, 'fsdp')
- grad_qv: float32 [2, 768], P(None, 'tp')
- grad_bias_up: float32 [3072], P('tp')
- statistics: float32 [4], replicated
Inputs may be any that keep to these rules, and one draw needn't show every extreme that they name: `valid_mask`: the valid positions of each sequence are its first ones, half of its 1024 positions or more. `segment_ids`: segment numbers never fall along a sequence. `qkv_quant`: row 1 is positive. `up_quant`: row 1 is positive. `out_quant`: row 1 is positive. `down_quant`: row 1 is positive. `row_params`: rows 2 and 4 are positive. `t_rows`: rows 2 and 4 are positive.
All inputs are finite; a program needn't handle non-finite values.
Results may differ from a plain program's by a relative error of at most 0.023.
Values may be sent and summed in bfloat16 or wider, within the bound.
No kernel may reach another device: no remote copies, remote signals or barrier semaphores. Data moves between devices by JAX's collectives and lax.ppermute only.
A program may use at most 192 MiB of HBM per device.

v0:
```python
import math

import jax
import jax.numpy as jnp
from jax import lax
from jax.sharding import PartitionSpec as P

HEAD_DIM = 64


epsilon = 1e-05
floor_score = -1e30


def binarize(latent, shift, scales):
    return (scales * jnp.sign(latent - shift)).astype(jnp.bfloat16)


def straight(summed, latent, shift, scales):
    inside = (jnp.abs(latent - shift) < 1.0).astype(jnp.float32)
    return summed * scales * inside


def layer_norm(stream, gains, biases):
    centred = stream - jnp.mean(stream, axis=-1, keepdims=True)
    spread = jnp.mean(centred * centred, axis=-1, keepdims=True)
    return centred * lax.rsqrt(spread + epsilon) * gains + biases


def exact_gelu(values):
    return jax.nn.gelu(values, approximate=False)


def key_block(count):
    return math.gcd(count, 512)


def headed(array):
    return array.reshape(array.shape[0], array.shape[1], array.shape[2] // HEAD_DIM, HEAD_DIM)


def allowed_pairs(query_seg, query_pos, key_tags, key_pos):
    same = query_seg[:, :, None] == jnp.transpose(key_tags)[:, None, :]
    diagonal = query_pos[:, None] == key_pos[None, :]
    return (same | diagonal[None])[:, None]


def online_step(state, queries, keys, values, allowed, scale):
    running, total, accum = state
    scores = (
        jnp.einsum("tshe,kshe->shtk", queries, keys, preferred_element_type=jnp.float32) * scale
    )
    scores = jnp.where(allowed, scores, floor_score)
    newest = jnp.maximum(running, jnp.max(scores, axis=-1))
    weights = jnp.where(allowed, jnp.exp(scores - newest[..., None]), 0.0)
    factor = jnp.exp(running - newest)
    total = total * factor + jnp.sum(weights, axis=-1)
    accum = accum * factor[..., None] + jnp.einsum(
        "shtk,kshe->shte", weights.astype(jnp.bfloat16), values, preferred_element_type=jnp.float32
    )
    return (newest, total, accum)


def finish(state):
    running, total, accum = state
    merged = accum / total[..., None]
    return (jnp.transpose(merged, (2, 0, 1, 3)), running + jnp.log(total))


def body(
    tokens,
    cotangent,
    segment_ids,
    valid_mask,
    latent_qkv,
    latent_out,
    latent_up,
    latent_down,
    qkv_quant,
    up_quant,
    out_quant,
    down_quant,
    bias_qv,
    bias_up,
    row_params,
    clip_in,
    clip_ctx,
    clip_hidden,
    t_qkv,
    t_out,
    t_up,
    t_down,
    t_bias_qv,
    t_bias_up,
    t_rows,
):
    local_len, seq_count, width = tokens.shape
    share = cotangent.shape[0]
    col_width = latent_qkv.shape[2]
    hidden_width = latent_up.shape[1]
    row_width = latent_qkv.shape[0]
    local_heads = col_width // HEAD_DIM
    scale = HEAD_DIM ** (-0.5)
    tp_rank = lax.axis_index("tp")
    ctx_rank = lax.axis_index("ctx")
    fsdp_rank = lax.axis_index("fsdp")
    full_len = local_len * lax.axis_size("ctx")
    bin_qkv = binarize(latent_qkv, qkv_quant[0][None], qkv_quant[1][None])
    bin_out = binarize(latent_out, out_quant[0][:, None], out_quant[1][:, None])
    bin_up = binarize(latent_up, up_quant[0][None], up_quant[1][None])
    bin_down = binarize(latent_down, down_quant[0][:, None], down_quant[1][:, None])
    gathered = (
        lax.all_gather(bin_qkv, "fsdp", axis=0, tiled=True),
        lax.all_gather(bin_out, "fsdp", axis=0, tiled=True),
        lax.all_gather(bin_up, "fsdp", axis=0, tiled=True),
        lax.all_gather(bin_down, "fsdp", axis=0, tiled=True),
        lax.all_gather(t_qkv, "fsdp", axis=0, tiled=True),
        lax.all_gather(t_out, "fsdp", axis=0, tiled=True),
        lax.all_gather(t_up, "fsdp", axis=0, tiled=True),
        lax.all_gather(t_down, "fsdp", axis=0, tiled=True),
    )
    full_qkv, full_out, full_up, full_down, teach_qkv, teach_out, teach_up, teach_down = gathered
    stream = tokens.astype(jnp.float32)
    a_in = jnp.clip(stream, -clip_in, clip_in).astype(jnp.bfloat16)
    proj_student = jnp.einsum("tsd,dkh->tskh", a_in, full_qkv, preferred_element_type=jnp.float32)
    proj_teacher = jnp.einsum(
        "tsd,dkh->tskh", tokens, teach_qkv, preferred_element_type=jnp.float32
    )
    student_q = (proj_student[:, :, 0] + bias_qv[0]).astype(jnp.bfloat16)
    student_k = proj_student[:, :, 1].astype(jnp.bfloat16)
    student_v = (proj_student[:, :, 2] + bias_qv[1]).astype(jnp.bfloat16)
    teacher_q = (proj_teacher[:, :, 0] + t_bias_qv[0]).astype(jnp.bfloat16)
    teacher_k = proj_teacher[:, :, 1].astype(jnp.bfloat16)
    teacher_v = (proj_teacher[:, :, 2] + t_bias_qv[1]).astype(jnp.bfloat16)
    student_queries = headed(student_q)
    teacher_queries = headed(teacher_q)
    query_pos = ctx_rank * local_len + jnp.arange(local_len, dtype=jnp.int32)
    key_tags = jnp.transpose(jnp.where(valid_mask > 0, segment_ids, -1))
    empty_state = (
        jnp.full((seq_count, local_heads, local_len), floor_score, jnp.float32),
        jnp.zeros((seq_count, local_heads, local_len), jnp.float32),
        jnp.zeros((seq_count, local_heads, local_len, HEAD_DIM), jnp.float32),
    )
    buffers = (
        jnp.zeros((full_len, seq_count, col_width), jnp.bfloat16),
        jnp.zeros((full_len, seq_count, col_width), jnp.bfloat16),
        jnp.zeros((full_len, seq_count), jnp.int32),
    )
    carry = (empty_state, empty_state, buffers)
    pieces = (
        lax.all_gather(student_k, "ctx", axis=0, tiled=True),
        lax.all_gather(student_v, "ctx", axis=0, tiled=True),
        lax.all_gather(teacher_k, "ctx", axis=0, tiled=True),
        lax.all_gather(teacher_v, "ctx", axis=0, tiled=True),
        lax.all_gather(key_tags, "ctx", axis=0, tiled=True),
    )
    start = jnp.int32(0)
    count = pieces[0].shape[0]
    block = key_block(count)

    def inner(states, index):
        offset = index * block
        parts = [lax.dynamic_slice_in_dim(piece, offset, block, 0) for piece in pieces]
        key_pos = offset + jnp.arange(block, dtype=jnp.int32)
        allowed = allowed_pairs(segment_ids, query_pos, parts[4], key_pos)
        states = (
            online_step(
                states[0], student_queries, headed(parts[0]), headed(parts[1]), allowed, scale
            ),
            online_step(
                states[1], teacher_queries, headed(parts[2]), headed(parts[3]), allowed, scale
            ),
        )
        return (states, None)

    states, _ = lax.scan(inner, (carry[0], carry[1]), jnp.arange(count // block, dtype=jnp.int32))
    kept = tuple(
        (
            lax.dynamic_update_slice_in_dim(buffer, piece, start, 0)
            for buffer, piece in zip(carry[2], (pieces[0], pieces[1], pieces[4]))
        )
    )
    student_state, teacher_state, kept = (states[0], states[1], kept)
    attended, log_total = finish(student_state)
    teacher_attended, _ = finish(teacher_state)
    attended_flat = attended.reshape(local_len, seq_count, col_width)
    ctx_ratio = jnp.tanh(attended_flat / clip_ctx)
    context = (clip_ctx * ctx_ratio).astype(jnp.bfloat16)
    teacher_context = teacher_attended.reshape(local_len, seq_count, col_width).astype(jnp.bfloat16)
    rows_student = context
    rows_teacher = teacher_context
    attn_both = lax.psum_scatter(
        jnp.concatenate(
            [
                jnp.einsum(
                    "tsh,dh->tsd", rows_student, full_out, preferred_element_type=jnp.float32
                ),
                jnp.einsum(
                    "tsh,dh->tsd", rows_teacher, teach_out, preferred_element_type=jnp.float32
                ),
            ],
            axis=-1,
        ).astype(jnp.bfloat16),
        "tp",
        scatter_dimension=0,
        tiled=True,
    ).astype(jnp.float32)
    attn_student = attn_both[..., :width] + row_params[0]
    attn_teacher = attn_both[..., width:] + t_rows[0]
    stream_rows = lax.dynamic_slice_in_dim(stream, tp_rank * share, share, 0)
    first_sum = stream_rows + attn_student
    h_one = layer_norm(first_sum, row_params[2], row_params[3])
    h_teacher = layer_norm(stream_rows + attn_teacher, t_rows[2], t_rows[3])
    h_full, h_teacher_full = (
        lax.all_gather(h_one.astype(jnp.bfloat16), "tp", axis=0, tiled=True),
        lax.all_gather(h_teacher.astype(jnp.bfloat16), "tp", axis=0, tiled=True),
    )
    upper = jnp.einsum("tsd,df->tsf", h_full, full_up, preferred_element_type=jnp.float32) + bias_up
    activated = exact_gelu(upper)
    hid_ratio = jnp.tanh(activated / clip_hidden)
    hidden = (clip_hidden * hid_ratio).astype(jnp.bfloat16)
    upper_teacher = (
        jnp.einsum("tsd,df->tsf", h_teacher_full, teach_up, preferred_element_type=jnp.float32)
        + t_bias_up
    )
    hidden_teacher = exact_gelu(upper_teacher).astype(jnp.bfloat16)
    rows_student = hidden
    rows_teacher = hidden_teacher
    ffn_both = lax.psum_scatter(
        jnp.concatenate(
            [
                jnp.einsum(
                    "tsf,df->tsd", rows_student, full_down, preferred_element_type=jnp.float32
                ),
                jnp.einsum(
                    "tsf,df->tsd", rows_teacher, teach_down, preferred_element_type=jnp.float32
                ),
            ],
            axis=-1,
        ).astype(jnp.bfloat16),
        "tp",
        scatter_dimension=0,
        tiled=True,
    ).astype(jnp.float32)
    ffn_student = ffn_both[..., :width] + row_params[1]
    ffn_teacher = ffn_both[..., width:] + t_rows[1]
    second_sum = h_one + ffn_student
    out = layer_norm(second_sum, row_params[4], row_params[5])
    teacher_out = layer_norm(h_teacher + ffn_teacher, t_rows[4], t_rows[5])
    layer_out = out.astype(jnp.bfloat16)
    valid_rows = jnp.transpose(
        lax.dynamic_slice_in_dim(valid_mask, tp_rank * share, share, 1)
    ).astype(jnp.float32)[..., None]
    difference = out - teacher_out
    grad_out_total = cotangent.astype(jnp.float32) + valid_rows * difference
    stat_terms = jnp.stack(
        [
            jnp.sum(valid_rows) + 0.0 * jnp.sum(stream_rows[:1, :1, :1]),
            jnp.sum(valid_rows * stream_rows * stream_rows),
            jnp.sum(valid_rows * attn_student * attn_student),
            jnp.sum(valid_rows * ffn_student * ffn_student),
            jnp.sum(valid_rows * difference * difference),
        ]
    )
    _, second_pull = jax.vjp(layer_norm, second_sum, row_params[4], row_params[5])
    d_second, d_gain_two, d_bias_two = second_pull(grad_out_total)
    d_ffn = d_second.astype(jnp.bfloat16)
    d_bias_down = jnp.sum(d_ffn.astype(jnp.float32), axis=(0, 1))
    d_ffn_full = lax.all_gather(d_ffn, "tp", axis=0, tiled=True)
    grad_bin_down = jnp.einsum(
        "tsd,tsf->df", d_ffn_full, hidden, preferred_element_type=jnp.float32
    )
    d_hidden = jnp.einsum("tsd,df->tsf", d_ffn_full, full_down, preferred_element_type=jnp.float32)
    d_hidden = d_hidden * (1.0 - hid_ratio * hid_ratio)
    _, gelu_pull = jax.vjp(exact_gelu, upper)
    d_upper = gelu_pull(d_hidden)[0].astype(jnp.bfloat16)
    d_bias_up = jnp.sum(d_upper.astype(jnp.float32), axis=(0, 1))
    grad_bin_up = jnp.einsum("tsd,tsf->df", h_full, d_upper, preferred_element_type=jnp.float32)
    rows = d_upper
    d_h_one = d_second + lax.psum_scatter(
        jnp.einsum("tsf,df->tsd", rows, full_up, preferred_element_type=jnp.float32).astype(
            jnp.bfloat16
        ),
        "tp",
        scatter_dimension=0,
        tiled=True,
    ).astype(jnp.float32)
    _, first_pull = jax.vjp(layer_norm, first_sum, row_params[2], row_params[3])
    d_first, d_gain_one, d_bias_one = first_pull(d_h_one)
    d_attn = d_first.astype(jnp.bfloat16)
    d_bias_out = jnp.sum(d_attn.astype(jnp.float32), axis=(0, 1))
    d_attn_full = lax.all_gather(d_attn, "tp", axis=0, tiled=True)
    grad_bin_out = jnp.einsum(
        "tsd,tsh->dh", d_attn_full, context, preferred_element_type=jnp.float32
    )
    d_context = jnp.einsum("tsd,dh->tsh", d_attn_full, full_out, preferred_element_type=jnp.float32)
    d_attended = (d_context * (1.0 - ctx_ratio * ctx_ratio)).astype(jnp.bfloat16)
    d_attended_heads = headed(d_attended)
    delta = jnp.transpose(
        jnp.sum(d_attended_heads.astype(jnp.float32) * attended, axis=-1), (1, 2, 0)
    )
    key_all, value_all, tag_all = kept
    back_block = key_block(full_len)

    def back_step(grad_q, index):
        offset = index * back_block
        keys = headed(lax.dynamic_slice_in_dim(key_all, offset, back_block, 0))
        values = headed(lax.dynamic_slice_in_dim(value_all, offset, back_block, 0))
        block_tags = lax.dynamic_slice_in_dim(tag_all, offset, back_block, 0)
        key_pos = offset + jnp.arange(back_block, dtype=jnp.int32)
        allowed = allowed_pairs(segment_ids, query_pos, block_tags, key_pos)
        current = grad_q
        scores = (
            jnp.einsum("tshe,kshe->shtk", student_queries, keys, preferred_element_type=jnp.float32)
            * scale
        )
        probs = jnp.where(allowed, jnp.exp(scores - log_total[..., None]), 0.0)
        d_probs = jnp.einsum(
            "tshe,kshe->shtk", d_attended_heads, values, preferred_element_type=jnp.float32
        )
        d_scores = (probs * (d_probs - delta[..., None])).astype(jnp.bfloat16)
        current = (
            current
            + jnp.einsum("shtk,kshe->shte", d_scores, keys, preferred_element_type=jnp.float32)
            * scale
        )
        grad_k = (
            jnp.einsum(
                "shtk,tshe->kshe", d_scores, student_queries, preferred_element_type=jnp.float32
            )
            * scale
        )
        grad_v = jnp.einsum(
            "shtk,tshe->kshe",
            probs.astype(jnp.bfloat16),
            d_attended_heads,
            preferred_element_type=jnp.float32,
        )
        joined = jnp.concatenate(
            [
                grad_k.reshape(back_block, seq_count, col_width),
                grad_v.reshape(back_block, seq_count, col_width),
            ],
            axis=-1,
        )
        return (current, joined)

    grad_q, key_terms = lax.scan(
        back_step,
        jnp.zeros((seq_count, local_heads, local_len, HEAD_DIM), jnp.float32),
        jnp.arange(full_len // back_block, dtype=jnp.int32),
    )
    key_terms = key_terms.reshape(full_len, seq_count, 2 * col_width)
    key_sums = lax.psum_scatter(
        key_terms.astype(jnp.bfloat16), "ctx", scatter_dimension=0, tiled=True
    ).astype(jnp.float32)
    grad_q_flat = jnp.transpose(grad_q, (2, 0, 1, 3)).reshape(local_len, seq_count, col_width)
    d_proj = jnp.stack(
        [grad_q_flat, key_sums[..., :col_width], key_sums[..., col_width:]], axis=2
    ).astype(jnp.bfloat16)
    d_bias_qv = jnp.stack(
        [
            jnp.sum(d_proj[:, :, 0].astype(jnp.float32), axis=(0, 1)),
            jnp.sum(d_proj[:, :, 2].astype(jnp.float32), axis=(0, 1)),
        ]
    )
    grad_bin_qkv = jnp.einsum("tsd,tskh->dkh", a_in, d_proj, preferred_element_type=jnp.float32)
    rows = d_proj
    through = lax.psum_scatter(
        jnp.einsum("tskh,dkh->tsd", rows, full_qkv, preferred_element_type=jnp.float32).astype(
            jnp.bfloat16
        ),
        "tp",
        scatter_dimension=0,
        tiled=True,
    ).astype(jnp.float32)
    input_grad = d_first + through * (jnp.abs(stream_rows) < clip_in).astype(jnp.float32)
    shards = (
        lax.psum_scatter(
            grad_bin_qkv.astype(jnp.bfloat16), "fsdp", scatter_dimension=0, tiled=True
        ).astype(jnp.float32),
        lax.psum_scatter(
            grad_bin_out.astype(jnp.bfloat16), "fsdp", scatter_dimension=0, tiled=True
        ).astype(jnp.float32),
        lax.psum_scatter(
            grad_bin_up.astype(jnp.bfloat16), "fsdp", scatter_dimension=0, tiled=True
        ).astype(jnp.float32),
        lax.psum_scatter(
            grad_bin_down.astype(jnp.bfloat16), "fsdp", scatter_dimension=0, tiled=True
        ).astype(jnp.float32),
    )
    summed = (
        lax.psum(shards[0].astype(jnp.bfloat16), "ctx").astype(jnp.float32),
        lax.psum(shards[1].astype(jnp.bfloat16), "ctx").astype(jnp.float32),
        lax.psum(shards[2].astype(jnp.bfloat16), "ctx").astype(jnp.float32),
        lax.psum(shards[3].astype(jnp.bfloat16), "ctx").astype(jnp.float32),
    )
    grad_qkv = straight(summed[0], latent_qkv, qkv_quant[0][None], qkv_quant[1][None])
    grad_out = straight(summed[1], latent_out, out_quant[0][:, None], out_quant[1][:, None])
    grad_up = straight(summed[2], latent_up, up_quant[0][None], up_quant[1][None])
    grad_down = straight(summed[3], latent_down, down_quant[0][:, None], down_quant[1][:, None])
    vector_grads = jnp.stack(
        [d_bias_out, d_bias_down, d_gain_one, d_bias_one, d_gain_two, d_bias_two]
    )
    placed_qv = lax.dynamic_update_slice_in_dim(
        jnp.zeros((2, width), jnp.float32), d_bias_qv, tp_rank * col_width, 1
    )
    placed_up = lax.dynamic_update_slice_in_dim(
        jnp.zeros((hidden_width * lax.axis_size("tp"),), jnp.float32),
        d_bias_up,
        tp_rank * hidden_width,
        0,
    )
    stat_sums, vector_sums, qv_sums, up_sums = lax.psum(
        (stat_terms, vector_grads, placed_qv, placed_up), ("fsdp", "ctx", "tp")
    )
    grad_rows = lax.dynamic_slice_in_dim(vector_sums, fsdp_rank * row_width, row_width, 1)
    grad_qv = lax.dynamic_slice_in_dim(qv_sums, tp_rank * col_width, col_width, 1)
    grad_bias_up = lax.dynamic_slice_in_dim(up_sums, tp_rank * hidden_width, hidden_width, 0)
    denom = stat_sums[0] * width
    statistics = jnp.stack(
        [
            jnp.sqrt(stat_sums[1] / denom),
            jnp.sqrt(stat_sums[2] / denom),
            jnp.sqrt(stat_sums[3] / denom),
            stat_sums[4] / denom,
        ]
    )
    return (
        layer_out,
        input_grad,
        grad_qkv,
        grad_out,
        grad_up,
        grad_down,
        grad_rows,
        grad_qv,
        grad_bias_up,
        statistics,
    )


def solution(mesh):
    return jax.shard_map(
        body,
        mesh=mesh,
        in_specs=(
            P("ctx", "fsdp", None),
            P(("ctx", "tp"), "fsdp", None),
            P("fsdp", "ctx"),
            P("fsdp", "ctx"),
            P("fsdp", None, "tp"),
            P("fsdp", "tp"),
            P("fsdp", "tp"),
            P("fsdp", "tp"),
            P(None, None, "tp"),
            P(None, "tp"),
            P(None, "fsdp"),
            P(None, "fsdp"),
            P(None, "tp"),
            P("tp"),
            P(),
            P(),
            P("tp"),
            P("tp"),
            P("fsdp", None, "tp"),
            P("fsdp", "tp"),
            P("fsdp", "tp"),
            P("fsdp", "tp"),
            P(None, "tp"),
            P("tp"),
            P(),
        ),
        out_specs=(
            P(("ctx", "tp"), "fsdp", None),
            P(("ctx", "tp"), "fsdp", None),
            P("fsdp", None, "tp"),
            P("fsdp", "tp"),
            P("fsdp", "tp"),
            P("fsdp", "tp"),
            P(None, "fsdp"),
            P(None, "tp"),
            P("tp"),
            P(),
        ),
        check_vma=False,
    )
```

profile of v0, /device:TPU:0, one launch (start us, length us, event | category | flops | bytes accessed | tf_op | source)
XLA Modules:
  0.0 835.3 jit_solution(1516105437006764085)
XLA Ops:
  10.6 14.3 %all_gather.52 = bf16[768,3,192]{2,1,0:T(4,128)(2,1)S(1)} all-gather(bf16[192,3,192]{2,1,0:T(4,128)(2,1)S(1)} %multiply_convert_fusion.2), channel_id=1, replica_groups=mesh['fsdp'=4,'ctx'=2,'tp'=4] {'fsdp'}, dimensions={0}, use_global_device_ids=true | all-gather | bytes 1105920 | tf_op jit(solution)/shard_map/all_gather | solution.py:113
  25.9 2.6 fusion.71
  30.4 13.0 %all_gather.55 = bf16[768,3,192]{2,1,0:T(4,128)(2,1)S(1)} all-gather(bf16[192,3,192]{2,1,0:T(4,128)(2,1)S(1)} %copy.89), channel_id=1, replica_groups=mesh['fsdp'=4,'ctx'=2,'tp'=4] {'fsdp'}, dimensions={0}, use_global_device_ids=true | all-gather | bytes 1105920 | tf_op jit(solution)/shard_map/all_gather | solution.py:117
  43.4 2.1 copy.91
  45.5 2.8 fusion.55
  50.7 4.3 all_gather.51
  55.1 11.0 %all-gather = bf16[1024,2,1,192]{0,3,2,1:T(8,128)(2,1)} all-gather(bf16[512,2,1,192]{0,3,2,1:T(8,128)(2,1)S(1)} %slice.245), channel_id=2, replica_groups=mesh['fsdp'=4,'ctx'=2,'tp'=4] {'ctx'}, dimensions={0}, use_global_device_ids=true | all-gather | bytes 1179648 | tf_op jit(solution)/shard_map/all_gather | solution.py:151
  67.5 10.1 %all_gather.54 = bf16[1024,2,192]{0,2,1:T(8,128)(2,1)} all-gather(bf16[512,2,192]{0,2,1:T(8,128)(2,1)S(1)} %fusion.82), channel_id=1, replica_groups=mesh['fsdp'=4,'ctx'=2,'tp'=4] {'ctx'}, dimensions={0}, use_global_device_ids=true | all-gather | bytes 1179648 | tf_op jit(solution)/shard_map/all_gather | solution.py:152
  77.6 9.0 %all-gather.1 = bf16[1024,2,1,192]{0,3,2,1:T(8,128)(2,1)S(1)} all-gather(bf16[512,2,1,192]{0,3,2,1:T(8,128)(2,1)S(1)} %slice.244), channel_id=3, replica_groups=mesh['fsdp'=4,'ctx'=2,'tp'=4] {'ctx'}, dimensions={0}, use_global_device_ids=true | all-gather | bytes 1179648 | tf_op jit(solution)/shard_map/all_gather | solution.py:153
  88.0 8.6 %all_gather.57 = bf16[1024,2,192]{0,2,1:T(8,128)(2,1)S(1)} all-gather(bf16[512,2,192]{0,2,1:T(8,128)(2,1)S(1)} %fusion.80), channel_id=1, replica_groups=mesh['fsdp'=4,'ctx'=2,'tp'=4] {'ctx'}, dimensions={0}, use_global_device_ids=true | all-gather | bytes 1179648 | tf_op jit(solution)/shard_map/all_gather | solution.py:154
  98.0 44.7 %while.34 = (s32[]{:T(128)}, f32[2,3,512]{2,1,0:T(4,128)S(1)}, f32[2,3,512]{2,1,0:T(4,128)S(1)}, f32[2,3,512,64]{2,3,1,0:T(8,128)}, f32[2,3,512]{2,1,0:T(4,128)S...) while((s32[]{:T(128)}, f32[2,3,512]{2,1,0:T(4,128)S(1)}, ...), condition=%wide.region_5.6_spmd.clone, body=%wide.region_0.5_spmd.clone.sunk | while | flops 848722944 | bytes 138043920 | solution.py:176
  102.1 4.7 fusion.225
  106.8 7.2 fusion.226
  115.4 1.9 fusion.228
  117.6 1.9 fusion.229
  124.5 4.7 fusion.225
  129.2 7.2 fusion.226
  137.8 1.9 fusion.228
  139.9 1.9 fusion.229
  142.7 6.3 all_gather.59
  149.7 6.6 all_gather.58
  159.2 1.9 pad_maximum_fusion
  163.4 3.3 copy_convert_fusion
  166.7 55.8 %reduce-scatter.12.cloned.1.call-done = bf16[128,2,1536]{2,0,1:T(8,128)(2,1)} async-done(((bf16[512,2,1536]{2,0,1:T(8,128)(2,1)}), bf16[128,2,1536]{2,0,1:T(8,128)(2,1)}) %reduce-scatter.12.cloned.1.call-update) | async-done | bytes 786448 | tf_op jit(solution)/shard_map/reduce_scatter | solution.py:192
  227.8 2.0 multiply_convert_fusion.3
  232.9 31.9 %all-gather.11.cloned.1.call-done = bf16[512,2,768]{2,0,1:T(8,128)(2,1)} async-done(((bf16[128,2,768]{2,0,1:T(8,128)(2,1)}), bf16[512,2,768]{2,0,1:T(8,128)(2,1)}) %all-gather.11.cloned.1.call-update) | async-done | bytes 1572880 | tf_op jit(solution)/shard_map/all_gather | solution.py:215
  264.8 11.5 %multiply_convert_fusion = (bf16[512,2,768]{2,0,1:T(8,128)(2,1)}, f32[512,2,768]{2,0,1:T(8,128)}, f32[512,2,768]{2,0,1:T(8,128)}) fusion(f32[768]{0:T(1024)S(1)} %copy-done.80, f32[768]{0:T(1024)S(1)} %copy-done.81, bf16[512,2,768]{2,0,1:T(8,128)(2,1)} %all-gather.11.cloned.1.call-done, bf16[768,768]{1,0:T(8,128)(2,1)} %all-gather.13.cloned.1.call-done), kind=kOutput, calls=%fused_computation.92 | convolution fusion | flops 1261436928 | bytes 10622976 | tf_op jit(solution)/shard_map/tsd,df->tsf/dot_general | solution.py:218
  276.3 6.7 all-gather.15.cloned.1.call-done
  283.0 4.3 convolution_convert_fusion.2
  287.3 14.6 %all-gather.19.cloned.1.call-done = bf16[768,768]{1,0:T(8,128)(2,1)} async-done(((bf16[192,768]{1,0:T(8,128)(2,1)}), bf16[768,768]{1,0:T(8,128)(2,1)}) %all-gather.19.cloned.1.call-update) | async-done | bytes 1179664 | tf_op jit(solution)/shard_map/all_gather | solution.py:119
  301.9 39.1 %all-gather.17.cloned.1.call-done = bf16[512,2,768]{2,0,1:T(8,128)(2,1)} async-done(((bf16[128,2,768]{2,0,1:T(8,128)(2,1)}), bf16[512,2,768]{2,0,1:T(8,128)(2,1)}) %all-gather.17.cloned.1.call-update) | async-done | bytes 1572880 | tf_op jit(solution)/shard_map/all_gather | solution.py:216
  341.0 6.4 fusion.86
  347.4 11.4 %all-gather.21.cloned.1.call-done = bf16[768,768]{1,0:T(8,128)(2,1)} async-done(((bf16[192,768]{1,0:T(8,128)(2,1)}), bf16[768,768]{1,0:T(8,128)(2,1)}) %all-gather.21.cloned.1.call-update) | async-done | bytes 1179664 | tf_op jit(solution)/shard_map/all_gather | solution.py:120
  358.8 10.6 %convolution_convert_fusion.1 = bf16[512,2,768]{2,0,1:T(8,128)(2,1)S(1)} fusion(f32[512,2,768]{2,0,1:T(8,128)} %get-tuple-element.460, f32[768]{0:T(1024)S(1)} %copy-done.79, bf16[768,768]{1,0:T(8,128)(2,1)} %all-gather.21.cloned.1.call-done, u8[512,768]{1,0:T(8,128)(4,1)} %get-tuple-element.313, u8[512,768]{1,0:T(8,128)(4,1)} %get-tuple-element.312), kind=kOutput, calls=%fused_computation.112 | convolution fusion | flops 1264582656 | bytes 6687744 | tf_op jit(solution)/shard_map/tsf,df->tsd/dot_general | solution.py:235
  369.4 1.9 pad_maximum_fusion.1
  372.0 59.7 %reduce-scatter.14.cloned.1.call-done = bf16[128,2,1536]{2,0,1:T(8,128)(2,1)} async-done(((bf16[512,2,1536]{2,0,1:T(8,128)(2,1)}), bf16[128,2,1536]{2,0,1:T(8,128)(2,1)}) %reduce-scatter.14.cloned.1.call-update) | async-done | bytes 786448 | tf_op jit(solution)/shard_map/reduce_scatter | solution.py:229
  434.5 2.8 fusion.139
  440.3 37.0 %all-gather.23.cloned.1.call-done = bf16[512,2,768]{2,0,1:T(8,128)(2,1)} async-done(((bf16[128,2,768]{2,0,1:T(8,128)(2,1)}), bf16[512,2,768]{2,0,1:T(8,128)(2,1)}) %all-gather.23.cloned.1.call-update) | async-done | bytes 1572880 | tf_op jit(solution)/shard_map/all_gather | solution.py:269
  477.3 7.1 convert_reduce_fusion
  485.6 2.6 convolution_convert_fusion
  488.2 34.2 %reduce-scatter.16.cloned.1.call-done = bf16[128,2,768]{2,0,1:T(8,128)(2,1)} async-done(((bf16[512,2,768]{2,0,1:T(8,128)(2,1)}), bf16[128,2,768]{2,0,1:T(8,128)(2,1)}) %reduce-scatter.16.cloned.1.call-update) | async-done | bytes 393232 | tf_op jit(solution)/shard_map/reduce_scatter | solution.py:280
  522.5 2.0 multiply_reduce_fusion.1
  529.2 35.2 %all-gather.25.cloned.1.call-done = bf16[512,2,768]{2,0,1:T(8,128)(2,1)} async-done(((bf16[128,2,768]{2,0,1:T(8,128)(2,1)}), bf16[512,2,768]{2,0,1:T(8,128)(2,1)}) %all-gather.25.cloned.1.call-update) | async-done | bytes 1572880 | tf_op jit(solution)/shard_map/all_gather | solution.py:292
  564.4 2.8 fusion.59
  569.5 36.4 %while.35 = (s32[]{:T(128)}, f32[2,3,512,64]{2,3,1,0:T(8,128)}, bf16[2,512,2,384]{1,3,2,0:T(8,128)(2,1)}, s32[2,512]{1,0:T(2,128)S(1)}, s32[2]{0:T(128)}, /*inde...) while((s32[]{:T(128)}, f32[2,3,512,64]{2,3,1,0:T(8,128)}, ...), condition=%wide.region_23.24_spmd.clone, body=%wide.region_22.23_spmd.clone.sunk | while | flops 1026229248 | bytes 82391544 | solution.py:348
  574.4 3.6 fusion.241
  578.1 2.6 fusion.242
  580.7 4.3 fusion.243
  592.5 3.6 fusion.241
  596.2 2.8 fusion.242
  599.0 4.3 fusion.243
  605.9 2.9 copy.131
  609.0 25.0 %reduce-scatter.18.cloned.1.call-done = bf16[512,2,384]{0,2,1:T(8,128)(2,1)} async-done(((bf16[1024,2,384]{0,2,1:T(8,128)(2,1)}), bf16[512,2,384]{0,2,1:T(8,128)(2,1)}) %reduce-scatter.18.cloned.1.call-update) | async-done | bytes 786448 | tf_op jit(solution)/shard_map/reduce_scatter | solution.py:354
  638.4 2.3 reshape.309
  640.8 4.3 bitcast_convert_fusion.3
  645.4 4.6 bitcast_convert_fusion.2
  651.7 13.6 %reduce-scatter.28.cloned.1.call-done = bf16[192,576]{1,0:T(8,128)(2,1)} async-done(((bf16[768,576]{1,0:T(8,128)(2,1)}), bf16[192,576]{1,0:T(8,128)(2,1)}) %reduce-scatter.28.cloned.1.call-update) | async-done | bytes 221200
  667.3 26.2 %reduce-scatter.24.cloned.1.call-done = bf16[192,768]{1,0:T(8,128)(2,1)} async-done(((bf16[768,768]{1,0:T(8,128)(2,1)}), bf16[192,768]{1,0:T(8,128)(2,1)}) %reduce-scatter.24.cloned.1.call-update) | async-done | bytes 294928 | tf_op jit(solution)/shard_map/reduce_scatter | solution.py:385
  693.5 28.3 %reduce-scatter.26.cloned.1.call-done = bf16[192,768]{1,0:T(8,128)(2,1)} async-done(((bf16[768,768]{1,0:T(8,128)(2,1)}), bf16[192,768]{1,0:T(8,128)(2,1)}) %reduce-scatter.26.cloned.1.call-update) | async-done | bytes 294928 | tf_op jit(solution)/shard_map/reduce_scatter | solution.py:388
  721.8 23.8 %reduce-scatter.22.cloned.1.call-done = bf16[192,192]{1,0:T(8,128)(2,1)} async-done(((bf16[768,192]{1,0:T(8,128)(2,1)}), bf16[192,192]{1,0:T(8,128)(2,1)}) %reduce-scatter.22.cloned.1.call-update) | async-done | bytes 73744 | tf_op jit(solution)/shard_map/reduce_scatter | solution.py:382
  745.7 4.3 bitcast_convert_fusion
  756.8 2.6 stack.85
  762.8 40.0 %all-reduce = (f32[6,768]{1,0:T(8,128)S(1)}, f32[2,768]{1,0:T(2,128)S(1)}, f32[3072]{0:T(1024)S(1)}, f32[5]{0:T(128)S(1)}) all-reduce(f32[6,768]{1,0:T(8,128)S(1)} %stack.76, f32[2,768]{1,0:T(2,128)S(1)} %dynamic_update_slice.10, f32[3072]{0:T(1024)S(1)} %dynamic_update_slice.11, ...), channel_id=1, replica_groups=mesh['fsdp'=4,'ctx'=2,'tp'=4] {'fsdp','ctx','tp'}, use_global_device_ids=true, to_apply=%region_40.41 | all-reduce | flops 9221 | bytes 73768 | tf_op jit(solution)/shard_map/psum | solution.py:414
  816.1 8.6 %reduce-scatter.20.cloned.1.call-done = bf16[128,2,768]{2,0,1:T(8,128)(2,1)} async-done(((bf16[512,2,768]{2,0,1:T(8,128)(2,1)}), bf16[128,2,768]{2,0,1:T(8,128)(2,1)}) %reduce-scatter.20.cloned.1.call-update) | async-done | bytes 393232 | tf_op jit(solution)/shard_map/reduce_scatter | solution.py:369
  (397 shorter events, 95.5 us)
Async XLA Ops:
  8.0 17.8 %copy-start.54 = (f32[768]{0:T(1024)S(1)}, f32[768]{0:T(1024)}, u32[]{:S(2)}) copy-start(f32[768]{0:T(1024)} %param.44) | copy-start | bytes 9220
  8.0 214.4 %reduce-scatter.12.cloned.1.call-start = ((), (), s32[]{:S(2)}) async-start(), calls=%async_computation.9 | async-start | bytes 3932160 | tf_op jit(solution)/shard_map/reduce_scatter | solution.py:192
  8.9 19.6 %copy-start.45 = (f32[3,192]{1,0:T(4,128)}, f32[3,192]{1,0:T(4,128)S(1)}, u32[]{:S(2)}) copy-start(f32[3,192]{1,0:T(4,128)S(1)} %get-tuple-element.463) | copy-start | bytes 6916
  8.9 19.6 %copy-start.47 = (f32[3,192]{1,0:T(4,128)}, f32[3,192]{1,0:T(4,128)S(1)}, u32[]{:S(2)}) copy-start(f32[3,192]{1,0:T(4,128)S(1)} %get-tuple-element.464) | copy-start | bytes 6916
  45.5 5.2 copy-start.37
  45.5 5.2 copy-start.65
  48.3 17.7 %copy-start.76 = (f32[2,192]{1,0:T(2,128)S(1)}, f32[2,192]{1,0:T(2,128)}, u32[]{:S(2)}) copy-start(f32[2,192]{1,0:T(2,128)} %param.51) | copy-start | bytes 4612
  48.4 17.7 %copy-start.77 = (f32[2,192]{1,0:T(2,128)S(1)}, f32[2,192]{1,0:T(2,128)}, u32[]{:S(2)}) copy-start(f32[2,192]{1,0:T(2,128)} %param.41) | copy-start | bytes 4612
  66.1 30.5 %copy-start.19 = (f32[512,2,1,192]{0,3,2,1:T(8,128)S(1)}, f32[512,2,1,192]{0,3,2,1:T(8,128)}, u32[]{:S(2)}) copy-start(f32[512,2,1,192]{0,3,2,1:T(8,128)} %slice.185) | copy-start | bytes 2359300
  98.0 44.8 %copy-start.43 = (bf16[192,192]{1,0:T(8,128)(2,1)S(1)}, bf16[192,192]{1,0:T(8,128)(2,1)}, u32[]{:S(2)}) copy-start(bf16[192,192]{1,0:T(8,128)(2,1)} %param.48) | copy-start | bytes 221188
  98.0 51.0 %copy-start.74 = (f32[2,192]{1,0:T(2,128)S(1)}, f32[2,192]{1,0:T(2,128)}, u32[]{:S(2)}) copy-start(f32[2,192]{1,0:T(2,128)} %param.39) | copy-start | bytes 4612
  98.0 51.6 %copy-start.35 = (f32[192,192]{1,0:T(8,128)S(1)}, f32[192,192]{1,0:T(8,128)}, u32[]{:S(2)}) copy-start(f32[192,192]{1,0:T(8,128)} %param.34) | copy-start | bytes 442372
  106.8 8.5 %copy-start.1 = (f32[2,3,512,512]{3,2,1,0:T(8,128)S(1)}, f32[2,3,512,512]{3,2,1,0:T(8,128)}, u32[]{:S(2)}) copy-start(f32[2,3,512,512]{3,2,1,0:T(8,128)} %copy-done) | copy-start | bytes 18874372 | tf_op jit(solution)/shard_map/while
  106.8 8.5 %copy-start.15 = (f32[2,3,512,64]{2,3,1,0:T(8,128)S(1)}, f32[2,3,512,64]{2,3,1,0:T(8,128)}, u32[]{:S(2)}) copy-start(f32[2,3,512,64]{2,3,1,0:T(8,128)} %get-tuple-element.703) | copy-start | bytes 2359300 | tf_op jit(solution)/shard_map/while
  129.2 8.5 %copy-start.1 = (f32[2,3,512,512]{3,2,1,0:T(8,128)S(1)}, f32[2,3,512,512]{3,2,1,0:T(8,128)}, u32[]{:S(2)}) copy-start(f32[2,3,512,512]{3,2,1,0:T(8,128)} %copy-done) | copy-start | bytes 18874372 | tf_op jit(solution)/shard_map/while
  129.2 8.5 %copy-start.15 = (f32[2,3,512,64]{2,3,1,0:T(8,128)S(1)}, f32[2,3,512,64]{2,3,1,0:T(8,128)}, u32[]{:S(2)}) copy-start(f32[2,3,512,64]{2,3,1,0:T(8,128)} %get-tuple-element.703) | copy-start | bytes 2359300 | tf_op jit(solution)/shard_map/while
  142.7 15.4 %copy-start.17 = (f32[2,3,512,64]{2,3,1,0:T(8,128)S(1)}, f32[2,3,512,64]{2,3,1,0:T(8,128)}, u32[]{:S(2)}) copy-start(f32[2,3,512,64]{2,3,1,0:T(8,128)} %get-tuple-element.169) | copy-start | bytes 2359300
  142.7 15.6 %copy-start.61 = (f32[192]{0:T(256)S(1)}, f32[192]{0:T(256)}, u32[]{:S(2)}) copy-start(f32[192]{0:T(256)} %param.45) | copy-start | bytes 2308
  158.5 405.8 %copy-start.7 = (f32[512,2,192]{0,2,1:T(8,128)}, f32[512,2,192]{0,2,1:T(8,128)S(1)}, u32[]{:S(2)}) copy-start(f32[512,2,192]{0,2,1:T(8,128)S(1)} %fusion.83) | copy-start | bytes 2359300
  161.2 71.7 %all-gather.13.cloned.1.call-start = ((), (), s32[]{:S(2)}) async-start(), calls=%async_computation.11 | async-start | bytes 1474560 | tf_op jit(solution)/shard_map/all_gather | solution.py:115
  161.9 61.9 %copy-start.51 = (f32[768]{0:T(1024)}, f32[768]{0:T(1024)S(1)}, u32[]{:S(2)}) copy-start(f32[768]{0:T(1024)S(1)} %get-tuple-element.334) | copy-start | bytes 9220
  163.2 101.6 %all-gather.11.cloned.1.call-start = ((), (), s32[]{:S(2)}) async-start(), calls=%async_computation.10 | async-start | bytes 1966080 | tf_op jit(solution)/shard_map/all_gather | solution.py:215
  226.4 38.3 %copy-start.80 = (f32[768]{0:T(1024)S(1)}, f32[768]{0:T(1024)}, u32[]{:S(2)}) copy-start(f32[768]{0:T(1024)} %param.42) | copy-start | bytes 9220
  226.5 38.3 %copy-start.81 = (f32[768]{0:T(1024)S(1)}, f32[768]{0:T(1024)}, u32[]{:S(2)}) copy-start(f32[768]{0:T(1024)} %param.46) | copy-start | bytes 9220
  227.7 55.3 %all-gather.15.cloned.1.call-start = ((), (), s32[]{:S(2)}) async-start(), calls=%async_computation.12 | async-start | bytes 1474560 | tf_op jit(solution)/shard_map/all_gather | solution.py:116
  227.8 48.5 %copy-start.70 = (f32[1,192]{1,0:T(1,128)}, f32[1,192]{1,0:T(1,128)S(1)}, u32[]{:S(2)}) copy-start(f32[1,192]{1,0:T(1,128)S(1)} %get-tuple-element.447) | copy-start | bytes 2308
  229.8 72.0 %all-gather.19.cloned.1.call-start = ((), (), s32[]{:S(2)}) async-start(), calls=%async_computation.14 | async-start | bytes 1474560 | tf_op jit(solution)/shard_map/all_gather | solution.py:119
  230.6 110.4 %all-gather.17.cloned.1.call-start = ((), (), s32[]{:S(2)}) async-start(), calls=%async_computation.13 | async-start | bytes 1966080 | tf_op jit(solution)/shard_map/all_gather | solution.py:216
  231.9 126.9 %all-gather.21.cloned.1.call-start = ((), (), s32[]{:S(2)}) async-start(), calls=%async_computation.15 | async-start | bytes 1474560 | tf_op jit(solution)/shard_map/all_gather | solution.py:120
  232.6 199.1 %reduce-scatter.14.cloned.1.call-start = ((), (), s32[]{:S(2)}) async-start(), calls=%async_computation.16 | async-start | bytes 3932160 | tf_op jit(solution)/shard_map/reduce_scatter | solution.py:229
  283.0 58.0 %copy-start.79 = (f32[768]{0:T(1024)S(1)}, f32[768]{0:T(1024)}, u32[]{:S(2)}) copy-start(f32[768]{0:T(1024)} %param.52) | copy-start | bytes 9220
  358.8 10.6 %copy-start.32 = (bf16[512,2,768]{2,0,1:T(8,128)(2,1)S(1)}, bf16[512,2,768]{2,0,1:T(8,128)(2,1)}, u32[]{:S(2)}) copy-start(bf16[512,2,768]{2,0,1:T(8,128)(2,1)} %convolution_convert_fusion.2) | copy-start | bytes 4718596
  371.3 106.0 %all-gather.23.cloned.1.call-start = ((), (), s32[]{:S(2)}) async-start(), calls=%async_computation.17 | async-start | bytes 1966080 | tf_op jit(solution)/shard_map/all_gather | solution.py:269
  440.3 82.2 %reduce-scatter.16.cloned.1.call-start = ((), (), s32[]{:S(2)}) async-start(), calls=%async_computation.18 | async-start | bytes 1966080 | tf_op jit(solution)/shard_map/reduce_scatter | solution.py:280
  477.3 8.3 copy-start.78
  488.2 76.2 %all-gather.25.cloned.1.call-start = ((), (), s32[]{:S(2)}) async-start(), calls=%async_computation.19 | async-start | bytes 1966080 | tf_op jit(solution)/shard_map/all_gather | solution.py:292
  526.0 41.2 %copy-start.18 = (f32[2,3,512,64]{2,3,1,0:T(8,128)S(1)}, f32[2,3,512,64]{2,3,1,0:T(8,128)}, u32[]{:S(2)}) copy-start(f32[2,3,512,64]{2,3,1,0:T(8,128)} %get-tuple-element.169) | copy-start | bytes 2359300
  526.0 43.5 %copy-start.67 = (f32[128,2]{0,1:T(2,128)}, f32[128,2]{0,1:T(2,128)S(1)}, u32[]{:S(2)}) copy-start(f32[128,2]{0,1:T(2,128)S(1)} %negate_multiply_fusion.2) | copy-start | bytes 3076
  528.3 105.7 %reduce-scatter.18.cloned.1.call-start = ((), (), s32[]{:S(2)}) async-start(), calls=%async_computation.20 | async-start | bytes 2359296 | tf_op jit(solution)/shard_map/reduce_scatter | solution.py:354
  605.9 30.0 %copy-start.31 = (bf16[512,2,768]{2,1,0:T(2,128)(2,1)S(1)}, bf16[512,2,768]{2,1,0:T(2,128)(2,1)}, u32[]{:S(2)}) copy-start(bf16[512,2,768]{2,1,0:T(2,128)(2,1)} %param.29) | copy-start | bytes 4718596
  605.9 30.0 %copy-start.55 = (f32[768]{0:T(1024)S(1)}, f32[768]{0:T(1024)}, u32[]{:S(2)}) copy-start(f32[768]{0:T(1024)} %param.44) | copy-start | bytes 9220
  605.9 30.0 %copy-start.73 = (bf16[768]{0:T(1024)(128)(2,1)S(1)}, bf16[768]{0:T(1024)(128)(2,1)}, u32[]{:S(2)}) copy-start(bf16[768]{0:T(1024)(128)(2,1)} %copy-done.72) | copy-start | bytes 4612
  608.9 56.3 %reduce-scatter.28.cloned.1.call-start = ((), (), s32[]{:S(2)}) async-start(), calls=%async_computation.25 | async-start | bytes 1228800
  640.7 52.8 %reduce-scatter.24.cloned.1.call-start = ((), (), s32[]{:S(2)}) async-start(), calls=%async_computation.23 | async-start | bytes 1474560 | tf_op jit(solution)/shard_map/reduce_scatter | solution.py:385
  645.1 5.0 copy-start.8
  645.1 5.0 copy-start.13
  645.2 76.6 %reduce-scatter.26.cloned.1.call-start = ((), (), s32[]{:S(2)}) async-start(), calls=%async_computation.24 | async-start | bytes 1474560 | tf_op jit(solution)/shard_map/reduce_scatter | solution.py:388
  650.1 95.5 %reduce-scatter.22.cloned.1.call-start = ((), (), s32[]{:S(2)}) async-start(), calls=%async_computation.22 | async-start | bytes 491520 | tf_op jit(solution)/shard_map/reduce_scatter | solution.py:382
  651.6 157.7 %all-reduce.4.cloned.1.call-start = ((), (), s32[]{:S(2)}) async-start(), calls=%async_computation.26 | async-start | bytes 2162688 | tf_op jit(solution)/shard_map/psum | solution.py:393
  745.6 7.9 copy-start.30
  745.6 79.1 %reduce-scatter.20.cloned.1.call-start = ((), (), s32[]{:S(2)}) async-start(), calls=%async_computation.21 | async-start | bytes 1966080 | tf_op jit(solution)/shard_map/reduce_scatter | solution.py:369
  750.0 12.4 %copy-start.24 = (bf16[512,2,384]{0,2,1:T(8,128)(2,1)S(1)}, bf16[512,2,384]{0,2,1:T(8,128)(2,1)}, u32[]{:S(2)}) copy-start(bf16[512,2,384]{0,2,1:T(8,128)(2,1)} %reduce-scatter.18.cloned.1.call-done) | copy-start | bytes 2359300
  750.0 59.3 %copy-start.20 = (f32[192,3,192]{2,0,1:T(8,128)S(1)}, f32[192,3,192]{2,0,1:T(8,128)}, u32[]{:S(2)}) copy-start(f32[192,3,192]{2,0,1:T(8,128)} %param.33) | copy-start | bytes 1327108
  750.0 59.3 %copy-start.46 = (f32[3,192]{1,0:T(4,128)S(1)}, f32[3,192]{1,0:T(4,128)}, u32[]{:S(2)}) copy-start(f32[3,192]{1,0:T(4,128)} %copy-done.45) | copy-start | bytes 6916
  750.0 59.3 %copy-start.48 = (f32[3,192]{1,0:T(4,128)S(1)}, f32[3,192]{1,0:T(4,128)}, u32[]{:S(2)}) copy-start(f32[3,192]{1,0:T(4,128)} %copy-done.47) | copy-start | bytes 6916
  750.0 62.0 %copy-start.36 = (f32[192,192]{1,0:T(8,128)S(1)}, f32[192,192]{1,0:T(8,128)}, u32[]{:S(2)}) copy-start(f32[192,192]{1,0:T(8,128)} %param.34) | copy-start | bytes 442372
  750.1 63.5 %copy-start.21 = (f32[192,768]{1,0:T(8,128)S(1)}, f32[192,768]{1,0:T(8,128)}, u32[]{:S(2)}) copy-start(f32[192,768]{1,0:T(8,128)} %param.36) | copy-start | bytes 1769476
  754.7 60.5 %copy-start.23 = (f32[192,768]{1,0:T(8,128)S(1)}, f32[192,768]{1,0:T(8,128)}, u32[]{:S(2)}) copy-start(f32[192,768]{1,0:T(8,128)} %param.35) | copy-start | bytes 1769476
  754.7 60.5 %copy-start.50 = (f32[768]{0:T(1024)S(1)}, f32[768]{0:T(1024)}, u32[]{:S(2)}) copy-start(f32[768]{0:T(1024)} %copy-done.49) | copy-start | bytes 9220
  754.7 60.5 %copy-start.52 = (f32[768]{0:T(1024)S(1)}, f32[768]{0:T(1024)}, u32[]{:S(2)}) copy-start(f32[768]{0:T(1024)} %copy-done.51) | copy-start | bytes 9220
  809.3 5.8 copy-start.41
  809.4 15.3 %copy-start.12 = (f32[128,2,768]{2,0,1:T(8,128)S(1)}, f32[128,2,768]{2,0,1:T(8,128)}, u32[]{:S(2)}) copy-start(f32[128,2,768]{2,0,1:T(8,128)} %copy-done.11) | copy-start | bytes 2359300
  809.4 15.3 %copy-start.56 = (f32[768]{0:T(1024)S(1)}, f32[768]{0:T(1024)}, u32[]{:S(2)}) copy-start(f32[768]{0:T(1024)} %param.44) | copy-start | bytes 9220
  809.4 15.3 %copy-start.68 = (f32[128,2]{0,1:T(2,128)S(1)}, f32[128,2]{0,1:T(2,128)}, u32[]{:S(2)}) copy-start(f32[128,2]{0,1:T(2,128)} %copy-done.67) | copy-start | bytes 3076
  (56 other events, 124.5 us)
Sparse Core Ops, SparseCore 0:
  161.3 61.1 reduce-scatter.11
  371.4 60.2 reduce-scatter.13
  488.3 34.1 reduce-scatter.15
  609.0 24.9 reduce-scatter.17
  745.7 41.5 all-reduce.3
  789.5 35.1 reduce-scatter.19
Sparse Core Ops, SparseCore 1:
  163.8 18.2 all-gather.12
  227.8 36.9 all-gather.10
  266.8 16.1 all-gather.14
  284.5 17.3 all-gather.18
  304.0 36.9 all-gather.16
  342.6 16.1 all-gather.20
  440.3 36.9 all-gather.22
  528.4 35.9 all-gather.24
  640.8 24.4 reduce-scatter.27
  667.8 25.6 reduce-scatter.23
  696.1 25.6 reduce-scatter.25
  724.9 20.7 reduce-scatter.21
where the time goes:
time: 841 us; the launch traced here: 835 us
  waiting for transfers between devices  453 us (54%)
  blocking collectives  123 us (15%)
  matrix products  113 us (13%)
  other arithmetic  65.4 us (8%)
  local copies, waits for them, and re-layouts  54.5 us (6%)
  between operations  21.6 us (3%)
    reduce_scatter x1, waiting for transfers between devices, body(): lax.psum_scatter(jnp.concatenate([jnp.einsum('tsf,df->tsd', rows_student,...  59.7 us
    reduce_scatter x1, waiting for transfers between devices, body(): lax.psum_scatter(jnp.concatenate([jnp.einsum('tsh,dh->tsd', rows_student,...  55.8 us
    psum x1, blocking collectives, body(): lax.psum((stat_terms, vector_grads, placed_qv, placed_up), ('fsdp', 'ctx'...  40 us
    all_gather x1, waiting for transfers between devices, body(): lax.all_gather(h_teacher.astype(jnp.bfloat16), 'tp', axis=0, tiled=True)  39.1 us
    all_gather x1, waiting for transfers between devices, body(): d_ffn_full = lax.all_gather(d_ffn, 'tp', axis=0, tiled=True)  37 us
    all_gather x1, waiting for transfers between devices, body(): d_attn_full = lax.all_gather(d_attn, 'tp', axis=0, tiled=True)  35.2 us
    reduce_scatter x1, waiting for transfers between devices, body(): lax.psum_scatter(jnp.einsum('tsf,df->tsd', rows, full_up, preferred_eleme...  34.2 us
    all_gather x1, waiting for transfers between devices, body(): lax.all_gather(h_one.astype(jnp.bfloat16), 'tp', axis=0, tiled=True)  31.9 us
  transfers between devices with their start and end apart: 18, of which 16 were waited for; matrix products, arithmetic and copies ran while one was open for 9% of the time, Pallas kernels for 0%

commit v1 on v0

--- a/solution.py
+++ b/solution.py
@@ -1,8 +1,11 @@
+import functools
 import math
 
 import jax
 import jax.numpy as jnp
 from jax import lax
+from jax.experimental import pallas as pl
+from jax.experimental.pallas import tpu as pltpu
 from jax.sharding import PartitionSpec as P
 
 HEAD_DIM = 64
@@ -67,7 +70,908 @@
     return (jnp.transpose(merged, (2, 0, 1, 3)), running + jnp.log(total))
 
 
-def body(
+def vmem_specs(count):
+    return [pl.BlockSpec(memory_space=pltpu.VMEM)] * count
+
+
+def call_kernel(kernel, place, inputs, outs, scratch=(), flops=0, moved=0, exps=0):
+    return pl.pallas_call(
+        kernel,
+        out_shape=outs,
+        in_specs=[pl.BlockSpec(memory_space=pltpu.SMEM)] + vmem_specs(len(inputs)),
+        out_specs=jax.tree.map(lambda _: pl.BlockSpec(memory_space=pltpu.VMEM), outs),
+        scratch_shapes=list(scratch),
+        compiler_params=pltpu.CompilerParams(vmem_limit_bytes=60 * 2**20),
+        cost_estimate=pl.CostEstimate(flops=flops, bytes_accessed=moved, transcendentals=exps),
+    )(place, *inputs)
+
+
+def shaped(shape, dtype):
+    return jax.ShapeDtypeStruct(shape, dtype)
+
+
+NT = (((1,), (1,)), ((), ()))
+
+
+def dot_nt(left, right):
+    return lax.dot_general(left, right, NT, preferred_element_type=jnp.float32)
+
+
+def dot_nn(left, right):
+    return jnp.dot(left, right, preferred_element_type=jnp.float32)
+
+
+def place_rows(place_ref, pieces, target, index=()):
+    size = pieces[0].shape[-2]
+    for distance, piece in zip((0, 2, 1, 3), pieces):
+        start = pl.multiple_of((place_ref[0] ^ distance) * size, 64)
+        target[(*index, pl.ds(start, size), slice(None))] = piece[...] if not index else piece[index]
+
+
+def masked_bias(code_col, code_row, block, count, size):
+    segments = code_row >> 1
+    tags = jnp.where((code_col & 1) > 0, code_col >> 1, -1)
+    key_at = lax.broadcasted_iota(jnp.int32, (count, size), 0)
+    query_at = lax.broadcasted_iota(jnp.int32, (count, size), 1) + block * size
+    allowed = (tags == segments) | (key_at == query_at)
+    return jnp.where(allowed, 0.0, floor_score)
+
+
+def attention_kernel(
+    student,
+    place_ref,
+    own_ref,
+    other_ref,
+    w0_ref,
+    w2_ref,
+    w1_ref,
+    w3_ref,
+    bias_ref,
+    clip_in_ref,
+    clip_ref,
+    col_ref,
+    row_ref,
+    *refs,
+):
+    if student:
+        c_ref, a_ref, q_ref, k_ref, v_ref, ratio_ref, lse_ref, w_ref, vt_ref, mask_ref = refs
+    else:
+        c_ref, w_ref, q_ref, k_ref, v_ref, vt_ref, mask_ref = refs
+    half = own_ref.shape[0]
+    count = 2 * half
+    cols = w_ref.shape[-1]
+    heads = cols // HEAD_DIM
+    size = 256
+    bf16 = jnp.bfloat16
+    for kind in range(3):
+        for distance, piece in zip((0, 2, 1, 3), (w0_ref, w2_ref, w1_ref, w3_ref)):
+            rows = piece.shape[1]
+            start = pl.multiple_of((place_ref[0] ^ distance) * rows, 64)
+            w_ref[kind, pl.ds(start, rows), :] = piece[kind]
+    for part, source in enumerate((own_ref, other_ref)):
+        inputs = source[...]
+        base = part * half
+        if student:
+            wide = inputs.astype(jnp.float32)
+            inputs = jnp.clip(wide, -clip_in_ref[...], clip_in_ref[...]).astype(bf16)
+            a_ref[base : base + half, :] = inputs
+        queries = (dot_nn(inputs, w_ref[0]) + bias_ref[0:1, :]).astype(bf16)
+        keys = dot_nn(inputs, w_ref[1]).astype(bf16)
+        values = (dot_nn(inputs, w_ref[2]) + bias_ref[1:2, :]).astype(bf16)
+        for head in range(heads):
+            lanes = slice(head * HEAD_DIM, (head + 1) * HEAD_DIM)
+            q_ref[head, base : base + half, :] = queries[:, lanes] * (HEAD_DIM**-0.5)
+            k_ref[head, base : base + half, :] = keys[:, lanes]
+            v_ref[head, base : base + half, :] = values[:, lanes]
+    eye = (
+        lax.broadcasted_iota(jnp.int32, (HEAD_DIM, HEAD_DIM), 0)
+        == lax.broadcasted_iota(jnp.int32, (HEAD_DIM, HEAD_DIM), 1)
+    ).astype(bf16)
+    for head in range(heads):
+        vt_ref[head] = dot_nt(eye, v_ref[head]).astype(bf16)
+
+    def one_block(block, carry):
+        at = pl.multiple_of(block * size, size)
+        mask_ref[...] = masked_bias(col_ref[...], row_ref[:, pl.ds(at, size)], block, count, size)
+        outs = []
+        for head in range(heads):
+            scores = dot_nt(k_ref[head], q_ref[head, pl.ds(at, size), :]) + mask_ref[...]
+            top = jnp.max(scores, axis=0, keepdims=True)
+            weights = jnp.exp(scores - top)
+            total = jnp.sum(weights, axis=0, keepdims=True)
+            merged = dot_nn(vt_ref[head], weights.astype(bf16)) * (1.0 / total)
+            outs.append(merged)
+            if student:
+                lse_ref[pl.ds(head, 1), pl.ds(at, size)] = top + jnp.log(total)
+        merged = jnp.concatenate(outs + [jnp.zeros((256 - cols, size), jnp.float32)], axis=0)
+        merged = jnp.transpose(merged)[:, :cols]
+        if student:
+            ratio = jnp.tanh(merged / clip_ref[...])
+            ratio_ref[pl.ds(at, size), :] = ratio
+            merged = clip_ref[...] * ratio
+        merged = merged.astype(bf16)
+        part, pair = block >> 1, block & 1
+        share = size // 2
+        c_ref[2 * pair, part] = merged[:share]
+        c_ref[2 * pair + 1, part] = merged[share:]
+        return carry
+
+    lax.fori_loop(0, count // size, one_block, 0)
+
+
+def attention_forward(student, place, own, other, pieces, bias, clip_in, clip, code_col, code_row):
+    half, width = own.shape
+    cols = pieces[0].shape[-1]
+    heads = cols // HEAD_DIM
+    count = 2 * half
+    bf16, f32 = jnp.bfloat16, jnp.float32
+    head_shape = (heads, count, HEAD_DIM)
+    c_shape = shaped((4, 2, half // 4, cols), bf16)
+    w = pltpu.VMEM((3, width, cols), bf16)
+    vt = pltpu.VMEM((heads, HEAD_DIM, count), bf16)
+    mask = pltpu.VMEM((count, 256), f32)
+    if student:
+        outs = (
+            c_shape,
+            shaped((count, width), bf16),
+            shaped(head_shape, bf16),
+            shaped(head_shape, bf16),
+            shaped(head_shape, bf16),
+            shaped((count, cols), f32),
+            shaped((8, count), f32),
+        )
+        scratch = (w, vt, mask)
+    else:
+        outs = (c_shape,)
+        scratch = (w,) + (pltpu.VMEM(head_shape, bf16),) * 3 + (vt, mask)
+    return call_kernel(
+        functools.partial(attention_kernel, student),
+        place,
+        (own, other, *pieces, bias, clip_in, clip, code_col, code_row),
+        outs,
+        scratch,
+        flops=2 * count * width * cols * 3 + 4 * count * count * cols,
+        moved=6 * count * width,
+        exps=heads * count * count,
+    )
+
+
+def attention_pull_kernel(
+    place_ref,
+    a_ref,
+    q_ref,
+    k_ref,
+    v_ref,
+    ratio_ref,
+    lse_ref,
+    col_ref,
+    row_ref,
+    d0_ref,
+    d1_ref,
+    d2_ref,
+    d3_ref,
+    w0_ref,
+    w2_ref,
+    w1_ref,
+    w3_ref,
+    back_ref,
+    dproj_ref,
+    sums_ref,
+    w_ref,
+    grad_ref,
+    kt_ref,
+    mask_ref,
+    dk_ref,
+    dv_ref,
+):
+    heads, count, _ = q_ref.shape
+    cols = heads * HEAD_DIM
+    size = 256
+    share = size // 2
+    bf16, f32 = jnp.bfloat16, jnp.float32
+    for kind in range(3):
+        for distance, piece in zip((0, 2, 1, 3), (w0_ref, w2_ref, w1_ref, w3_ref)):
+            rows = piece.shape[1]
+            start = pl.multiple_of((place_ref[0] ^ distance) * rows, 64)
+            w_ref[kind, pl.ds(start, rows), :] = piece[kind]
+    eye = (
+        lax.broadcasted_iota(jnp.int32, (HEAD_DIM, HEAD_DIM), 0)
+        == lax.broadcasted_iota(jnp.int32, (HEAD_DIM, HEAD_DIM), 1)
+    ).astype(bf16)
+    for head in range(heads):
+        kt_ref[head] = dot_nt(eye, k_ref[head]).astype(bf16)
+    for distance, source in enumerate((d0_ref, d1_ref, d2_ref, d3_ref)):
+        for part in range(2):
+            at = part * (count // 2) + distance * share
+            ratio = ratio_ref[at : at + share, :]
+            grad = source[part].astype(f32) * (1.0 - ratio * ratio)
+            for head in range(heads):
+                lanes = slice(head * HEAD_DIM, (head + 1) * HEAD_DIM)
+                grad_ref[head, at : at + share, :] = grad[:, lanes].astype(bf16)
+    dk_ref[...] = jnp.zeros_like(dk_ref)
+    dv_ref[...] = jnp.zeros_like(dv_ref)
+
+    def one_block(block, carry):
+        at = pl.multiple_of(block * size, size)
+        mask_ref[...] = masked_bias(col_ref[...], row_ref[:, pl.ds(at, size)], block, count, size)
+        outs = []
+        for head in range(heads):
+            query = q_ref[head, pl.ds(at, size), :]
+            grad = grad_ref[head, pl.ds(at, size), :]
+            lse = lse_ref[pl.ds(head, 1), pl.ds(at, size)]
+            probs = jnp.exp(dot_nt(k_ref[head], query) + mask_ref[...] - lse)
+            d_probs = dot_nt(v_ref[head], grad)
+            delta = jnp.sum(probs * d_probs, axis=0, keepdims=True)
+            d_scores = (probs * (d_probs - delta)).astype(bf16)
+            dv_ref[head] += dot_nn(probs.astype(bf16), grad)
+            dk_ref[head] += dot_nn(d_scores, query)
+            outs.append(dot_nn(kt_ref[head], d_scores) * (HEAD_DIM**-0.5))
+        merged = jnp.concatenate(outs + [jnp.zeros((256 - cols, size), f32)], axis=0)
+        dproj_ref[0, pl.ds(at, size), :] = jnp.transpose(merged)[:, :cols].astype(bf16)
+        return carry
+
+    lax.fori_loop(0, count // size, one_block, 0)
+    for head in range(heads):
+        lanes = slice(head * HEAD_DIM, (head + 1) * HEAD_DIM)
+        dproj_ref[1, :, lanes] = dk_ref[head].astype(bf16)
+        dproj_ref[2, :, lanes] = dv_ref[head].astype(bf16)
+    sums_ref[0:1, :] = jnp.sum(dproj_ref[0].astype(f32), axis=0, keepdims=True)
+    sums_ref[1:2, :] = jnp.sum(dproj_ref[2].astype(f32), axis=0, keepdims=True)
+    for part in range(2):
+        at = slice(part * (count // 2), (part + 1) * (count // 2))
+        back = (
+            dot_nt(dproj_ref[0, at, :], w_ref[0])
+            + dot_nt(dproj_ref[1, at, :], w_ref[1])
+            + dot_nt(dproj_ref[2, at, :], w_ref[2])
+        ).astype(bf16)
+        for distance in range(4):
+            back_ref[distance, part] = back[distance * share : (distance + 1) * share]
+
+
+def attention_backward(place, a_in, q, k, v, ratio, lse, code_col, code_row, grads, pieces):
+    heads, count, _ = q.shape
+    cols = heads * HEAD_DIM
+    width = a_in.shape[1]
+    bf16, f32 = jnp.bfloat16, jnp.float32
+    return call_kernel(
+        attention_pull_kernel,
+        place,
+        (a_in, q, k, v, ratio, lse, code_col, code_row, *grads, *pieces),
+        (
+            shaped((4, 2, count // 8, width), bf16),
+            shaped((3, count, cols), bf16),
+            shaped((2, cols), f32),
+        ),
+        (
+            pltpu.VMEM((3, width, cols), bf16),
+            pltpu.VMEM((heads, count, HEAD_DIM), bf16),
+            pltpu.VMEM((heads, HEAD_DIM, count), bf16),
+            pltpu.VMEM((count, 256), f32),
+            pltpu.VMEM((heads, count, HEAD_DIM), f32),
+            pltpu.VMEM((heads, count, HEAD_DIM), f32),
+        ),
+        flops=2 * count * width * cols * 3 + 10 * count * count * cols,
+        moved=8 * count * width,
+        exps=heads * count * count,
+    )
+
+
+def unit_of(stream):
+    mean = jnp.mean(stream, axis=-1, keepdims=True)
+    centred = stream - mean
+    scale = lax.rsqrt(jnp.mean(centred * centred, axis=-1, keepdims=True) + epsilon)
+    return centred * scale, scale
+
+
+def column_sum(value):
+    return jnp.sum(value, axis=0, keepdims=True)
+
+
+def dot_tn(left, right):
+    return lax.dot_general(left, right, (((0,), (0,)), ((), ())), preferred_element_type=jnp.float32)
+
+
+def out_norm_kernel(student, model, place_ref, c0, c1, c2, c3, w0, w2, w1, w3, own_ref, other_ref, valid_ref, params_ref, *refs):
+    if student:
+        w_ref, unit_ref, scale_ref, low_ref, sums_ref = refs
+    else:
+        wide_ref, low_ref, w_ref = refs
+    share = own_ref.shape[0]
+    total = None
+    for r, source in enumerate((c0, c1, c2, c3)):
+        for distance, piece in zip((0, 2, 1, 3), (w0, w2, w1, w3)):
+            size = piece.shape[2]
+            start = pl.multiple_of((place_ref[0] ^ distance) * size, 64)
+            w_ref[r, pl.ds(start, size), :] = piece[r, model]
+        context = jnp.concatenate([source[0], source[1]], axis=0)
+        term = dot_nt(context, w_ref[r])
+        total = term if total is None else total + term
+    attn = total + params_ref[0:1, :]
+    stream = jnp.concatenate([own_ref[...], other_ref[...]], axis=0).astype(jnp.float32)
+    unit, scale = unit_of(stream + attn)
+    wide = unit * params_ref[2:3, :] + params_ref[3:4, :]
+    low_ref[...] = wide.astype(jnp.bfloat16)
+    if student:
+        unit_ref[...] = unit
+        scale_ref[...] = scale
+        valid = valid_ref[...]
+        sums_ref[0:1, :] = column_sum(valid * jnp.ones_like(stream))
+        sums_ref[1:2, :] = column_sum(valid * stream * stream)
+        sums_ref[2:3, :] = column_sum(valid * attn * attn)
+    else:
+        wide_ref[...] = wide
+
+
+def out_norm(student, place, contexts, pieces, own, other, valid, params):
+    share, width = own.shape
+    rows = 2 * share
+    cols = contexts[0].shape[-1]
+    f32, bf16 = jnp.float32, jnp.bfloat16
+    w = (4, width, cols)
+    if student:
+        outs = (
+            shaped(w, bf16),
+            shaped((rows, width), f32),
+            shaped((rows, 1), f32),
+            shaped((rows, width), bf16),
+            shaped((3, width), f32),
+        )
+        scratch = ()
+    else:
+        outs = (shaped((rows, width), f32), shaped((rows, width), bf16))
+        scratch = (pltpu.VMEM(w, bf16),)
+    return call_kernel(
+        functools.partial(out_norm_kernel, student, 0 if student else 1),
+        place,
+        (*contexts, *pieces, own, other, valid, params),
+        outs,
+        scratch,
+        flops=2 * rows * width * cols * 4,
+        moved=12 * rows * width,
+    )
+
+
+def gelu_parts(values):
+    cdf = 0.5 * (1.0 + lax.erf(values * (2.0**-0.5)))
+    return values * cdf, cdf
+
+
+def hidden_kernel(student, assemble, far, place_ref, h_ref, *refs):
+    refs = list(refs)
+    pieces = [refs.pop(0) for _ in range(8 if assemble else 1)]
+    bias_ref = refs.pop(0)
+    clip_ref = refs.pop(0) if student else None
+    w_ref = refs.pop(0) if assemble else pieces[0]
+    if student:
+        hid_ref, slope_ref = refs.pop(0), refs.pop(0)
+    part_ref = refs.pop(0)
+    bf16 = jnp.bfloat16
+    total = None
+    inputs = h_ref[...]
+    for r in range(4):
+        if assemble:
+            group = pieces[:4] if r < 2 else pieces[4:]
+            for mat in range(2):
+                for distance, piece in zip((0, 2, 1, 3), group):
+                    size = piece.shape[2]
+                    start = pl.multiple_of((place_ref[0] ^ distance) * size, 64)
+                    w_ref[r, mat, pl.ds(start, size), :] = piece[r & 1, mat]
+        upper = dot_nn(inputs, w_ref[r, 0]) + bias_ref[r : r + 1, :]
+        active, cdf = gelu_parts(upper)
+        if student:
+            clip = clip_ref[r : r + 1, :]
+            ratio = jnp.tanh(active / clip)
+            pdf = jnp.exp(-0.5 * upper * upper) * ((2.0 * math.pi) ** -0.5)
+            slope_ref[r] = ((1.0 - ratio * ratio) * (cdf + upper * pdf)).astype(bf16)
+            hidden = (clip * ratio).astype(bf16)
+            hid_ref[r] = hidden
+        else:
+            hidden = active.astype(bf16)
+        term = dot_nt(hidden, w_ref[r, 1])
+        total = term if total is None else total + term
+    part_ref[...] = total.astype(part_ref.dtype)
+
+
+def hidden_layer(student, far, place, h, weights, bias, clip):
+    rows, width = h.shape
+    half = bias.shape[-1]
+    f32, bf16 = jnp.float32, jnp.bfloat16
+    assemble = isinstance(weights, tuple)
+    outs = []
+    if assemble:
+        outs.append(shaped((4, 2, width, half), bf16))
+    if student:
+        outs += [shaped((4, rows, half), bf16)] * 2
+    outs.append(shaped((rows, width), bf16 if far else f32))
+    inputs = (h, *(weights if assemble else (weights,)), bias) + ((clip,) if student else ())
+    return call_kernel(
+        functools.partial(hidden_kernel, student, assemble, far),
+        place,
+        inputs,
+        tuple(outs),
+        flops=2 * rows * width * half * 8,
+        moved=8 * width * half * 2 + 16 * rows * half,
+        exps=(3 if student else 1) * rows * half * 4,
+    )
+
+
+def loss_kernel(
+    place_ref, unit_ref, ffn_ref, got_ref, ht_ref, ffnt_ref, gott_ref, cot_ref, cot_other_ref, valid_ref, params_ref, t_ref,
+    layer_ref, layer_other_ref, dz_ref, low_ref, sums_ref,
+):
+    share = cot_ref.shape[0]
+    f32, bf16 = jnp.float32, jnp.bfloat16
+    h_one = unit_ref[...] * params_ref[2:3, :] + params_ref[3:4, :]
+    ffn = ffn_ref[...] + got_ref[...].astype(f32) + params_ref[1:2, :]
+    unit, scale = unit_of(h_one + ffn)
+    out = unit * params_ref[4:5, :] + params_ref[5:6, :]
+    low = out.astype(bf16)
+    layer_ref[...] = low[:share]
+    layer_other_ref[...] = low[share:]
+    t_unit, _ = unit_of(ht_ref[...] + ffnt_ref[...] + gott_ref[...].astype(f32) + t_ref[1:2, :])
+    difference = out - (t_unit * t_ref[4:5, :] + t_ref[5:6, :])
+    valid = valid_ref[...]
+    gap = valid * difference
+    arriving = jnp.concatenate([cot_ref[...], cot_other_ref[...]], axis=0).astype(f32)
+    grad = arriving + gap
+    inner = grad * params_ref[4:5, :]
+    dz = scale * (
+        inner
+        - jnp.mean(inner, axis=-1, keepdims=True)
+        - unit * jnp.mean(inner * unit, axis=-1, keepdims=True)
+    )
+    dz_ref[...] = dz
+    dz_low = dz.astype(bf16)
+    low_ref[...] = dz_low
+    sums_ref[0:1, :] = column_sum(dz_low.astype(f32))
+    sums_ref[1:2, :] = column_sum(grad * unit)
+    sums_ref[2:3, :] = column_sum(grad)
+    sums_ref[3:4, :] = column_sum(valid * ffn * ffn)
+    sums_ref[4:5, :] = column_sum(gap * difference)
+
+
+def loss_step(place, unit, ffn, got, ht, ffnt, gott, cot, cot_other, valid, params, t_rows):
+    rows, width = unit.shape
+    share = cot.shape[0]
+    f32, bf16 = jnp.float32, jnp.bfloat16
+    return call_kernel(
+        loss_kernel,
+        place,
+        (unit, ffn, got, ht, ffnt, gott, cot, cot_other, valid, params, t_rows),
+        (
+            shaped((share, width), bf16),
+            shaped((share, width), bf16),
+            shaped((rows, width), f32),
+            shaped((rows, width), bf16),
+            shaped((5, width), f32),
+        ),
+        flops=60 * rows * width,
+        moved=30 * rows * width,
+    )
+
+
+def hidden_pull_kernel(place_ref, grad_ref, w_ref, slope_ref, du_ref, part_ref, sums_ref):
+    grad = grad_ref[...]
+    total = None
+    for r in range(4):
+        upper = (dot_nn(grad, w_ref[r, 1]) * slope_ref[r].astype(jnp.float32)).astype(jnp.bfloat16)
+        du_ref[r] = upper
+        sums_ref[r : r + 1, :] = column_sum(upper.astype(jnp.float32))
+        term = dot_nt(upper, w_ref[r, 0])
+        total = term if total is None else total + term
+    part_ref[...] = total.astype(part_ref.dtype)
+
+
+def hidden_pull(far, place, grad, weights, slope):
+    rows, width = grad.shape
+    half = slope.shape[-1]
+    f32, bf16 = jnp.float32, jnp.bfloat16
+    return call_kernel(
+        hidden_pull_kernel,
+        place,
+        (grad, weights, slope),
+        (shaped((4, rows, half), bf16), shaped((rows, width), bf16 if far else f32), shaped((4, half), f32)),
+        flops=2 * rows * width * half * 8,
+        moved=8 * width * half * 2 + 16 * rows * half,
+    )
+
+
+def keep_and_send(place_ref, full_ref, keep_ref, send_ref, index):
+    size = full_ref.shape[0] // 4
+    for slot in range(2):
+        for target, distance in ((keep_ref, 2 * slot), (send_ref, 2 * slot + 1)):
+            start = pl.multiple_of((place_ref[0] ^ distance) * size, 64)
+            target[(slot, *index)] = full_ref[pl.ds(start, size), :].astype(jnp.bfloat16)
+
+
+def hidden_grads_kernel(place_ref, f0, f1, hid0, hid1, h0, h1, du0, du1, keep_ref, send_ref, full_ref):
+    for mat, (left0, left1, right0, right1) in enumerate(((h0, h1, du0, du1), (f0, f1, hid0, hid1))):
+        left = jnp.concatenate([left0[...], left1[...]], axis=0)
+        for r in range(4):
+            right = jnp.concatenate([right0[r], right1[r]], axis=0)
+            full_ref[...] = dot_tn(left, right)
+            keep_and_send(place_ref, full_ref, keep_ref, send_ref, (mat, r))
+
+
+def hidden_grads(place, grads, hidden, inputs, d_upper):
+    rows, width = grads[0].shape
+    half = hidden[0].shape[-1]
+    bf16 = jnp.bfloat16
+    out = shaped((2, 2, 4, width // 4, half), bf16)
+    return call_kernel(
+        hidden_grads_kernel,
+        place,
+        (*grads, *hidden, *inputs, *d_upper),
+        (out, out),
+        (pltpu.VMEM((width, half), jnp.float32),),
+        flops=4 * rows * width * half * 8,
+        moved=16 * width * half * 2,
+    )
+
+
+def first_pull_kernel(place_ref, dz_ref, part_ref, got_ref, unit_ref, scale_ref, params_ref, w_ref, first_ref, low_ref, sums_ref, ctx_ref):
+    f32, bf16 = jnp.float32, jnp.bfloat16
+    grad = dz_ref[...] + part_ref[...] + got_ref[...].astype(f32)
+    unit = unit_ref[...]
+    inner = grad * params_ref[2:3, :]
+    first = scale_ref[...] * (
+        inner
+        - jnp.mean(inner, axis=-1, keepdims=True)
+        - unit * jnp.mean(inner * unit, axis=-1, keepdims=True)
+    )
+    first_ref[...] = first
+    low = first.astype(bf16)
+    low_ref[...] = low
+    sums_ref[0:1, :] = column_sum(low.astype(f32))
+    sums_ref[1:2, :] = column_sum(grad * unit)
+    sums_ref[2:3, :] = column_sum(grad)
+    share = ctx_ref.shape[2]
+    for r in range(4):
+        back = dot_nn(low, w_ref[r]).astype(bf16)
+        ctx_ref[r, 0] = back[:share]
+        ctx_ref[r, 1] = back[share:]
+
+
+def first_pull(place, dz, part, got, unit, scale, params, weights):
+    rows, width = dz.shape
+    cols = weights.shape[-1]
+    f32, bf16 = jnp.float32, jnp.bfloat16
+    return call_kernel(
+        first_pull_kernel,
+        place,
+        (dz, part, got, unit, scale, params, weights),
+        (
+            shaped((rows, width), f32),
+            shaped((rows, width), bf16),
+            shaped((3, width), f32),
+            shaped((4, 2, rows // 2, cols), bf16),
+        ),
+        flops=2 * rows * width * cols * 4,
+        moved=20 * rows * width,
+    )
+
+
+def out_grads_kernel(place_ref, low_ref, c0, c1, c2, c3, keep_ref, send_ref, full_ref):
+    for r, source in enumerate((c0, c1, c2, c3)):
+        context = jnp.concatenate([source[0], source[1]], axis=0)
+        full_ref[...] = dot_tn(low_ref[...], context)
+        keep_and_send(place_ref, full_ref, keep_ref, send_ref, (r,))
+
+
+def out_grads(place, low, contexts):
+    rows, width = low.shape
+    cols = contexts[0].shape[-1]
+    out = shaped((2, 4, width // 4, cols), jnp.bfloat16)
+    return call_kernel(
+        out_grads_kernel,
+        place,
+        (low, *contexts),
+        (out, out),
+        (pltpu.VMEM((width, cols), jnp.float32),),
+        flops=2 * rows * width * cols * 4,
+        moved=20 * width * cols,
+    )
+
+
+def in_grads_kernel(place_ref, a_ref, d_ref, keep_ref, send_ref, full_ref):
+    for kind in range(3):
+        full_ref[...] = dot_tn(a_ref[...], d_ref[kind])
+        keep_and_send(place_ref, full_ref, keep_ref, send_ref, (kind,))
+
+
+def in_grads(place, a_in, d_proj):
+    count, width = a_in.shape
+    cols = d_proj.shape[-1]
+    out = shaped((2, 3, width // 4, cols), jnp.bfloat16)
+    return call_kernel(
+        in_grads_kernel,
+        place,
+        (a_in, d_proj),
+        (out, out),
+        (pltpu.VMEM((width, cols), jnp.float32),),
+        flops=2 * count * width * cols * 3,
+        moved=4 * count * width,
+    )
+
+
+def input_kernel(place_ref, first_ref, b0, b1, b2, b3, own_ref, other_ref, clip_ref, mine_ref, other_out_ref):
+    f32 = jnp.float32
+    share = own_ref.shape[0]
+    for part, (source, target) in enumerate(((own_ref, mine_ref), (other_ref, other_out_ref))):
+        through = b0[part].astype(f32) + b1[part].astype(f32) + b2[part].astype(f32) + b3[part].astype(f32)
+        inside = jnp.abs(source[...].astype(f32)) < clip_ref[...]
+        first = first_ref[part * share : (part + 1) * share, :]
+        target[...] = (first + jnp.where(inside, through, 0.0)).astype(target.dtype)
+
+
+def input_rows(place, first, backs, own, other, clip_in):
+    share, width = own.shape
+    return call_kernel(
+        input_kernel,
+        place,
+        (first, *backs, own, other, clip_in),
+        (shaped((share, width), jnp.float32), shaped((share, width), jnp.bfloat16)),
+        flops=10 * share * width,
+        moved=20 * share * width,
+    )
+
+
+def swap_ctx(value):
+    return lax.ppermute(value, "ctx", [(0, 1), (1, 0)])
+
+
+def swap_core(value):
+    return lax.ppermute(value, "fsdp", [(i, i ^ 1) for i in range(4)])
+
+
+def swap_row(value):
+    return lax.ppermute(value, "fsdp", [(i, i ^ 2) for i in range(4)])
+
+
+def swap_tp(value, distance):
+    return lax.ppermute(value, "tp", [(i, i ^ distance) for i in range(4)])
+
+
+def fsdp_pieces(piece):
+    far = swap_row(piece)
+    return (piece, far, swap_core(piece), swap_core(far))
+
+
+def tp_pieces(piece):
+    return [piece] + [swap_tp(piece, r) for r in (1, 2, 3)]
+
+
+def exchange_tp(stacked):
+    return [stacked[0]] + [swap_tp(stacked[r], r) for r in (1, 2, 3)]
+
+
+def paired_body(
+    tokens,
+    cotangent,
+    segment_ids,
+    valid_mask,
+    latent_qkv,
+    latent_out,
+    latent_up,
+    latent_down,
+    qkv_quant,
+    up_quant,
+    out_quant,
+    down_quant,
+    bias_qv,
+    bias_up,
+    row_params,
+    clip_in,
+    clip_ctx,
+    clip_hidden,
+    t_qkv,
+    t_out,
+    t_up,
+    t_down,
+    t_bias_qv,
+    t_bias_up,
+    t_rows,
+):
+    local_len, seq_count, width = tokens.shape
+    share = cotangent.shape[0]
+    col_width = latent_qkv.shape[2]
+    hidden_width = latent_up.shape[1]
+    half_hidden = hidden_width // 2
+    row_width = latent_qkv.shape[0]
+    tp_rank = lax.axis_index("tp")
+    ctx_rank = lax.axis_index("ctx")
+    fsdp_rank = lax.axis_index("fsdp")
+    f32, bf16 = jnp.float32, jnp.bfloat16
+    place = jnp.stack([fsdp_rank, tp_rank, ctx_rank]).astype(jnp.int32)
+
+    def by_distance(value):
+        pairs = value.reshape(2, 2, *value.shape[1:])
+        pairs = jnp.where((tp_rank & 1) > 0, pairs[:, ::-1], pairs)
+        pairs = jnp.where((tp_rank >> 1) > 0, pairs[::-1], pairs)
+        return pairs.reshape(value.shape)
+
+    def mine(value, axis):
+        return lax.dynamic_index_in_dim(value, ctx_rank, axis, keepdims=False)
+
+    def theirs(value, axis):
+        return lax.dynamic_index_in_dim(value, 1 - ctx_rank, axis, keepdims=False)
+
+    def half_of(weight):
+        return mine(weight.reshape(row_width, 2, half_hidden), 1)
+
+    relative = by_distance(tokens.reshape(4, share, seq_count, width))
+    own = mine(relative, 2).reshape(local_len, width)
+    other = swap_ctx(theirs(relative, 2).reshape(local_len, width))
+    code = by_distance(
+        jnp.transpose(segment_ids * 2 + (valid_mask > 0).astype(jnp.int32)).reshape(
+            4, share, seq_count
+        )
+    )
+    code_all = jnp.concatenate(
+        [mine(code, 2).reshape(local_len), swap_ctx(theirs(code, 2)).reshape(local_len)]
+    )
+    code_col, code_row = code_all[:, None], code_all[None, :]
+    valid = (
+        jnp.concatenate([code_all[:share], code_all[local_len : local_len + share]]) & 1
+    ).astype(f32)[:, None]
+    bin_qkv = jnp.transpose(
+        binarize(latent_qkv, qkv_quant[0][None], qkv_quant[1][None]), (1, 0, 2)
+    )
+    student_qkv = fsdp_pieces(bin_qkv)
+    teacher_qkv = fsdp_pieces(jnp.transpose(t_qkv, (1, 0, 2)))
+    bin_out = binarize(latent_out, out_quant[0][:, None], out_quant[1][:, None])
+    bin_up = binarize(latent_up, up_quant[0][None], up_quant[1][None])
+    bin_down = binarize(latent_down, down_quant[0][:, None], down_quant[1][:, None])
+    out_pieces = fsdp_pieces(jnp.stack(tp_pieces(jnp.stack([bin_out, t_out]))))
+
+    def hidden_pieces(up, down):
+        parts = tp_pieces(jnp.stack([half_of(up), half_of(down)]))
+        return fsdp_pieces(jnp.stack(parts[:2])) + fsdp_pieces(jnp.stack(parts[2:]))
+
+    student_hidden = hidden_pieces(bin_up, bin_down)
+    teacher_hidden = hidden_pieces(t_up, t_down)
+    vectors = jnp.stack(
+        tp_pieces(
+            jnp.stack([mine(v.reshape(2, half_hidden), 0) for v in (bias_up, clip_hidden, t_bias_up)])
+        )
+    )
+    bias_up_all, clip_all, t_bias_up_all = vectors[:, 0], vectors[:, 1], vectors[:, 2]
+    clip_in_row, clip_row = clip_in[None], clip_ctx[None]
+
+    context, a_in, q, k, v, ratio, lse = attention_forward(
+        True, place, own, other, student_qkv, bias_qv, clip_in_row, clip_row, code_col, code_row
+    )
+    contexts = exchange_tp(context)
+    (teacher_context,) = attention_forward(
+        False, place, own, other, teacher_qkv, t_bias_qv, clip_in_row, clip_row, code_col, code_row
+    )
+    teacher_contexts = exchange_tp(teacher_context)
+    own_rows, other_rows = own[:share], other[:share]
+    out_full, unit, scale, h_low, first_sums = out_norm(
+        True, place, contexts, out_pieces, own_rows, other_rows, valid, row_params
+    )
+    h_teacher, ht_low = out_norm(
+        False, place, teacher_contexts, out_pieces, own_rows, other_rows, valid, t_rows
+    )
+    h_far = swap_ctx(h_low)
+    ht_far = swap_ctx(ht_low)
+    hidden_full, hid_own, slope_own, part_own = hidden_layer(
+        True, False, place, h_low, student_hidden, bias_up_all, clip_all
+    )
+    hid_far, slope_far, part_far = hidden_layer(
+        True, True, place, h_far, hidden_full, bias_up_all, clip_all
+    )
+    part_got = swap_ctx(part_far)
+    teacher_full, t_part_own = hidden_layer(
+        False, False, place, ht_low, teacher_hidden, t_bias_up_all, None
+    )
+    (t_part_far,) = hidden_layer(False, True, place, ht_far, teacher_full, t_bias_up_all, None)
+    t_part_got = swap_ctx(t_part_far)
+    cot_own = mine(cotangent, 1)
+    cot_other = swap_ctx(theirs(cotangent, 1))
+    layer_own, layer_other, d_second, d_ffn, second_sums = loss_step(
+        place, unit, part_own, part_got, h_teacher, t_part_own, t_part_got,
+        cot_own, cot_other, valid, row_params, t_rows,
+    )
+
+    def home(own_part, other_part):
+        got = swap_ctx(other_part).astype(own_part.dtype)
+        first = jnp.where(ctx_rank == 0, own_part, got)
+        second = jnp.where(ctx_rank == 0, got, own_part)
+        return jnp.stack([first, second], axis=1)
+
+    layer_out = home(layer_own, layer_other)
+    d_ffn_far = swap_ctx(d_ffn)
+    du_own, d_part_own, du_sums_own = hidden_pull(False, place, d_ffn, hidden_full, slope_own)
+    du_far, d_part_far, du_sums_far = hidden_pull(True, place, d_ffn_far, hidden_full, slope_far)
+    d_part_got = swap_ctx(d_part_far)
+    keep_hidden, send_hidden = hidden_grads(
+        place, (d_ffn, d_ffn_far), (hid_own, hid_far), (h_low, h_far), (du_own, du_far)
+    )
+    d_first, d_attn, third_sums, d_context = first_pull(
+        place, d_second, d_part_own, d_part_got, unit, scale, row_params, out_full
+    )
+    d_contexts = exchange_tp(d_context)
+    keep_out, send_out = out_grads(place, d_attn, contexts)
+    back, d_proj, d_bias_qv = attention_backward(
+        place, a_in, q, k, v, ratio, lse, code_col, code_row, d_contexts, student_qkv
+    )
+    backs = exchange_tp(back)
+    keep_in, send_in = in_grads(place, a_in, d_proj)
+    input_own, input_other = input_rows(place, d_first, backs, own_rows, other_rows, clip_in_row)
+    input_grad = home(input_own, input_other)
+
+    def over_fsdp(keep, send):
+        got = swap_core(send)
+        stay = keep[0].astype(f32) + got[0].astype(f32)
+        leave = (keep[1].astype(f32) + got[1].astype(f32)).astype(bf16)
+        return stay + swap_row(leave).astype(f32)
+
+    def over_tp(value, axis):
+        parts = [lax.index_in_dim(value, r, axis, keepdims=False) for r in range(4)]
+        return parts[0] + sum(swap_tp(parts[r].astype(bf16), r).astype(f32) for r in (1, 2, 3))
+
+    low_hidden = over_tp(over_fsdp(keep_hidden, send_hidden), 1).astype(bf16)
+    low_far = swap_ctx(low_hidden)
+    hidden_halves = [
+        jnp.where(ctx_rank == 0, low_hidden, low_far),
+        jnp.where(ctx_rank == 0, low_far, low_hidden),
+    ]
+    grad_hidden = jnp.concatenate(hidden_halves, axis=-1).astype(f32)
+    low_out = over_tp(over_fsdp(keep_out, send_out), 0).astype(bf16)
+    sum_out = low_out.astype(f32) + swap_ctx(low_out).astype(f32)
+    low_in = over_fsdp(keep_in, send_in).astype(bf16)
+    sum_in = low_in.astype(f32) + swap_ctx(low_in).astype(f32)
+    grad_qkv = straight(
+        jnp.transpose(sum_in, (1, 0, 2)), latent_qkv, qkv_quant[0][None], qkv_quant[1][None]
+    )
+    grad_out = straight(sum_out, latent_out, out_quant[0][:, None], out_quant[1][:, None])
+    grad_up = straight(grad_hidden[0], latent_up, up_quant[0][None], up_quant[1][None])
+    grad_down = straight(
+        grad_hidden[1], latent_down, down_quant[0][:, None], down_quant[1][:, None]
+    )
+    placed_up = by_distance(du_sums_own + du_sums_far)
+    placed_up = jnp.where(
+        jnp.arange(2)[None, :, None] == ctx_rank, placed_up[:, None], 0.0
+    ).reshape(hidden_width * 4 // width, width)
+    vector = jnp.concatenate([third_sums, second_sums, first_sums, placed_up], axis=0)
+    vector = vector + swap_core(vector)
+    vector = vector + swap_row(vector)
+    vector = vector + swap_ctx(vector)
+    vector = vector + swap_tp(vector, 1)
+    vector = vector + swap_tp(vector, 2)
+    qv_sums = d_bias_qv + swap_core(d_bias_qv)
+    qv_sums = qv_sums + swap_row(qv_sums)
+    grad_qv = qv_sums + swap_ctx(qv_sums)
+    vector_sums = jnp.concatenate([vector[0:1], vector[3:4], vector[1:3], vector[4:6]], axis=0)
+    stat_sums = jnp.sum(vector[6:11], axis=-1)
+    up_sums = vector[11:].reshape(4 * hidden_width)
+    grad_rows = lax.dynamic_slice_in_dim(vector_sums, fsdp_rank * row_width, row_width, 1)
+    grad_bias_up = lax.dynamic_slice_in_dim(up_sums, tp_rank * hidden_width, hidden_width, 0)
+    denom = stat_sums[2]
+    statistics = jnp.stack(
+        [
+            jnp.sqrt(stat_sums[3] / denom),
+            jnp.sqrt(stat_sums[4] / denom),
+            jnp.sqrt(stat_sums[0] / denom),
+            stat_sums[1] / denom,
+        ]
+    )
+    return (
+        layer_out,
+        input_grad,
+        grad_qkv,
+        grad_out,
+        grad_up,
+        grad_down,
+        grad_rows,
+        grad_qv,
+        grad_bias_up,
+        statistics,
+    )
+
+
+def general_body(
     tokens,
     cotangent,
     segment_ids,
@@ -440,9 +1344,16 @@
     )
 
 
+def pick_body(mesh):
+    sizes = dict(mesh.shape)
+    if sizes["fsdp"] == 4 and sizes["tp"] == 4 and sizes["ctx"] == 2:
+        return paired_body
+    return general_body
+
+
 def solution(mesh):
     return jax.shard_map(
-        body,
+        pick_body(mesh),
         mesh=mesh,
         in_specs=(
             P("ctx", "fsdp", None),

time: 841 us -> 449 us (0.53)
  the two profiles are of different devices: /device:TPU:0 before, /device:TPU:8 now
where the time goes in v1:
time: 449 us; the launch traced here: 442 us
  waiting for transfers between devices  170 us (38%)
  Pallas kernels  117 us (26%)
  starting transfers between devices  72.4 us (16%)
  local copies, waits for them, and re-layouts  41.6 us (9%)
  other arithmetic  33.7 us (8%)
  between operations  7.49 us (2%)
    pallas_call x17, Pallas kernels, call_kernel(): pl.pallas_call(kernel, out_shape=outs, in_specs=[pl.BlockSpec(memory_spac...  117 us
    ppermute x32, waiting for transfers between devices, swap_tp(): return lax.ppermute(value, 'tp', [(i, i ^ distance) for i in range(4)])  97 us
    ppermute x12, waiting for transfers between devices, swap_row(): return lax.ppermute(value, 'fsdp', [(i, i ^ 2) for i in range(4)])  48.7 us
    ppermute x32, starting transfers between devices, swap_tp(): return lax.ppermute(value, 'tp', [(i, i ^ distance) for i in range(4)])  40.1 us
    ppermute x16, waiting for transfers between devices, swap_ctx(): return lax.ppermute(value, 'ctx', [(0, 1), (1, 0)])  23.8 us
    ppermute x16, starting transfers between devices, swap_ctx(): return lax.ppermute(value, 'ctx', [(0, 1), (1, 0)])  16.3 us
    ppermute x12, starting transfers between devices, swap_row(): return lax.ppermute(value, 'fsdp', [(i, i ^ 2) for i in range(4)])  13.8 us
    unnamed x161, local copies, waits for them, and re-layouts  9.48 us
  transfers between devices with their start and end apart: 79, of which 26 were waited for; matrix products, arithmetic and copies ran while one was open for 14% of the time, Pallas kernels for 24%

profile of v1, /device:TPU:8, one launch (start us, length us, event | category | flops | bytes accessed | tf_op | source)
XLA Modules:
  0.0 442.1 jit_solution(17290123145022289621)
XLA Ops:
  2.5 1.7 fusion.23
  4.2 3.0 collective-permute-start.9
  18.2 1.8 reshape.171
  20.1 1.7 reshape.172
  25.7 1.6 collective-permute-start.10
  29.1 6.7 %collective-permute-done.25 = f32[3,384]{1,0:T(4,128)} collective-permute-done((f32[3,384]{1,0:T(4,128)}, f32[3,384]{1,0:T(4,128)}, u32[]{:S(2)}, u32[]{:S(2)}) %collective-permute-start.25) | collective-permute-done | bytes 4640 | tf_op jit(solution)/shard_map/ppermute | solution.py:732
  40.0 5.9 %collective-permute-done.28.w2_ref = bf16[3,192,192]{2,1,0:T(8,128)(2,1)S(1)} collective-permute-done((bf16[3,192,192]{2,1,0:T(8,128)(2,1)}, bf16[3,192,192]{2,1,0:T(8,128)(2,1)S(1)}, u32[]{:S(2)}, u32[]{:S(2)}) %collective-permute-start.28) | collective-permute-done | bytes 221216 | tf_op jit(solution)/shard_map/ppermute | solution.py:728
  46.9 3.4 collective-permute-done.1.w2_ref
  53.3 6.3 %collective-permute-done.38 = bf16[2,192,384]{2,1,0:T(8,128)(2,1)S(1)} collective-permute-done((bf16[2,192,384]{2,1,0:T(8,128)(2,1)}, bf16[2,192,384]{2,1,0:T(8,128)(2,1)S(1)}, u32[]{:S(2)}, u32[]{:S(2)}) %collective-permute-start.38) | collective-permute-done | bytes 294944 | tf_op jit(solution)/shard_map/ppermute | solution.py:732
  61.0 19.0 %collective-permute-done.39 = bf16[2,192,384]{2,1,0:T(8,128)(2,1)} collective-permute-done((bf16[2,192,384]{2,1,0:T(8,128)(2,1)}, bf16[2,192,384]{2,1,0:T(8,128)(2,1)}, u32[]{:S(2)}, u32[]{:S(2)}) %collective-permute-start.39) | collective-permute-done | bytes 294944 | tf_op jit(solution)/shard_map/ppermute | solution.py:732
  81.6 1.9 pad_maximum_fusion.5.refs_4_
  84.6 13.8 %shard_map.316 = bf16[4,2,128,192]{3,2,1,0:T(8,128)(2,1)} custom-call(s32[3]{0:T(128)} %pad_add_fusion.2.place_ref, bf16[512,768]{1,0:T(8,128)(2,1)} %bitcast.188, bf16[512,768]{1,0:T(8,128)(2,1)} %collective-permute-done.other_ref, bf16[3,192,192]{2,1,0:T(8,128)(2,1)} %bitcast.217, bf16[3,192,192]{2,1,0:T(8,128)(2,1)} %copy-done.69, ...), custom_call_target="tpu_custom_call" | custom-call | flops 1711276032 | bytes 4718592 | tf_op jit(solution)/shard_map/pallas_call | solution.py:78
  98.6 1.8 slice_bitcast_fusion.11
  101.0 1.8 collective-permute-start.31
  102.8 1.8 pad_maximum_fusion.4.refs_0_
  106.7 2.3 collective-permute-start.32
  108.9 1.9 pad_maximum_fusion.3.refs_4_
  110.9 3.3 collective-permute-done.32.c2
  115.1 14.1 %shard_map.312 = (bf16[4,2,128,192]{3,2,1,0:T(8,128)(2,1)}, bf16[1024,768]{1,0:T(8,128)(2,1)}, bf16[3,1024,64]{2,1,0:T(8,128)(2,1)}, bf16[3,1024,64]{2,1,0:T(8,1...) custom-call(s32[3]{0:T(128)} %pad_add_fusion.2.place_ref, ...), custom_call_target="tpu_custom_call" | custom-call | flops 1711276032 | bytes 4718592 | tf_op jit(solution)/shard_map/pallas_call | solution.py:78
  130.6 1.8 slice_bitcast_fusion.19
  132.4 3.9 collective-permute-start.5
  136.3 1.8 pad_maximum_fusion.2.refs_0_
  139.4 2.2 collective-permute-start.6
  142.3 3.7 collective-permute-done.6.c2
  147.8 4.6 %collective-permute-done.7.c3 = bf16[2,128,192]{2,1,0:T(8,128)(2,1)S(1)} collective-permute-done((bf16[2,128,192]{2,1,0:T(8,128)(2,1)S(1)}, bf16[2,128,192]{2,1,0:T(8,128)(2,1)S(1)}, u32[]{:S(2)}, u32[]{:S(2)}) %collective-permute-start.7) | collective-permute-done | bytes 98336 | tf_op jit(solution)/shard_map/ppermute | solution.py:732
  154.5 2.3 collective-permute-done.15.refs_1_
  161.0 1.6 slice.276.other_ref
  162.7 4.2 shard_map.317
  166.8 4.3 shard_map.313
  173.8 6.4 %shard_map.318 = (bf16[4,2,768,384]{3,2,1,0:T(8,128)(2,1)}, f32[256,768]{1,0:T(8,128)}) custom-call(s32[3]{0:T(128)} %pad_add_fusion.2.place_ref, bf16[256,768]{1,0:T(8,128)(2,1)} %get-tuple-element.66.h_ref, bf16[2,2,192,384]{3,2,1,0:T(8,128)(2,1)} %pad_maximum_fusion.4.refs_0_, bf16[2,2,192,384]{3,2,1,0:T(8,128)(2,1)} %collective-permute-done.35.refs_1_, ...), custom_call_target="tpu_custom_call" | custom-call | flops 1207959552 | bytes 6291456 | tf_op jit(solution)/shard_map/pallas_call | solution.py:78
  181.4 7.3 %shard_map.314 = (bf16[4,2,768,384]{3,2,1,0:T(8,128)(2,1)}, bf16[4,256,384]{2,1,0:T(8,128)(2,1)}, bf16[4,256,384]{2,1,0:T(8,128)(2,1)}, f32[256,768]{1,0:T(8,128)}) custom-call(s32[3]{0:T(128)} %pad_add_fusion.2.place_ref, bf16[256,768]{1,0:T(8,128)(2,1)} %get-tuple-element.61.h_ref.h0, bf16[2,2,192,384]{3,2,1,0:T(8,128)(2,1)} %pad_maximum_fusion.2.refs_0_, ...), custom_call_target="tpu_custom_call" | custom-call | flops 1207959552 | bytes 6291456 | tf_op jit(solution)/shard_map/pallas_call | solution.py:78
  189.5 5.1 %shard_map.319 = bf16[256,768]{1,0:T(8,128)(2,1)} custom-call(s32[3]{0:T(128)} %pad_add_fusion.2.place_ref, bf16[256,768]{1,0:T(8,128)(2,1)} %copy-done.27, bf16[4,2,768,384]{3,2,1,0:T(8,128)(2,1)} %get-tuple-element.68.refs_0_, f32[4,384]{1,0:T(4,128)} %get-tuple-element.188.refs_8_.refs_1_), custom_call_target="tpu_custom_call" | custom-call | flops 1207959552 | bytes 6291456 | tf_op jit(solution)/shard_map/pallas_call | solution.py:78
  195.8 5.9 %shard_map.315 = (bf16[4,256,384]{2,1,0:T(8,128)(2,1)}, bf16[4,256,384]{2,1,0:T(8,128)(2,1)}, bf16[256,768]{1,0:T(8,128)(2,1)}) custom-call(s32[3]{0:T(128)} %pad_add_fusion.2.place_ref, bf16[256,768]{1,0:T(8,128)(2,1)} %copy-done.23, bf16[4,2,768,384]{3,2,1,0:T(8,128)(2,1)} %get-tuple-element.63.refs_0_.w_ref, f32[4,384]{1,0:T(4,128)} %get-tuple-element.190.refs_8_.refs_1_, ...), custom_call_target="tpu_custom_call" | custom-call | flops 1207959552 | bytes 6291456 | tf_op jit(solution)/shard_map/pallas_call | solution.py:78
  205.6 12.4 %collective-permute-done.45.cot_other_ref = bf16[128,768]{1,0:T(8,128)(2,1)S(1)} collective-permute-done((bf16[128,768]{1,0:T(8,128)(2,1)S(1)}, bf16[128,768]{1,0:T(8,128)(2,1)S(1)}, u32[]{:S(2)}, u32[]{:S(2)}) %collective-permute-start.45) | collective-permute-done | bytes 196640 | tf_op jit(solution)/shard_map/ppermute | solution.py:720
  219.0 4.7 %shard_map.320 = (bf16[128,768]{1,0:T(8,128)(2,1)}, bf16[128,768]{1,0:T(8,128)(2,1)}, f32[256,768]{1,0:T(8,128)}, bf16[256,768]{1,0:T(8,128)(2,1)}, f32[5,768]{1,0:T(8,128)}) custom-call(s32[3]{0:T(128)} %pad_add_fusion.2.place_ref, f32[256,768]{1,0:T(8,128)} %get-tuple-element.60.unit_ref, f32[256,768]{1,0:T(8,128)} %get-tuple-element.62.ffn_ref, ...), custom_call_target="tpu_custom_call" | custom-call | flops 11796480 | bytes 5898240 | tf_op jit(solution)/shard_map/pallas_call | solution.py:78
  225.8 5.5 %shard_map.321 = (bf16[4,256,384]{2,1,0:T(8,128)(2,1)}, f32[256,768]{1,0:T(8,128)}, f32[4,384]{1,0:T(4,128)}) custom-call(s32[3]{0:T(128)} %pad_add_fusion.2.place_ref, bf16[256,768]{1,0:T(8,128)(2,1)} %get-tuple-element.72.grad_ref.f0, bf16[4,2,768,384]{3,2,1,0:T(8,128)(2,1)} %get-tuple-element.63.refs_0_.w_ref, ...), custom_call_target="tpu_custom_call" | custom-call | flops 1207959552 | bytes 6291456 | tf_op jit(solution)/shard_map/pallas_call | solution.py:78
  231.4 6.5 %collective-permute-done.46 = bf16[128,768]{1,0:T(8,128)(2,1)S(1)} collective-permute-done((bf16[128,768]{1,0:T(8,128)(2,1)}, bf16[128,768]{1,0:T(8,128)(2,1)S(1)}, u32[]{:S(2)}, u32[]{:S(2)}) %collective-permute-start.46) | collective-permute-done | bytes 196640 | tf_op jit(solution)/shard_map/ppermute | solution.py:720
  238.7 5.4 %shard_map.322 = (bf16[4,256,384]{2,1,0:T(8,128)(2,1)}, bf16[256,768]{1,0:T(8,128)(2,1)}, f32[4,384]{1,0:T(4,128)}) custom-call(s32[3]{0:T(128)} %pad_add_fusion.2.place_ref, bf16[256,768]{1,0:T(8,128)(2,1)} %copy-done.25, bf16[4,2,768,384]{3,2,1,0:T(8,128)(2,1)} %get-tuple-element.63.refs_0_.w_ref, bf16[4,256,384]{2,1,0:T(8,128)(2,1)} %get-tuple-element.75.slope_ref), custom_call_target="tpu_custom_call" | custom-call | flops 1207959552 | bytes 6291456 | tf_op jit(solution)/shard_map/pallas_call | solution.py:78
  245.8 8.0 %shard_map.328 = (bf16[2,2,4,192,384]{4,3,2,1,0:T(8,128)(2,1)}, bf16[2,2,4,192,384]{4,3,2,1,0:T(8,128)(2,1)}) custom-call(s32[3]{0:T(128)} %pad_add_fusion.2.place_ref, bf16[256,768]{1,0:T(8,128)(2,1)} %get-tuple-element.72.grad_ref.f0, bf16[256,768]{1,0:T(8,128)(2,1)} %copy-done.25, bf16[4,256,384]{2,1,0:T(8,128)(2,1)} %get-tuple-element.96.hid0, ...), custom_call_target="tpu_custom_call" | custom-call | flops 2415919104 | bytes 9437184 | tf_op jit(solution)/shard_map/pallas_call | solution.py:78
  254.9 4.1 shard_map.323
  260.1 1.8 slice_bitcast_fusion.15
  261.8 3.9 collective-permute-start.49
  267.9 1.8 collective-permute-start.72
  273.4 2.2 collective-permute-done.50.d2_ref
  275.6 3.7 collective-permute-done.51.d3_ref
  280.0 18.2 %shard_map.324 = (bf16[4,2,128,768]{3,2,1,0:T(8,128)(2,1)}, bf16[3,1024,192]{2,1,0:T(8,128)(2,1)}, f32[2,192]{1,0:T(2,128)}) custom-call(s32[3]{0:T(128)} %pad_add_fusion.2.place_ref, bf16[1024,768]{1,0:T(8,128)(2,1)} %get-tuple-element.80.a_ref, bf16[3,1024,64]{2,1,0:T(8,128)(2,1)} %get-tuple-element.81.q_ref, ...), custom_call_target="tpu_custom_call" | custom-call | flops 2919235584 | bytes 6291456 | tf_op jit(solution)/shard_map/pallas_call | solution.py:78
  298.2 3.2 shard_map.327
  302.0 1.7 collective-permute-start.77
  303.8 4.5 %shard_map.326 = (bf16[2,3,192,192]{3,2,1,0:T(8,128)(2,1)}, bf16[2,3,192,192]{3,2,1,0:T(8,128)(2,1)}) custom-call(s32[3]{0:T(128)} %pad_add_fusion.2.place_ref, bf16[1024,768]{1,0:T(8,128)(2,1)} %get-tuple-element.80.a_ref, bf16[3,1024,192]{2,1,0:T(8,128)(2,1)} %get-tuple-element.90.d_ref), custom_call_target="tpu_custom_call" | custom-call | flops 905969664 | bytes 3145728 | tf_op jit(solution)/shard_map/pallas_call | solution.py:78
  309.6 2.3 collective-permute-start.75
  313.1 2.4 collective-permute-start.53
  324.0 5.6 %collective-permute-done.52.b1 = bf16[2,128,768]{2,1,0:T(8,128)(2,1)S(1)} collective-permute-done((bf16[2,128,768]{2,1,0:T(8,128)(2,1)S(1)}, bf16[2,128,768]{2,1,0:T(8,128)(2,1)S(1)}, u32[]{:S(2)}, u32[]{:S(2)}) %collective-permute-start.52) | collective-permute-done | bytes 393248 | tf_op jit(solution)/shard_map/ppermute | solution.py:732
  332.2 10.1 %collective-permute-done.53.b2 = bf16[2,128,768]{2,1,0:T(8,128)(2,1)} collective-permute-done((bf16[2,128,768]{2,1,0:T(8,128)(2,1)}, bf16[2,128,768]{2,1,0:T(8,128)(2,1)}, u32[]{:S(2)}, u32[]{:S(2)}) %collective-permute-start.53) | collective-permute-done | bytes 393248 | tf_op jit(solution)/shard_map/ppermute | solution.py:732
  342.2 8.5 %collective-permute-done.54.b3 = bf16[2,128,768]{2,1,0:T(8,128)(2,1)} collective-permute-done((bf16[2,128,768]{2,1,0:T(8,128)(2,1)}, bf16[2,128,768]{2,1,0:T(8,128)(2,1)}, u32[]{:S(2)}, u32[]{:S(2)}) %collective-permute-start.54) | collective-permute-done | bytes 393248 | tf_op jit(solution)/shard_map/ppermute | solution.py:732
  350.7 2.7 shard_map.325
  354.4 1.7 fusion
  357.6 1.8 collective-permute-start.57
  361.4 35.8 %collective-permute-done.60 = bf16[4,192,192]{2,1,0:T(8,128)(2,1)S(1)} collective-permute-done((bf16[4,192,192]{2,1,0:T(8,128)(2,1)S(1)}, bf16[4,192,192]{2,1,0:T(8,128)(2,1)S(1)}, u32[]{:S(2)}, u32[]{:S(2)}) %collective-permute-start.60) | collective-permute-done | bytes 294944 | tf_op jit(solution)/shard_map/ppermute | solution.py:728
  397.5 2.5 collective-permute-start.62
  401.0 1.8 fusion.26
  410.4 3.2 collective-permute-done.67
  413.5 12.9 %collective-permute-done.68 = bf16[2,192,384]{2,1,0:T(8,128)(2,1)S(1)} collective-permute-done((bf16[2,192,384]{2,1,0:T(8,128)(2,1)S(1)}, bf16[2,192,384]{2,1,0:T(8,128)(2,1)S(1)}, u32[]{:S(2)}, u32[]{:S(2)}) %collective-permute-start.68) | collective-permute-done | bytes 294944 | tf_op jit(solution)/shard_map/ppermute | solution.py:732
  426.5 6.2 %collective-permute-done.69 = bf16[2,192,384]{2,1,0:T(8,128)(2,1)S(1)} collective-permute-done((bf16[2,192,384]{2,1,0:T(8,128)(2,1)S(1)}, bf16[2,192,384]{2,1,0:T(8,128)(2,1)S(1)}, u32[]{:S(2)}, u32[]{:S(2)}) %collective-permute-start.69) | collective-permute-done | bytes 294944 | tf_op jit(solution)/shard_map/ppermute | solution.py:732
  435.7 4.5 %collective-permute-done.70 = bf16[2,192,384]{2,1,0:T(8,128)(2,1)S(1)} collective-permute-done((bf16[2,192,384]{2,1,0:T(8,128)(2,1)S(1)}, bf16[2,192,384]{2,1,0:T(8,128)(2,1)S(1)}, u32[]{:S(2)}, u32[]{:S(2)}) %collective-permute-start.70) | collective-permute-done | bytes 294944 | tf_op jit(solution)/shard_map/ppermute | solution.py:720
  (380 shorter events, 95.9 us)
Async XLA Ops:
  4.2 33.1 %collective-permute-start.8 = (bf16[2,192,192]{2,1,0:T(8,128)(2,1)}, bf16[2,192,192]{2,1,0:T(8,128)(2,1)S(1)}, u32[]{:S(2)}, u32[]{:S(2)}) collective-permute-start(bf16[2,192,192]{2,1,0:T(8,128)(2,1)} %get-tuple-element.183), channel_id=1, source_target_pairs={{0,1},{1,0},{2,3},{3,2},{4,5},{5,4},{6,7},{7,6},{8,9},{9,8},{10,11... | collective-permute-start | bytes 442376 | tf_op jit(solution)/shard_map/ppermute | solution.py:732
  4.2 33.1 %collective-permute-start.9 = (bf16[2,192,192]{2,1,0:T(8,128)(2,1)}, bf16[2,192,192]{2,1,0:T(8,128)(2,1)}, u32[]{:S(2)}, u32[]{:S(2)}) collective-permute-start(bf16[2,192,192]{2,1,0:T(8,128)(2,1)} %get-tuple-element.183), channel_id=1, source_target_pairs={{0,2},{1,3},{2,0},{3,1},{4,6},{5,7},{6,4},{7,5},{8,10},{9,11},{10,... | collective-permute-start | bytes 442376 | tf_op jit(solution)/shard_map/ppermute | solution.py:732
  9.9 17.4 %collective-permute-start.23 = (f32[3,384]{1,0:T(4,128)}, f32[3,384]{1,0:T(4,128)}, u32[]{:S(2)}, u32[]{:S(2)}) collective-permute-start(f32[3,384]{1,0:T(4,128)} %get-tuple-element.194), channel_id=1, source_target_pairs={{0,1},{1,0},{2,3},{3,2},{4,5},{5,4},{6,7},{7,6},{8,9},{9,8},{10,11... | collective-permute-start | bytes 13832 | tf_op jit(solution)/shard_map/ppermute | solution.py:732
  11.5 16.3 %collective-permute-start.24 = (f32[3,384]{1,0:T(4,128)}, f32[3,384]{1,0:T(4,128)}, u32[]{:S(2)}, u32[]{:S(2)}) collective-permute-start(f32[3,384]{1,0:T(4,128)} %get-tuple-element.194), channel_id=1, source_target_pairs={{0,2},{1,3},{2,0},{3,1},{4,6},{5,7},{6,4},{7,5},{8,10},{9,11},{10,... | collective-permute-start | bytes 13832 | tf_op jit(solution)/shard_map/ppermute | solution.py:732
  13.2 12.4 %collective-permute-start.4 = (s32[4,128]{1,0:T(4,128)}, s32[4,128]{1,0:T(4,128)}, u32[]{:S(2)}, u32[]{:S(2)}) collective-permute-start(s32[4,128]{1,0:T(4,128)} %bitcast.12), channel_id=1, source_target_pairs={{0,4},{4,0},{1,5},{5,1},{2,6},{6,2},{3,7},{7,3},{8,12},{12,8},{9,1... | collective-permute-start | bytes 6152 | tf_op jit(solution)/shard_map/ppermute | solution.py:720
  25.7 13.1 %collective-permute-start.10 = (bf16[2,192,192]{2,1,0:T(8,128)(2,1)}, bf16[2,192,192]{2,1,0:T(8,128)(2,1)}, u32[]{:S(2)}, u32[]{:S(2)}) collective-permute-start(bf16[2,192,192]{2,1,0:T(8,128)(2,1)} %get-tuple-element.183), channel_id=1, source_target_pairs={{0,3},{1,2},{2,1},{3,0},{4,7},{5,6},{6,5},{7,4},{8,11},{9,10},{10,... | collective-permute-start | bytes 442376 | tf_op jit(solution)/shard_map/ppermute | solution.py:732
  27.3 8.5 %collective-permute-start.25 = (f32[3,384]{1,0:T(4,128)}, f32[3,384]{1,0:T(4,128)}, u32[]{:S(2)}, u32[]{:S(2)}) collective-permute-start(f32[3,384]{1,0:T(4,128)} %get-tuple-element.194), channel_id=1, source_target_pairs={{0,3},{1,2},{2,1},{3,0},{4,7},{5,6},{6,5},{7,4},{8,11},{9,10},{10,... | collective-permute-start | bytes 13832 | tf_op jit(solution)/shard_map/ppermute | solution.py:732
  27.8 56.8 %collective-permute-start = (bf16[512,768]{1,0:T(8,128)(2,1)}, bf16[512,768]{1,0:T(8,128)(2,1)}, u32[]{:S(2)}, u32[]{:S(2)}) collective-permute-start(bf16[512,768]{1,0:T(8,128)(2,1)} %bitcast.190), channel_id=1, source_target_pairs={{0,4},{4,0},{1,5},{5,1},{2,6},{6,2},{3,7},{7,3},{8,12},{12,8},{9,1... | collective-permute-start | bytes 2359304 | tf_op jit(solution)/shard_map/ppermute | solution.py:720
  35.8 10.2 %collective-permute-start.28 = (bf16[3,192,192]{2,1,0:T(8,128)(2,1)}, bf16[3,192,192]{2,1,0:T(8,128)(2,1)S(1)}, u32[]{:S(2)}, u32[]{:S(2)}) collective-permute-start(bf16[3,192,192]{2,1,0:T(8,128)(2,1)} %bitcast.215), channel_id=1, source_target_pairs={{0,16},{8,24},{16,0},{24,8},{1,17},{9,25},{17,1},{25,9},{2,18},{10... | collective-permute-start | bytes 663560 | tf_op jit(solution)/shard_map/ppermute | solution.py:728
  37.3 9.2 %collective-permute-start.29 = (bf16[3,192,192]{2,1,0:T(8,128)(2,1)}, bf16[3,192,192]{2,1,0:T(8,128)(2,1)S(1)}, u32[]{:S(2)}, u32[]{:S(2)}) collective-permute-start(bf16[3,192,192]{2,1,0:T(8,128)(2,1)} %bitcast.216), channel_id=1, source_target_pairs={{0,8},{8,0},{16,24},{24,16},{1,9},{9,1},{17,25},{25,17},{2,10},{10... | collective-permute-start | bytes 663560 | tf_op jit(solution)/shard_map/ppermute | solution.py:724
  37.3 13.0 %collective-permute-start.1 = (bf16[3,192,192]{2,1,0:T(8,128)(2,1)}, bf16[3,192,192]{2,1,0:T(8,128)(2,1)S(1)}, u32[]{:S(2)}, u32[]{:S(2)}) collective-permute-start(bf16[3,192,192]{2,1,0:T(8,128)(2,1)} %fusion.11.w0_ref), channel_id=1, source_target_pairs={{0,16},{8,24},{16,0},{24,8},{1,17},{9,25},{17,1},{25,9},{2,18},{10... | collective-permute-start | bytes 663560 | tf_op jit(solution)/shard_map/ppermute | solution.py:728
  38.8 20.8 %collective-permute-start.38 = (bf16[2,192,384]{2,1,0:T(8,128)(2,1)}, bf16[2,192,384]{2,1,0:T(8,128)(2,1)S(1)}, u32[]{:S(2)}, u32[]{:S(2)}) collective-permute-start(bf16[2,192,384]{2,1,0:T(8,128)(2,1)} %get-tuple-element.179), channel_id=1, source_target_pairs={{0,2},{1,3},{2,0},{3,1},{4,6},{5,7},{6,4},{7,5},{8,10},{9,11},{10,... | collective-permute-start | bytes 884744 | tf_op jit(solution)/shard_map/ppermute | solution.py:732
  45.9 34.2 %collective-permute-start.39 = (bf16[2,192,384]{2,1,0:T(8,128)(2,1)}, bf16[2,192,384]{2,1,0:T(8,128)(2,1)}, u32[]{:S(2)}, u32[]{:S(2)}) collective-permute-start(bf16[2,192,384]{2,1,0:T(8,128)(2,1)} %get-tuple-element.179), channel_id=1, source_target_pairs={{0,3},{1,2},{2,1},{3,0},{4,7},{5,6},{6,5},{7,4},{8,11},{9,10},{10,... | collective-permute-start | bytes 884744 | tf_op jit(solution)/shard_map/ppermute | solution.py:732
  46.5 35.1 %collective-permute-start.34 = (bf16[2,192,384]{2,1,0:T(8,128)(2,1)}, bf16[2,192,384]{2,1,0:T(8,128)(2,1)}, u32[]{:S(2)}, u32[]{:S(2)}) collective-permute-start(bf16[2,192,384]{2,1,0:T(8,128)(2,1)} %get-tuple-element.179), channel_id=1, source_target_pairs={{0,1},{1,0},{2,3},{3,2},{4,5},{5,4},{6,7},{7,6},{8,9},{9,8},{10,11... | collective-permute-start | bytes 884744 | tf_op jit(solution)/shard_map/ppermute | solution.py:732
  53.3 45.1 %collective-permute-start.18 = (bf16[2,192,384]{2,1,0:T(8,128)(2,1)}, bf16[2,192,384]{2,1,0:T(8,128)(2,1)}, u32[]{:S(2)}, u32[]{:S(2)}) collective-permute-start(bf16[2,192,384]{2,1,0:T(8,128)(2,1)} %get-tuple-element.181), channel_id=1, source_target_pairs={{0,2},{1,3},{2,0},{3,1},{4,6},{5,7},{6,4},{7,5},{8,10},{9,11},{10,... | collective-permute-start | bytes 884744 | tf_op jit(solution)/shard_map/ppermute | solution.py:732
  59.6 23.9 %collective-permute-start.30 = (bf16[3,192,192]{2,1,0:T(8,128)(2,1)}, bf16[3,192,192]{2,1,0:T(8,128)(2,1)S(1)}, u32[]{:S(2)}, u32[]{:S(2)}) collective-permute-start(bf16[3,192,192]{2,1,0:T(8,128)(2,1)} %copy-done.69), channel_id=1, source_target_pairs={{0,8},{8,0},{16,24},{24,16},{1,9},{9,1},{17,25},{25,17},{2,10},{10... | collective-permute-start | bytes 663560 | tf_op jit(solution)/shard_map/ppermute | solution.py:724
  80.1 24.6 %collective-permute-start.11 = (bf16[4,2,192,192]{3,2,1,0:T(8,128)(2,1)S(1)}, bf16[4,2,192,192]{3,2,1,0:T(8,128)(2,1)S(1)}, u32[]{:S(2)}, u32[]{:S(2)}) collective-permute-start(bf16[4,2,192,192]{3,2,1,0:T(8,128)(2,1)S(1)} %pad_maximum_fusion.w0), channel_id=1, source_target_pairs={{0,16},{8,24},{16,0},{24,8},{1,17},{9,25},{17,1},{25,9},{2,18},{10... | collective-permute-start | bytes 1769480 | tf_op jit(solution)/shard_map/ppermute | solution.py:728
  81.6 24.6 %collective-permute-start.12 = (bf16[4,2,192,192]{3,2,1,0:T(8,128)(2,1)S(1)}, bf16[4,2,192,192]{3,2,1,0:T(8,128)(2,1)}, u32[]{:S(2)}, u32[]{:S(2)}) collective-permute-start(bf16[4,2,192,192]{3,2,1,0:T(8,128)(2,1)S(1)} %pad_maximum_fusion.w0), channel_id=1, source_target_pairs={{0,8},{8,0},{16,24},{24,16},{1,9},{9,1},{17,25},{25,17},{2,10},{10... | collective-permute-start | bytes 1769480 | tf_op jit(solution)/shard_map/ppermute | solution.py:724
  83.5 16.9 %collective-permute-start.19 = (bf16[2,192,384]{2,1,0:T(8,128)(2,1)}, bf16[2,192,384]{2,1,0:T(8,128)(2,1)}, u32[]{:S(2)}, u32[]{:S(2)}) collective-permute-start(bf16[2,192,384]{2,1,0:T(8,128)(2,1)} %get-tuple-element.181), channel_id=1, source_target_pairs={{0,3},{1,2},{2,1},{3,0},{4,7},{5,6},{6,5},{7,4},{8,11},{9,10},{10,... | collective-permute-start | bytes 884744 | tf_op jit(solution)/shard_map/ppermute | solution.py:732
  84.6 16.4 %collective-permute-start.14 = (bf16[2,192,384]{2,1,0:T(8,128)(2,1)}, bf16[2,192,384]{2,1,0:T(8,128)(2,1)}, u32[]{:S(2)}, u32[]{:S(2)}) collective-permute-start(bf16[2,192,384]{2,1,0:T(8,128)(2,1)} %get-tuple-element.181), channel_id=1, source_target_pairs={{0,1},{1,0},{2,3},{3,2},{4,5},{5,4},{6,7},{7,6},{8,9},{9,8},{10,11... | collective-permute-start | bytes 884744 | tf_op jit(solution)/shard_map/ppermute | solution.py:732
  100.5 31.9 %collective-permute-start.40 = (bf16[2,2,192,384]{3,2,1,0:T(8,128)(2,1)}, bf16[2,2,192,384]{3,2,1,0:T(8,128)(2,1)}, u32[]{:S(2)}, u32[]{:S(2)}) collective-permute-start(bf16[2,2,192,384]{3,2,1,0:T(8,128)(2,1)} %pad_maximum_fusion.5.refs_4_), channel_id=1, source_target_pairs={{0,16},{8,24},{16,0},{24,8},{1,17},{9,25},{17,1},{25,9},{2,18},{10... | collective-permute-start | bytes 1769480 | tf_op jit(solution)/shard_map/ppermute | solution.py:728
  104.6 33.5 %collective-permute-start.41 = (bf16[2,2,192,384]{3,2,1,0:T(8,128)(2,1)}, bf16[2,2,192,384]{3,2,1,0:T(8,128)(2,1)}, u32[]{:S(2)}, u32[]{:S(2)}) collective-permute-start(bf16[2,2,192,384]{3,2,1,0:T(8,128)(2,1)} %pad_maximum_fusion.5.refs_4_), channel_id=1, source_target_pairs={{0,8},{8,0},{16,24},{24,16},{1,9},{9,1},{17,25},{25,17},{2,10},{10... | collective-permute-start | bytes 1769480 | tf_op jit(solution)/shard_map/ppermute | solution.py:724
  104.7 33.4 %collective-permute-start.35 = (bf16[2,2,192,384]{3,2,1,0:T(8,128)(2,1)}, bf16[2,2,192,384]{3,2,1,0:T(8,128)(2,1)}, u32[]{:S(2)}, u32[]{:S(2)}) collective-permute-start(bf16[2,2,192,384]{3,2,1,0:T(8,128)(2,1)} %pad_maximum_fusion.4.refs_0_), channel_id=1, source_target_pairs={{0,16},{8,24},{16,0},{24,8},{1,17},{9,25},{17,1},{25,9},{2,18},{10... | collective-permute-start | bytes 1769480 | tf_op jit(solution)/shard_map/ppermute | solution.py:728
  106.2 32.7 %collective-permute-start.36 = (bf16[2,2,192,384]{3,2,1,0:T(8,128)(2,1)}, bf16[2,2,192,384]{3,2,1,0:T(8,128)(2,1)}, u32[]{:S(2)}, u32[]{:S(2)}) collective-permute-start(bf16[2,2,192,384]{3,2,1,0:T(8,128)(2,1)} %pad_maximum_fusion.4.refs_0_), channel_id=1, source_target_pairs={{0,8},{8,0},{16,24},{24,16},{1,9},{9,1},{17,25},{25,17},{2,10},{10... | collective-permute-start | bytes 1769480 | tf_op jit(solution)/shard_map/ppermute | solution.py:724
  106.7 7.5 %collective-permute-start.32 = (bf16[2,128,192]{2,1,0:T(8,128)(2,1)S(1)}, bf16[2,128,192]{2,1,0:T(8,128)(2,1)S(1)}, u32[]{:S(2)}, u32[]{:S(2)}) collective-permute-start(bf16[2,128,192]{2,1,0:T(8,128)(2,1)S(1)} %get-tuple-element.164), channel_id=1, source_target_pairs={{0,2},{1,3},{2,0},{3,1},{4,6},{5,7},{6,4},{7,5},{8,10},{9,11},{10,... | collective-permute-start | bytes 294920 | tf_op jit(solution)/shard_map/ppermute | solution.py:732
  114.2 15.1 %collective-permute-start.33 = (bf16[2,128,192]{2,1,0:T(8,128)(2,1)}, bf16[2,128,192]{2,1,0:T(8,128)(2,1)S(1)}, u32[]{:S(2)}, u32[]{:S(2)}) collective-permute-start(bf16[2,128,192]{2,1,0:T(8,128)(2,1)} %get-tuple-element.163), channel_id=1, source_target_pairs={{0,3},{1,2},{2,1},{3,0},{4,7},{5,6},{6,5},{7,4},{8,11},{9,10},{10,... | collective-permute-start | bytes 294920 | tf_op jit(solution)/shard_map/ppermute | solution.py:732
  129.2 23.2 %collective-permute-start.20 = (bf16[2,2,192,384]{3,2,1,0:T(8,128)(2,1)}, bf16[2,2,192,384]{3,2,1,0:T(8,128)(2,1)}, u32[]{:S(2)}, u32[]{:S(2)}) collective-permute-start(bf16[2,2,192,384]{3,2,1,0:T(8,128)(2,1)} %pad_maximum_fusion.3.refs_4_), channel_id=1, source_target_pairs={{0,16},{8,24},{16,0},{24,8},{1,17},{9,25},{17,1},{25,9},{2,18},{10... | collective-permute-start | bytes 1769480 | tf_op jit(solution)/shard_map/ppermute | solution.py:728
  138.1 16.3 %collective-permute-start.21 = (bf16[2,2,192,384]{3,2,1,0:T(8,128)(2,1)}, bf16[2,2,192,384]{3,2,1,0:T(8,128)(2,1)}, u32[]{:S(2)}, u32[]{:S(2)}) collective-permute-start(bf16[2,2,192,384]{3,2,1,0:T(8,128)(2,1)} %pad_maximum_fusion.3.refs_4_), channel_id=1, source_target_pairs={{0,8},{8,0},{16,24},{24,16},{1,9},{9,1},{17,25},{25,17},{2,10},{10... | collective-permute-start | bytes 1769480 | tf_op jit(solution)/shard_map/ppermute | solution.py:724
  138.1 18.7 %collective-permute-start.15 = (bf16[2,2,192,384]{3,2,1,0:T(8,128)(2,1)}, bf16[2,2,192,384]{3,2,1,0:T(8,128)(2,1)}, u32[]{:S(2)}, u32[]{:S(2)}) collective-permute-start(bf16[2,2,192,384]{3,2,1,0:T(8,128)(2,1)} %pad_maximum_fusion.2.refs_0_), channel_id=1, source_target_pairs={{0,16},{8,24},{16,0},{24,8},{1,17},{9,25},{17,1},{25,9},{2,18},{10... | collective-permute-start | bytes 1769480 | tf_op jit(solution)/shard_map/ppermute | solution.py:728
  138.9 17.9 %collective-permute-start.13 = (bf16[4,2,192,192]{3,2,1,0:T(8,128)(2,1)S(1)}, bf16[4,2,192,192]{3,2,1,0:T(8,128)(2,1)S(1)}, u32[]{:S(2)}, u32[]{:S(2)}) collective-permute-start(bf16[4,2,192,192]{3,2,1,0:T(8,128)(2,1)S(1)} %collective-permute-done.11.w2), channel_id=1, source_target_pairs={{0,8},{8,0},{16,24},{24,16},{1,9},{9,1},{17,25},{25,17},{2,10},{10... | collective-permute-start | bytes 1769480 | tf_op jit(solution)/shard_map/ppermute | solution.py:724
  152.4 18.7 %collective-permute-start.42 = (bf16[2,2,192,384]{3,2,1,0:T(8,128)(2,1)}, bf16[2,2,192,384]{3,2,1,0:T(8,128)(2,1)S(1)}, u32[]{:S(2)}, u32[]{:S(2)}) collective-permute-start(bf16[2,2,192,384]{3,2,1,0:T(8,128)(2,1)} %collective-permute-done.40.refs_5_), channel_id=1, source_target_pairs={{0,8},{8,0},{16,24},{24,16},{1,9},{9,1},{17,25},{25,17},{2,10},{10... | collective-permute-start | bytes 1769480 | tf_op jit(solution)/shard_map/ppermute | solution.py:724
  152.4 19.3 %collective-permute-start.37 = (bf16[2,2,192,384]{3,2,1,0:T(8,128)(2,1)}, bf16[2,2,192,384]{3,2,1,0:T(8,128)(2,1)}, u32[]{:S(2)}, u32[]{:S(2)}) collective-permute-start(bf16[2,2,192,384]{3,2,1,0:T(8,128)(2,1)} %collective-permute-done.35.refs_1_), channel_id=1, source_target_pairs={{0,8},{8,0},{16,24},{24,16},{1,9},{9,1},{17,25},{25,17},{2,10},{10... | collective-permute-start | bytes 1769480 | tf_op jit(solution)/shard_map/ppermute | solution.py:724
  154.4 25.8 %collective-permute-start.16 = (bf16[2,2,192,384]{3,2,1,0:T(8,128)(2,1)}, bf16[2,2,192,384]{3,2,1,0:T(8,128)(2,1)S(1)}, u32[]{:S(2)}, u32[]{:S(2)}) collective-permute-start(bf16[2,2,192,384]{3,2,1,0:T(8,128)(2,1)} %pad_maximum_fusion.2.refs_0_), channel_id=1, source_target_pairs={{0,8},{8,0},{16,24},{24,16},{1,9},{9,1},{17,25},{25,17},{2,10},{10... | collective-permute-start | bytes 1769480 | tf_op jit(solution)/shard_map/ppermute | solution.py:724
  156.9 23.4 %collective-permute-start.22 = (bf16[2,2,192,384]{3,2,1,0:T(8,128)(2,1)}, bf16[2,2,192,384]{3,2,1,0:T(8,128)(2,1)S(1)}, u32[]{:S(2)}, u32[]{:S(2)}) collective-permute-start(bf16[2,2,192,384]{3,2,1,0:T(8,128)(2,1)} %collective-permute-done.20.refs_5_), channel_id=1, source_target_pairs={{0,8},{8,0},{16,24},{24,16},{1,9},{9,1},{17,25},{25,17},{2,10},{10... | collective-permute-start | bytes 1769480 | tf_op jit(solution)/shard_map/ppermute | solution.py:724
  156.9 23.4 %collective-permute-start.17 = (bf16[2,2,192,384]{3,2,1,0:T(8,128)(2,1)}, bf16[2,2,192,384]{3,2,1,0:T(8,128)(2,1)S(1)}, u32[]{:S(2)}, u32[]{:S(2)}) collective-permute-start(bf16[2,2,192,384]{3,2,1,0:T(8,128)(2,1)} %collective-permute-done.15.refs_1_), channel_id=1, source_target_pairs={{0,8},{8,0},{16,24},{24,16},{1,9},{9,1},{17,25},{25,17},{2,10},{10... | collective-permute-start | bytes 1769480 | tf_op jit(solution)/shard_map/ppermute | solution.py:724
  171.1 17.6 %collective-permute-start.43 = (bf16[256,768]{1,0:T(8,128)(2,1)S(1)}, bf16[256,768]{1,0:T(8,128)(2,1)S(1)}, u32[]{:S(2)}, u32[]{:S(2)}) collective-permute-start(bf16[256,768]{1,0:T(8,128)(2,1)S(1)} %copy-done.26), channel_id=1, source_target_pairs={{0,4},{4,0},{1,5},{5,1},{2,6},{6,2},{3,7},{7,3},{8,12},{12,8},{9,1... | collective-permute-start | bytes 1179656 | tf_op jit(solution)/shard_map/ppermute | solution.py:720
  171.7 23.4 %collective-permute-start.26 = (bf16[256,768]{1,0:T(8,128)(2,1)}, bf16[256,768]{1,0:T(8,128)(2,1)S(1)}, u32[]{:S(2)}, u32[]{:S(2)}) collective-permute-start(bf16[256,768]{1,0:T(8,128)(2,1)} %get-tuple-element.61.h_ref.h0), channel_id=1, source_target_pairs={{0,4},{4,0},{1,5},{5,1},{2,6},{6,2},{3,7},{7,3},{8,12},{12,8},{9,1... | collective-permute-start | bytes 1179656 | tf_op jit(solution)/shard_map/ppermute | solution.py:720
  194.5 23.5 %collective-permute-start.44 = (bf16[256,768]{1,0:T(8,128)(2,1)}, bf16[256,768]{1,0:T(8,128)(2,1)S(1)}, u32[]{:S(2)}, u32[]{:S(2)}) collective-permute-start(bf16[256,768]{1,0:T(8,128)(2,1)} %shard_map.319), channel_id=1, source_target_pairs={{0,4},{4,0},{1,5},{5,1},{2,6},{6,2},{3,7},{7,3},{8,12},{12,8},{9,1... | collective-permute-start | bytes 1179656 | tf_op jit(solution)/shard_map/ppermute | solution.py:720
  201.7 16.4 %collective-permute-start.27 = (bf16[256,768]{1,0:T(8,128)(2,1)}, bf16[256,768]{1,0:T(8,128)(2,1)S(1)}, u32[]{:S(2)}, u32[]{:S(2)}) collective-permute-start(bf16[256,768]{1,0:T(8,128)(2,1)} %get-tuple-element.64), channel_id=1, source_target_pairs={{0,4},{4,0},{1,5},{5,1},{2,6},{6,2},{3,7},{7,3},{8,12},{12,8},{9,1... | collective-permute-start | bytes 1179656 | tf_op jit(solution)/shard_map/ppermute | solution.py:720
  204.3 13.8 %collective-permute-start.45 = (bf16[128,768]{1,0:T(8,128)(2,1)S(1)}, bf16[128,768]{1,0:T(8,128)(2,1)S(1)}, u32[]{:S(2)}, u32[]{:S(2)}) collective-permute-start(bf16[128,768]{1,0:T(8,128)(2,1)S(1)} %bitcast.197), channel_id=1, source_target_pairs={{0,4},{4,0},{1,5},{5,1},{2,6},{6,2},{3,7},{7,3},{8,12},{12,8},{9,1... | collective-permute-start | bytes 589832 | tf_op jit(solution)/shard_map/ppermute | solution.py:720
  223.7 14.3 %collective-permute-start.47 = (bf16[256,768]{1,0:T(8,128)(2,1)}, bf16[256,768]{1,0:T(8,128)(2,1)S(1)}, u32[]{:S(2)}, u32[]{:S(2)}) collective-permute-start(bf16[256,768]{1,0:T(8,128)(2,1)} %get-tuple-element.72.grad_ref.f0), channel_id=1, source_target_pairs={{0,4},{4,0},{1,5},{5,1},{2,6},{6,2},{3,7},{7,3},{8,12},{12,8},{9,1... | collective-permute-start | bytes 1179656 | tf_op jit(solution)/shard_map/ppermute | solution.py:720
  224.2 13.7 %collective-permute-start.46 = (bf16[128,768]{1,0:T(8,128)(2,1)}, bf16[128,768]{1,0:T(8,128)(2,1)S(1)}, u32[]{:S(2)}, u32[]{:S(2)}) collective-permute-start(bf16[128,768]{1,0:T(8,128)(2,1)} %get-tuple-element.70), channel_id=1, source_target_pairs={{0,4},{4,0},{1,5},{5,1},{2,6},{6,2},{3,7},{7,3},{8,12},{12,8},{9,1... | collective-permute-start | bytes 589832 | tf_op jit(solution)/shard_map/ppermute | solution.py:720
  245.0 9.1 %collective-permute-start.48 = (bf16[256,768]{1,0:T(8,128)(2,1)}, bf16[256,768]{1,0:T(8,128)(2,1)S(1)}, u32[]{:S(2)}, u32[]{:S(2)}) collective-permute-start(bf16[256,768]{1,0:T(8,128)(2,1)} %get-tuple-element.76), channel_id=1, source_target_pairs={{0,4},{4,0},{1,5},{5,1},{2,6},{6,2},{3,7},{7,3},{8,12},{12,8},{9,1... | collective-permute-start | bytes 1179656 | tf_op jit(solution)/shard_map/ppermute | solution.py:720
  253.8 100.6 %collective-permute-start.65 = (bf16[2,2,4,192,384]{4,3,2,1,0:T(8,128)(2,1)}, bf16[2,2,4,192,384]{4,3,2,1,0:T(8,128)(2,1)}, u32[]{:S(2)}, u32[]{:S(2)}) collective-permute-start(bf16[2,2,4,192,384]{4,3,2,1,0:T(8,128)(2,1)} %get-tuple-element.101), channel_id=1, source_target_pairs={{0,8},{8,0},{16,24},{24,16},{1,9},{9,1},{17,25},{25,17},{2,10},{10... | collective-permute-start | bytes 7077896 | tf_op jit(solution)/shard_map/ppermute | solution.py:724
  261.8 11.6 %collective-permute-start.49 = (bf16[2,128,192]{2,1,0:T(8,128)(2,1)S(1)}, bf16[2,128,192]{2,1,0:T(8,128)(2,1)S(1)}, u32[]{:S(2)}, u32[]{:S(2)}) collective-permute-start(bf16[2,128,192]{2,1,0:T(8,128)(2,1)S(1)} %get-tuple-element.161), channel_id=1, source_target_pairs={{0,1},{1,0},{2,3},{3,2},{4,5},{5,4},{6,7},{7,6},{8,9},{9,8},{10,11... | collective-permute-start | bytes 294920 | tf_op jit(solution)/shard_map/ppermute | solution.py:732
  265.7 9.9 %collective-permute-start.50 = (bf16[2,128,192]{2,1,0:T(8,128)(2,1)S(1)}, bf16[2,128,192]{2,1,0:T(8,128)(2,1)S(1)}, u32[]{:S(2)}, u32[]{:S(2)}) collective-permute-start(bf16[2,128,192]{2,1,0:T(8,128)(2,1)S(1)} %get-tuple-element.160), channel_id=1, source_target_pairs={{0,2},{1,3},{2,0},{3,1},{4,6},{5,7},{6,4},{7,5},{8,10},{9,11},{10,... | collective-permute-start | bytes 294920 | tf_op jit(solution)/shard_map/ppermute | solution.py:732
  266.1 13.2 %collective-permute-start.51 = (bf16[2,128,192]{2,1,0:T(8,128)(2,1)S(1)}, bf16[2,128,192]{2,1,0:T(8,128)(2,1)S(1)}, u32[]{:S(2)}, u32[]{:S(2)}) collective-permute-start(bf16[2,128,192]{2,1,0:T(8,128)(2,1)S(1)} %get-tuple-element.159), channel_id=1, source_target_pairs={{0,3},{1,2},{2,1},{3,0},{4,7},{5,6},{6,5},{7,4},{8,11},{9,10},{10,... | collective-permute-start | bytes 294920 | tf_op jit(solution)/shard_map/ppermute | solution.py:732
  272.1 31.6 %collective-permute-start.73 = (f32[15,768]{1,0:T(8,128)S(1)}, f32[15,768]{1,0:T(8,128)S(1)}, u32[]{:S(2)}, u32[]{:S(2)}) collective-permute-start(f32[15,768]{1,0:T(8,128)S(1)} %add.147), channel_id=1, source_target_pairs={{0,4},{4,0},{1,5},{5,1},{2,6},{6,2},{3,7},{7,3},{8,12},{12,8},{9,1... | collective-permute-start | bytes 138248 | tf_op jit(solution)/shard_map/ppermute | solution.py:720
  308.4 48.1 %collective-permute-start.56 = (bf16[2,3,192,192]{3,2,1,0:T(8,128)(2,1)}, bf16[2,3,192,192]{3,2,1,0:T(8,128)(2,1)}, u32[]{:S(2)}, u32[]{:S(2)}) collective-permute-start(bf16[2,3,192,192]{3,2,1,0:T(8,128)(2,1)} %get-tuple-element.92), channel_id=1, source_target_pairs={{0,8},{8,0},{16,24},{24,16},{1,9},{9,1},{17,25},{25,17},{2,10},{10... | collective-permute-start | bytes 1327112 | tf_op jit(solution)/shard_map/ppermute | solution.py:724
  313.0 16.6 %collective-permute-start.52 = (bf16[2,128,768]{2,1,0:T(8,128)(2,1)S(1)}, bf16[2,128,768]{2,1,0:T(8,128)(2,1)S(1)}, u32[]{:S(2)}, u32[]{:S(2)}) collective-permute-start(bf16[2,128,768]{2,1,0:T(8,128)(2,1)S(1)} %get-tuple-element.146), channel_id=1, source_target_pairs={{0,1},{1,0},{2,3},{3,2},{4,5},{5,4},{6,7},{7,6},{8,9},{9,8},{10,11... | collective-permute-start | bytes 1179656 | tf_op jit(solution)/shard_map/ppermute | solution.py:732
  313.1 29.1 %collective-permute-start.53 = (bf16[2,128,768]{2,1,0:T(8,128)(2,1)}, bf16[2,128,768]{2,1,0:T(8,128)(2,1)}, u32[]{:S(2)}, u32[]{:S(2)}) collective-permute-start(bf16[2,128,768]{2,1,0:T(8,128)(2,1)} %get-tuple-element.145), channel_id=1, source_target_pairs={{0,2},{1,3},{2,0},{3,1},{4,6},{5,7},{6,4},{7,5},{8,10},{9,11},{10,... | collective-permute-start | bytes 1179656 | tf_op jit(solution)/shard_map/ppermute | solution.py:732
  316.1 34.6 %collective-permute-start.54 = (bf16[2,128,768]{2,1,0:T(8,128)(2,1)}, bf16[2,128,768]{2,1,0:T(8,128)(2,1)}, u32[]{:S(2)}, u32[]{:S(2)}) collective-permute-start(bf16[2,128,768]{2,1,0:T(8,128)(2,1)} %get-tuple-element.144), channel_id=1, source_target_pairs={{0,3},{1,2},{2,1},{3,0},{4,7},{5,6},{6,5},{7,4},{8,11},{9,10},{10,... | collective-permute-start | bytes 1179656 | tf_op jit(solution)/shard_map/ppermute | solution.py:732
  329.6 29.7 %collective-permute-start.59 = (bf16[2,4,192,192]{3,2,1,0:T(8,128)(2,1)}, bf16[2,4,192,192]{3,2,1,0:T(8,128)(2,1)S(1)}, u32[]{:S(2)}, u32[]{:S(2)}) collective-permute-start(bf16[2,4,192,192]{3,2,1,0:T(8,128)(2,1)} %get-tuple-element.95), channel_id=1, source_target_pairs={{0,8},{8,0},{16,24},{24,16},{1,9},{9,1},{17,25},{25,17},{2,10},{10... | collective-permute-start | bytes 1769480 | tf_op jit(solution)/shard_map/ppermute | solution.py:724
  356.1 44.9 %collective-permute-start.66 = (bf16[2,4,192,384]{3,2,1,0:T(8,128)(2,1)S(1)}, bf16[2,4,192,384]{3,2,1,0:T(8,128)(2,1)S(1)}, u32[]{:S(2)}, u32[]{:S(2)}) collective-permute-start(bf16[2,4,192,384]{3,2,1,0:T(8,128)(2,1)S(1)} %fusion), channel_id=1, source_target_pairs={{0,16},{8,24},{16,0},{24,8},{1,17},{9,25},{17,1},{25,9},{2,18},{10... | collective-permute-start | bytes 3538952 | tf_op jit(solution)/shard_map/ppermute | solution.py:728
  357.6 46.4 %collective-permute-start.57 = (bf16[3,192,192]{2,1,0:T(8,128)(2,1)S(1)}, bf16[3,192,192]{2,1,0:T(8,128)(2,1)S(1)}, u32[]{:S(2)}, u32[]{:S(2)}) collective-permute-start(bf16[3,192,192]{2,1,0:T(8,128)(2,1)S(1)} %fusion.12), channel_id=1, source_target_pairs={{0,16},{8,24},{16,0},{24,8},{1,17},{9,25},{17,1},{25,9},{2,18},{10... | collective-permute-start | bytes 663560 | tf_op jit(solution)/shard_map/ppermute | solution.py:728
  359.4 37.8 %collective-permute-start.60 = (bf16[4,192,192]{2,1,0:T(8,128)(2,1)S(1)}, bf16[4,192,192]{2,1,0:T(8,128)(2,1)S(1)}, u32[]{:S(2)}, u32[]{:S(2)}) collective-permute-start(bf16[4,192,192]{2,1,0:T(8,128)(2,1)S(1)} %fusion.10), channel_id=1, source_target_pairs={{0,16},{8,24},{16,0},{24,8},{1,17},{9,25},{17,1},{25,9},{2,18},{10... | collective-permute-start | bytes 884744 | tf_op jit(solution)/shard_map/ppermute | solution.py:728
  397.5 8.0 %collective-permute-start.61 = (bf16[192,192]{1,0:T(8,128)(2,1)S(1)}, bf16[192,192]{1,0:T(8,128)(2,1)S(1)}, u32[]{:S(2)}, u32[]{:S(2)}) collective-permute-start(bf16[192,192]{1,0:T(8,128)(2,1)S(1)} %get-tuple-element.171), channel_id=1, source_target_pairs={{0,1},{1,0},{2,3},{3,2},{4,5},{5,4},{6,7},{7,6},{8,9},{9,8},{10,11... | collective-permute-start | bytes 221192 | tf_op jit(solution)/shard_map/ppermute | solution.py:732
  397.5 10.1 %collective-permute-start.62 = (bf16[192,192]{1,0:T(8,128)(2,1)S(1)}, bf16[192,192]{1,0:T(8,128)(2,1)S(1)}, u32[]{:S(2)}, u32[]{:S(2)}) collective-permute-start(bf16[192,192]{1,0:T(8,128)(2,1)S(1)} %get-tuple-element.173), channel_id=1, source_target_pairs={{0,2},{1,3},{2,0},{3,1},{4,6},{5,7},{6,4},{7,5},{8,10},{9,11},{10,... | collective-permute-start | bytes 221192 | tf_op jit(solution)/shard_map/ppermute | solution.py:732
  400.1 9.1 %collective-permute-start.63 = (bf16[192,192]{1,0:T(8,128)(2,1)S(1)}, bf16[192,192]{1,0:T(8,128)(2,1)S(1)}, u32[]{:S(2)}, u32[]{:S(2)}) collective-permute-start(bf16[192,192]{1,0:T(8,128)(2,1)S(1)} %get-tuple-element.172), channel_id=1, source_target_pairs={{0,3},{1,2},{2,1},{3,0},{4,7},{5,6},{6,5},{7,4},{8,11},{9,10},{10,... | collective-permute-start | bytes 221192 | tf_op jit(solution)/shard_map/ppermute | solution.py:732
  402.9 10.6 %collective-permute-start.67 = (bf16[2,192,384]{2,1,0:T(8,128)(2,1)S(1)}, bf16[2,192,384]{2,1,0:T(8,128)(2,1)S(1)}, u32[]{:S(2)}, u32[]{:S(2)}) collective-permute-start(bf16[2,192,384]{2,1,0:T(8,128)(2,1)S(1)} %get-tuple-element.152), channel_id=1, source_target_pairs={{0,1},{1,0},{2,3},{3,2},{4,5},{5,4},{6,7},{7,6},{8,9},{9,8},{10,11... | collective-permute-start | bytes 884744 | tf_op jit(solution)/shard_map/ppermute | solution.py:732
  403.9 22.5 %collective-permute-start.68 = (bf16[2,192,384]{2,1,0:T(8,128)(2,1)S(1)}, bf16[2,192,384]{2,1,0:T(8,128)(2,1)S(1)}, u32[]{:S(2)}, u32[]{:S(2)}) collective-permute-start(bf16[2,192,384]{2,1,0:T(8,128)(2,1)S(1)} %get-tuple-element.154), channel_id=1, source_target_pairs={{0,2},{1,3},{2,0},{3,1},{4,6},{5,7},{6,4},{7,5},{8,10},{9,11},{10,... | collective-permute-start | bytes 884744 | tf_op jit(solution)/shard_map/ppermute | solution.py:732
  405.5 27.1 %collective-permute-start.69 = (bf16[2,192,384]{2,1,0:T(8,128)(2,1)S(1)}, bf16[2,192,384]{2,1,0:T(8,128)(2,1)S(1)}, u32[]{:S(2)}, u32[]{:S(2)}) collective-permute-start(bf16[2,192,384]{2,1,0:T(8,128)(2,1)S(1)} %get-tuple-element.153), channel_id=1, source_target_pairs={{0,3},{1,2},{2,1},{3,0},{4,7},{5,6},{6,5},{7,4},{8,11},{9,10},{10,... | collective-permute-start | bytes 884744 | tf_op jit(solution)/shard_map/ppermute | solution.py:732
  407.6 26.3 %collective-permute-start.58 = (bf16[3,192,192]{2,1,0:T(8,128)(2,1)S(1)}, bf16[3,192,192]{2,1,0:T(8,128)(2,1)S(1)}, u32[]{:S(2)}, u32[]{:S(2)}) collective-permute-start(bf16[3,192,192]{2,1,0:T(8,128)(2,1)S(1)} %fusion.7), channel_id=1, source_target_pairs={{0,4},{4,0},{1,5},{5,1},{2,6},{6,2},{3,7},{7,3},{8,12},{12,8},{9,1... | collective-permute-start | bytes 663560 | tf_op jit(solution)/shard_map/ppermute | solution.py:720
  409.3 25.7 %collective-permute-start.64 = (bf16[192,192]{1,0:T(8,128)(2,1)S(1)}, bf16[192,192]{1,0:T(8,128)(2,1)S(1)}, u32[]{:S(2)}, u32[]{:S(2)}) collective-permute-start(bf16[192,192]{1,0:T(8,128)(2,1)S(1)} %fusion.14), channel_id=1, source_target_pairs={{0,4},{4,0},{1,5},{5,1},{2,6},{6,2},{3,7},{7,3},{8,12},{12,8},{9,1... | collective-permute-start | bytes 221192 | tf_op jit(solution)/shard_map/ppermute | solution.py:720
  (90 other events, 761.7 us)

commit v2 on v1

--- a/solution.py
+++ b/solution.py
@@ -70,26 +70,58 @@
     return (jnp.transpose(merged, (2, 0, 1, 3)), running + jnp.log(total))
 
 
+WORK_FACTOR = 4
+TOKEN = (8, 128)
+ROOM = 8 * 2**20
+
+
 def vmem_specs(count):
     return [pl.BlockSpec(memory_space=pltpu.VMEM)] * count
 
 
+def vmem_room(inputs, outs, scratch):
+    total = 0
+    for array in (*inputs, *jax.tree.leaves(outs), *scratch):
+        *lead, rows, lanes = (1, 1, *array.shape)
+        size = jnp.dtype(array.dtype).itemsize
+        tile = 8 * (4 // size)
+        total += math.prod(lead) * size * (-(-rows // tile) * tile) * (-(-lanes // 128) * 128)
+    return min(total + ROOM, 60 * 2**20)
+
+
 def call_kernel(kernel, place, inputs, outs, scratch=(), flops=0, moved=0, exps=0):
+    place, after = place if isinstance(place, tuple) else (place, ())
+
+    def body(place_ref, *refs):
+        kernel(place_ref, *refs[len(after) :])
+
     return pl.pallas_call(
-        kernel,
+        body,
         out_shape=outs,
-        in_specs=[pl.BlockSpec(memory_space=pltpu.SMEM)] + vmem_specs(len(inputs)),
+        in_specs=[pl.BlockSpec(memory_space=pltpu.SMEM)]
+        + [pl.BlockSpec(memory_space=pl.ANY)] * len(after)
+        + vmem_specs(len(inputs)),
         out_specs=jax.tree.map(lambda _: pl.BlockSpec(memory_space=pltpu.VMEM), outs),
         scratch_shapes=list(scratch),
-        compiler_params=pltpu.CompilerParams(vmem_limit_bytes=60 * 2**20),
-        cost_estimate=pl.CostEstimate(flops=flops, bytes_accessed=moved, transcendentals=exps),
-    )(place, *inputs)
+        compiler_params=pltpu.CompilerParams(vmem_limit_bytes=vmem_room(inputs, outs, scratch)),
+        cost_estimate=pl.CostEstimate(
+            flops=WORK_FACTOR * flops, bytes_accessed=moved, transcendentals=exps
+        ),
+    )(place, *after, *inputs)
 
 
 def shaped(shape, dtype):
     return jax.ShapeDtypeStruct(shape, dtype)
 
 
+def gate_kernel(place_ref, token_ref):
+    token_ref[...] = jnp.zeros_like(token_ref)
+
+
+def gate(place, *arrays):
+    return call_kernel(gate_kernel, (place, arrays), (), shaped(TOKEN, jnp.float32), flops=1, moved=1)
+
+
 NT = (((1,), (1,)), ((), ()))
 
 
@@ -101,136 +133,236 @@
     return jnp.dot(left, right, preferred_element_type=jnp.float32)
 
 
-def place_rows(place_ref, pieces, target, index=()):
-    size = pieces[0].shape[-2]
-    for distance, piece in zip((0, 2, 1, 3), pieces):
-        start = pl.multiple_of((place_ref[0] ^ distance) * size, 64)
-        target[(*index, pl.ds(start, size), slice(None))] = piece[...] if not index else piece[index]
-
-
-def masked_bias(code_col, code_row, block, count, size):
-    segments = code_row >> 1
-    tags = jnp.where((code_col & 1) > 0, code_col >> 1, -1)
-    key_at = lax.broadcasted_iota(jnp.int32, (count, size), 0)
-    query_at = lax.broadcasted_iota(jnp.int32, (count, size), 1) + block * size
-    allowed = (tags == segments) | (key_at == query_at)
-    return jnp.where(allowed, 0.0, floor_score)
-
-
-def attention_kernel(
-    student,
-    place_ref,
-    own_ref,
-    other_ref,
-    w0_ref,
-    w2_ref,
-    w1_ref,
-    w3_ref,
-    bias_ref,
-    clip_in_ref,
-    clip_ref,
-    col_ref,
-    row_ref,
-    *refs,
-):
-    if student:
-        c_ref, a_ref, q_ref, k_ref, v_ref, ratio_ref, lse_ref, w_ref, vt_ref, mask_ref = refs
-    else:
-        c_ref, w_ref, q_ref, k_ref, v_ref, vt_ref, mask_ref = refs
-    half = own_ref.shape[0]
-    count = 2 * half
-    cols = w_ref.shape[-1]
-    heads = cols // HEAD_DIM
-    size = 256
-    bf16 = jnp.bfloat16
+QUERY_BLOCK = 256
+
+
+def place_projections(place_ref, pieces, target, first):
+    size = pieces[0].shape[1]
     for kind in range(3):
-        for distance, piece in zip((0, 2, 1, 3), (w0_ref, w2_ref, w1_ref, w3_ref)):
-            rows = piece.shape[1]
-            start = pl.multiple_of((place_ref[0] ^ distance) * rows, 64)
-            w_ref[kind, pl.ds(start, rows), :] = piece[kind]
-    for part, source in enumerate((own_ref, other_ref)):
-        inputs = source[...]
-        base = part * half
-        if student:
-            wide = inputs.astype(jnp.float32)
-            inputs = jnp.clip(wide, -clip_in_ref[...], clip_in_ref[...]).astype(bf16)
-            a_ref[base : base + half, :] = inputs
-        queries = (dot_nn(inputs, w_ref[0]) + bias_ref[0:1, :]).astype(bf16)
-        keys = dot_nn(inputs, w_ref[1]).astype(bf16)
-        values = (dot_nn(inputs, w_ref[2]) + bias_ref[1:2, :]).astype(bf16)
-        for head in range(heads):
-            lanes = slice(head * HEAD_DIM, (head + 1) * HEAD_DIM)
-            q_ref[head, base : base + half, :] = queries[:, lanes] * (HEAD_DIM**-0.5)
-            k_ref[head, base : base + half, :] = keys[:, lanes]
-            v_ref[head, base : base + half, :] = values[:, lanes]
-    eye = (
-        lax.broadcasted_iota(jnp.int32, (HEAD_DIM, HEAD_DIM), 0)
-        == lax.broadcasted_iota(jnp.int32, (HEAD_DIM, HEAD_DIM), 1)
-    ).astype(bf16)
-    for head in range(heads):
-        vt_ref[head] = dot_nt(eye, v_ref[head]).astype(bf16)
-
-    def one_block(block, carry):
-        at = pl.multiple_of(block * size, size)
-        mask_ref[...] = masked_bias(col_ref[...], row_ref[:, pl.ds(at, size)], block, count, size)
-        outs = []
-        for head in range(heads):
-            scores = dot_nt(k_ref[head], q_ref[head, pl.ds(at, size), :]) + mask_ref[...]
-            top = jnp.max(scores, axis=0, keepdims=True)
-            weights = jnp.exp(scores - top)
-            total = jnp.sum(weights, axis=0, keepdims=True)
-            merged = dot_nn(vt_ref[head], weights.astype(bf16)) * (1.0 / total)
-            outs.append(merged)
-            if student:
-                lse_ref[pl.ds(head, 1), pl.ds(at, size)] = top + jnp.log(total)
-        merged = jnp.concatenate(outs + [jnp.zeros((256 - cols, size), jnp.float32)], axis=0)
-        merged = jnp.transpose(merged)[:, :cols]
-        if student:
-            ratio = jnp.tanh(merged / clip_ref[...])
-            ratio_ref[pl.ds(at, size), :] = ratio
-            merged = clip_ref[...] * ratio
-        merged = merged.astype(bf16)
-        part, pair = block >> 1, block & 1
-        share = size // 2
-        c_ref[2 * pair, part] = merged[:share]
-        c_ref[2 * pair + 1, part] = merged[share:]
-        return carry
-
-    lax.fori_loop(0, count // size, one_block, 0)
-
-
-def attention_forward(student, place, own, other, pieces, bias, clip_in, clip, code_col, code_row):
+        for distance, piece in zip((0, 2, 1, 3), pieces):
+            start = pl.multiple_of((place_ref[0] ^ distance) * size, 64)
+            target[kind, pl.ds(start, size), :] = piece[kind + first]
+
+
+def project_kernel(place_ref, own_ref, w0, w2, w1, w3, bias_ref, clip_in_ref, full_ref, a_ref, q_ref, token_ref):
+    place_projections(place_ref, (w0, w2, w1, w3), full_ref, 0)
+    clipped = jnp.clip(own_ref[...].astype(jnp.float32), -clip_in_ref[...], clip_in_ref[...])
+    clipped = clipped.astype(jnp.bfloat16)
+    a_ref[...] = clipped
+    write_heads(clipped, full_ref, bias_ref, q_ref, 0)
+    token_ref[...] = jnp.zeros_like(token_ref)
+
+
+def write_heads(inputs, w_ref, bias_ref, target, base):
+    rows = inputs.shape[0]
+    for kind in range(3):
+        values = dot_nn(inputs, w_ref[kind])
+        if kind != 1:
+            values = values + bias_ref[kind >> 1 : (kind >> 1) + 1, :]
+        values = values.astype(jnp.bfloat16)
+        if kind == 0:
+            values = values * (HEAD_DIM**-0.5)
+        for head in range(target.shape[1]):
+            target[kind, head, base : base + rows, :] = values[:, head * HEAD_DIM : (head + 1) * HEAD_DIM]
+
+
+def project_own(place, own, pieces, bias, clip_in):
     half, width = own.shape
     cols = pieces[0].shape[-1]
     heads = cols // HEAD_DIM
+    bf16 = jnp.bfloat16
+    return call_kernel(
+        project_kernel,
+        place,
+        (own, *pieces, bias, clip_in),
+        (
+            shaped((3, width, cols), bf16),
+            shaped((half, width), bf16),
+            shaped((3, heads, half, HEAD_DIM), bf16),
+            shaped(TOKEN, jnp.float32),
+        ),
+        flops=1,
+        moved=1,
+    )
+
+
+def unit_matrix():
+    shape = (HEAD_DIM, HEAD_DIM)
+    ones = lax.broadcasted_iota(jnp.int32, shape, 0) == lax.broadcasted_iota(jnp.int32, shape, 1)
+    return ones.astype(jnp.bfloat16)
+
+
+def block_window(row_ref, place_ref, blocks):
+    mask = order_mask(place_ref)
+    low, high = [], []
+    for block in range(blocks):
+        segment = row_ref[:, block * QUERY_BLOCK : (block + 1) * QUERY_BLOCK] >> 1
+        low.append(jnp.min(segment))
+        high.append(jnp.max(segment))
+    windows = []
+    for query in range(blocks):
+        first, last = jnp.int32(blocks - 1), jnp.int32(0)
+        for key in range(blocks):
+            meets = (low[key] <= high[query]) & (high[key] >= low[query])
+            at = key ^ mask
+            first = jnp.where(meets, jnp.minimum(first, at), first)
+            last = jnp.where(meets, jnp.maximum(last, at), last)
+        windows.append((first, last - first + 1))
+    return windows
+
+
+def order_mask(place_ref):
+    return 2 * place_ref[2] + (place_ref[1] >> 1)
+
+
+def pick(values, index):
+    chosen = values[0]
+    for at in range(1, len(values)):
+        chosen = jnp.where(index == at, values[at], chosen)
+    return chosen
+
+
+def pair_bias(col_ref, row_ref, query, key):
+    size = QUERY_BLOCK
+    code_col = col_ref[pl.ds(pl.multiple_of(key * size, size), size), :]
+    code_row = row_ref[:, pl.ds(pl.multiple_of(query * size, size), size)]
+    tags = jnp.where((code_col & 1) > 0, code_col >> 1, -1)
+    apart = lax.broadcasted_iota(jnp.int32, (size, size), 0) - lax.broadcasted_iota(
+        jnp.int32, (size, size), 1
+    )
+    allowed = (tags == (code_row >> 1)) | (apart == (query - key) * size)
+    return jnp.where(allowed, 0.0, floor_score)
+
+
+def each_count(windows, query, blocks, body):
+    first = pick([w[0] for w in windows], query)
+    count = pick([w[1] for w in windows], query)
+    for fixed in range(1, blocks + 1):
+
+        @pl.when(count == fixed)
+        def _():
+            body(first, fixed)
+
+
+def attention_kernel(
+    student, place_ref, other_ref, bias_ref, clip_in_ref, clip_ref, col_ref, row_ref, *refs
+):
+    if student:
+        w_ref, part_ref, *c_refs = refs[:6]
+        a_ref, rows_ref, qkv_ref, merged_ref, lse_ref, vt_ref, bias_at, score_ref, sum_ref = refs[6:]
+    else:
+        pieces, own_ref, c_refs, token_ref = refs[:4], refs[4], refs[5:9], refs[9]
+        w_ref, qkv_ref, vt_ref, bias_at, score_ref, sum_ref = refs[10:]
+        token_ref[...] = jnp.zeros_like(token_ref)
+    half = qkv_ref.shape[2] // 2
+    heads = qkv_ref.shape[1]
+    cols = heads * HEAD_DIM
+    size = QUERY_BLOCK
+    blocks = 2 * half // size
+    bf16, f32 = jnp.bfloat16, jnp.float32
+    inputs = other_ref[0:half, :]
+    if student:
+        qkv_ref[:, :, 0:half, :] = part_ref[...]
+        inputs = jnp.clip(inputs.astype(f32), -clip_in_ref[...], clip_in_ref[...]).astype(bf16)
+        a_ref[...] = inputs
+        rows_ref[...] = other_ref[0 : half // 4, :]
+    else:
+        place_projections(place_ref, pieces, w_ref, 3)
+        write_heads(own_ref[...], w_ref, bias_ref, qkv_ref, 0)
+    write_heads(inputs, w_ref, bias_ref, qkv_ref, half)
+    eye = unit_matrix()
+    for head in range(heads):
+        vt_ref[head] = dot_nt(eye, qkv_ref[2, head]).astype(bf16)
+    windows = block_window(row_ref, place_ref, blocks)
+    mask = order_mask(place_ref)
+    sum_ref[...] = jnp.zeros_like(sum_ref)
+
+    def one_query(query, carry):
+        at = pl.multiple_of(query * size, size)
+
+        def body(first, count):
+            keys = [(first + step) ^ mask for step in range(count)]
+            starts = [pl.multiple_of(key * size, size) for key in keys]
+            for step in range(count):
+                bias_at[step] = pair_bias(col_ref, row_ref, query, keys[step])
+            for head in range(heads):
+                queries = qkv_ref[0, head, pl.ds(at, size), :]
+                top = None
+                for step in range(count):
+                    scores = bias_at[step] + dot_nt(
+                        qkv_ref[1, head, pl.ds(starts[step], size), :], queries
+                    )
+                    score_ref[step] = scores
+                    part = jnp.max(scores, axis=0, keepdims=True)
+                    top = part if top is None else jnp.maximum(top, part)
+                total, merged = 0.0, 0.0
+                for step in range(count):
+                    weights = jnp.exp(score_ref[step] - top)
+                    total = total + jnp.sum(weights, axis=0, keepdims=True)
+                    merged = merged + dot_nn(
+                        vt_ref[head, :, pl.ds(starts[step], size)], weights.astype(bf16)
+                    )
+                sum_ref[head * HEAD_DIM : (head + 1) * HEAD_DIM, :] = merged * (1.0 / total)
+                if student:
+                    lse_ref[head : head + 1, pl.ds(at, size)] = top + jnp.log(total)
+
+        each_count(windows, query, blocks, body)
+        if student:
+            merged_ref[:, pl.ds(at, size)] = sum_ref[0:cols, :]
+        merged = jnp.transpose(sum_ref[...])[:, :cols]
+        if student:
+            merged = clip_ref[...] * jnp.tanh(merged / clip_ref[...])
+        merged = merged.astype(bf16)
+        part = query >> 1
+        share = size // 2
+        for pair in range(2):
+
+            @pl.when((query & 1) == pair)
+            def _():
+                c_refs[2 * pair][part] = merged[:share]
+                c_refs[2 * pair + 1][part] = merged[share:]
+
+        return carry
+
+    lax.fori_loop(0, blocks, one_query, 0)
+
+
+def attention_forward(student, place, other, weights, parts, bias, clip_in, clip, code_col, code_row):
+    width = other.shape[1]
+    half = parts.shape[2] if student else parts.shape[0]
+    cols = weights[0].shape[-1]
+    heads = cols // HEAD_DIM
     count = 2 * half
     bf16, f32 = jnp.bfloat16, jnp.float32
-    head_shape = (heads, count, HEAD_DIM)
-    c_shape = shaped((4, 2, half // 4, cols), bf16)
-    w = pltpu.VMEM((3, width, cols), bf16)
-    vt = pltpu.VMEM((heads, HEAD_DIM, count), bf16)
-    mask = pltpu.VMEM((count, 256), f32)
+    qkv = (3, heads, count, HEAD_DIM)
+    c_shape = (shaped((2, half // 4, cols), bf16),) * 4
+    scratch = (
+        pltpu.VMEM((heads, HEAD_DIM, count), bf16),
+        pltpu.VMEM((count // QUERY_BLOCK, QUERY_BLOCK, QUERY_BLOCK), f32),
+        pltpu.VMEM((count // QUERY_BLOCK, QUERY_BLOCK, QUERY_BLOCK), f32),
+        pltpu.VMEM((256, QUERY_BLOCK), f32),
+    )
     if student:
         outs = (
-            c_shape,
-            shaped((count, width), bf16),
-            shaped(head_shape, bf16),
-            shaped(head_shape, bf16),
-            shaped(head_shape, bf16),
-            shaped((count, cols), f32),
+            *c_shape,
+            shaped((half, width), bf16),
+            shaped((half // 4, width), bf16),
+            shaped(qkv, bf16),
+            shaped((cols, count), f32),
             shaped((8, count), f32),
         )
-        scratch = (w, vt, mask)
+        inputs = (weights, parts)
     else:
-        outs = (c_shape,)
-        scratch = (w,) + (pltpu.VMEM(head_shape, bf16),) * 3 + (vt, mask)
+        outs = (*c_shape, shaped(TOKEN, f32))
+        scratch = (pltpu.VMEM((3, width, cols), bf16), pltpu.VMEM(qkv, bf16), *scratch)
+        inputs = (*weights, parts)
     return call_kernel(
         functools.partial(attention_kernel, student),
         place,
-        (own, other, *pieces, bias, clip_in, clip, code_col, code_row),
+        (other, bias, clip_in, clip, code_col, code_row, *inputs),
         outs,
         scratch,
-        flops=2 * count * width * cols * 3 + 4 * count * count * cols,
+        flops=2 * half * width * cols * 3 + 4 * count * count * cols,
         moved=6 * count * width,
         exps=heads * count * count,
     )
@@ -238,11 +370,9 @@
 
 def attention_pull_kernel(
     place_ref,
-    a_ref,
-    q_ref,
-    k_ref,
-    v_ref,
-    ratio_ref,
+    qkv_ref,
+    clip_ref,
+    merged_ref,
     lse_ref,
     col_ref,
     row_ref,
@@ -250,67 +380,83 @@
     d1_ref,
     d2_ref,
     d3_ref,
-    w0_ref,
-    w2_ref,
-    w1_ref,
-    w3_ref,
-    back_ref,
+    w_ref,
+    keep_ref,
+    send_ref,
     dproj_ref,
     sums_ref,
-    w_ref,
     grad_ref,
     kt_ref,
-    mask_ref,
     dk_ref,
     dv_ref,
+    sum_ref,
+    delta_ref,
+    bias_at,
 ):
-    heads, count, _ = q_ref.shape
+    _, heads, count, _ = qkv_ref.shape
     cols = heads * HEAD_DIM
-    size = 256
+    size = QUERY_BLOCK
     share = size // 2
+    blocks = count // size
     bf16, f32 = jnp.bfloat16, jnp.float32
-    for kind in range(3):
-        for distance, piece in zip((0, 2, 1, 3), (w0_ref, w2_ref, w1_ref, w3_ref)):
-            rows = piece.shape[1]
-            start = pl.multiple_of((place_ref[0] ^ distance) * rows, 64)
-            w_ref[kind, pl.ds(start, rows), :] = piece[kind]
-    eye = (
-        lax.broadcasted_iota(jnp.int32, (HEAD_DIM, HEAD_DIM), 0)
-        == lax.broadcasted_iota(jnp.int32, (HEAD_DIM, HEAD_DIM), 1)
-    ).astype(bf16)
+    eye = unit_matrix()
     for head in range(heads):
-        kt_ref[head] = dot_nt(eye, k_ref[head]).astype(bf16)
+        kt_ref[head] = dot_nt(eye, qkv_ref[1, head]).astype(bf16)
     for distance, source in enumerate((d0_ref, d1_ref, d2_ref, d3_ref)):
         for part in range(2):
             at = part * (count // 2) + distance * share
-            ratio = ratio_ref[at : at + share, :]
-            grad = source[part].astype(f32) * (1.0 - ratio * ratio)
+            merged = merged_ref[:, at : at + share]
+            wide = jnp.concatenate([merged, jnp.zeros((256 - cols, share), f32)], axis=0)
+            ratio = jnp.tanh(jnp.transpose(wide)[:, :cols] / clip_ref[...])
+            grad = (source[part].astype(f32) * (1.0 - ratio * ratio)).astype(bf16)
             for head in range(heads):
-                lanes = slice(head * HEAD_DIM, (head + 1) * HEAD_DIM)
-                grad_ref[head, at : at + share, :] = grad[:, lanes].astype(bf16)
+                grad_ref[head, at : at + share, :] = grad[:, head * HEAD_DIM : (head + 1) * HEAD_DIM]
+            wide = jnp.concatenate(
+                [grad.astype(f32), jnp.zeros((share, 256 - cols), f32)], axis=1
+            )
+            turned = jnp.transpose(wide)[:cols] * merged
+            for head in range(heads):
+                delta_ref[head : head + 1, at : at + share] = jnp.sum(
+                    turned[head * HEAD_DIM : (head + 1) * HEAD_DIM], axis=0, keepdims=True
+                )
     dk_ref[...] = jnp.zeros_like(dk_ref)
     dv_ref[...] = jnp.zeros_like(dv_ref)
-
-    def one_block(block, carry):
-        at = pl.multiple_of(block * size, size)
-        mask_ref[...] = masked_bias(col_ref[...], row_ref[:, pl.ds(at, size)], block, count, size)
-        outs = []
-        for head in range(heads):
-            query = q_ref[head, pl.ds(at, size), :]
-            grad = grad_ref[head, pl.ds(at, size), :]
-            lse = lse_ref[pl.ds(head, 1), pl.ds(at, size)]
-            probs = jnp.exp(dot_nt(k_ref[head], query) + mask_ref[...] - lse)
-            d_probs = dot_nt(v_ref[head], grad)
-            delta = jnp.sum(probs * d_probs, axis=0, keepdims=True)
-            d_scores = (probs * (d_probs - delta)).astype(bf16)
-            dv_ref[head] += dot_nn(probs.astype(bf16), grad)
-            dk_ref[head] += dot_nn(d_scores, query)
-            outs.append(dot_nn(kt_ref[head], d_scores) * (HEAD_DIM**-0.5))
-        merged = jnp.concatenate(outs + [jnp.zeros((256 - cols, size), f32)], axis=0)
-        dproj_ref[0, pl.ds(at, size), :] = jnp.transpose(merged)[:, :cols].astype(bf16)
+    windows = block_window(row_ref, place_ref, blocks)
+    mask = order_mask(place_ref)
+    sum_ref[...] = jnp.zeros_like(sum_ref)
+
+    def one_query(query, carry):
+        at = pl.multiple_of(query * size, size)
+
+        def body(first, count):
+            keys = [(first + step) ^ mask for step in range(count)]
+            starts = [pl.multiple_of(key * size, size) for key in keys]
+            for step in range(count):
+                bias_at[step] = pair_bias(col_ref, row_ref, query, keys[step])
+            for head in range(heads):
+                queries = qkv_ref[0, head, pl.ds(at, size), :]
+                grad = grad_ref[head, pl.ds(at, size), :]
+                lse = lse_ref[head : head + 1, pl.ds(at, size)]
+                delta = delta_ref[head : head + 1, pl.ds(at, size)]
+                merged = 0.0
+                for step in range(count):
+                    rows = pl.ds(starts[step], size)
+                    probs = jnp.exp(
+                        dot_nt(qkv_ref[1, head, rows, :], queries) + (bias_at[step] - lse)
+                    )
+                    d_probs = dot_nt(qkv_ref[2, head, rows, :], grad)
+                    d_scores = (probs * (d_probs - delta)).astype(bf16)
+                    dv_ref[head, rows, :] += dot_nn(probs.astype(bf16), grad)
+                    dk_ref[head, rows, :] += dot_nn(d_scores, queries)
+                    merged = merged + dot_nn(kt_ref[head, :, rows], d_scores)
+                sum_ref[head * HEAD_DIM : (head + 1) * HEAD_DIM, :] = merged
+
+        each_count(windows, query, blocks, body)
+        merged = jnp.transpose(sum_ref[...])[:, :cols] * (HEAD_DIM**-0.5)
+        dproj_ref[0, pl.ds(at, size), :] = merged.astype(bf16)
         return carry
 
-    lax.fori_loop(0, count // size, one_block, 0)
+    lax.fori_loop(0, blocks, one_query, 0)
     for head in range(heads):
         lanes = slice(head * HEAD_DIM, (head + 1) * HEAD_DIM)
         dproj_ref[1, :, lanes] = dk_ref[head].astype(bf16)
@@ -325,30 +471,32 @@
             + dot_nt(dproj_ref[2, at, :], w_ref[2])
         ).astype(bf16)
         for distance in range(4):
-            back_ref[distance, part] = back[distance * share : (distance + 1) * share]
-
-
-def attention_backward(place, a_in, q, k, v, ratio, lse, code_col, code_row, grads, pieces):
-    heads, count, _ = q.shape
+            target = send_ref if distance & 1 else keep_ref
+            target[distance >> 1, part] = back[distance * share : (distance + 1) * share]
+
+
+def attention_backward(place, qkv, clip, merged, lse, code_col, code_row, grads, weights):
+    _, heads, count, _ = qkv.shape
     cols = heads * HEAD_DIM
-    width = a_in.shape[1]
+    width = weights.shape[1]
     bf16, f32 = jnp.bfloat16, jnp.float32
     return call_kernel(
         attention_pull_kernel,
         place,
-        (a_in, q, k, v, ratio, lse, code_col, code_row, *grads, *pieces),
+        (qkv, clip, merged, lse, code_col, code_row, *grads, weights),
         (
-            shaped((4, 2, count // 8, width), bf16),
+            *(shaped((2, 2, count // 8, width), bf16),) * 2,
             shaped((3, count, cols), bf16),
             shaped((2, cols), f32),
         ),
         (
-            pltpu.VMEM((3, width, cols), bf16),
             pltpu.VMEM((heads, count, HEAD_DIM), bf16),
             pltpu.VMEM((heads, HEAD_DIM, count), bf16),
-            pltpu.VMEM((count, 256), f32),
             pltpu.VMEM((heads, count, HEAD_DIM), f32),
             pltpu.VMEM((heads, count, HEAD_DIM), f32),
+            pltpu.VMEM((256, QUERY_BLOCK), f32),
+            pltpu.VMEM((8, count), f32),
+            pltpu.VMEM((count // QUERY_BLOCK, QUERY_BLOCK, QUERY_BLOCK), f32),
         ),
         flops=2 * count * width * cols * 3 + 10 * count * count * cols,
         moved=8 * count * width,
@@ -371,26 +519,37 @@
     return lax.dot_general(left, right, (((0,), (0,)), ((), ())), preferred_element_type=jnp.float32)
 
 
-def out_norm_kernel(student, model, place_ref, c0, c1, c2, c3, w0, w2, w1, w3, own_ref, other_ref, valid_ref, params_ref, *refs):
+def out_norm_kernel(student, place_ref, *refs):
     if student:
-        w_ref, unit_ref, scale_ref, low_ref, sums_ref = refs
+        c_refs, pieces = refs[:4], refs[4:12]
+        own_ref, other_ref, valid_ref, params_ref = refs[12:16]
+        w_ref, unit_ref, scale_ref, low_ref, sums_ref, token_ref = refs[16:]
+        token_ref[...] = jnp.zeros_like(token_ref)
     else:
-        wide_ref, low_ref, w_ref = refs
+        c_refs, w_ref = refs[:4], refs[4]
+        own_ref, other_ref, valid_ref, params_ref, cot_ref = refs[5:10]
+        wide_ref, low_ref = refs[10:]
     share = own_ref.shape[0]
+    cols = c_refs[0].shape[2]
+    size = w_ref.shape[1] // 4
     total = None
-    for r, source in enumerate((c0, c1, c2, c3)):
-        for distance, piece in zip((0, 2, 1, 3), (w0, w2, w1, w3)):
-            size = piece.shape[2]
-            start = pl.multiple_of((place_ref[0] ^ distance) * size, 64)
-            w_ref[r, pl.ds(start, size), :] = piece[r, model]
+    for r, source in enumerate(c_refs):
+        if student:
+            group = pieces[:4] if r % 2 == 0 else pieces[4:]
+            for distance, piece in zip((0, 2, 1, 3), group):
+                start = pl.multiple_of((place_ref[0] ^ distance) * size, 64)
+                w_ref[r, pl.ds(start, size), :] = piece[r >> 1, 2 * size : 3 * size, :]
+            weights = w_ref[r, :, 0:cols]
+        else:
+            weights = w_ref[r, :, cols : 2 * cols]
         context = jnp.concatenate([source[0], source[1]], axis=0)
-        term = dot_nt(context, w_ref[r])
+        term = dot_nt(context, weights)
         total = term if total is None else total + term
     attn = total + params_ref[0:1, :]
     stream = jnp.concatenate([own_ref[...], other_ref[...]], axis=0).astype(jnp.float32)
     unit, scale = unit_of(stream + attn)
     wide = unit * params_ref[2:3, :] + params_ref[3:4, :]
-    low_ref[...] = wide.astype(jnp.bfloat16)
+    low_ref[0 : 2 * share, :] = wide.astype(jnp.bfloat16)
     if student:
         unit_ref[...] = unit
         scale_ref[...] = scale
@@ -400,32 +559,30 @@
         sums_ref[2:3, :] = column_sum(valid * attn * attn)
     else:
         wide_ref[...] = wide
-
-
-def out_norm(student, place, contexts, pieces, own, other, valid, params):
+        low_ref[2 * share :, :] = cot_ref[...]
+
+
+def out_norm(student, place, contexts, weights, own, other, valid, params, cot=()):
     share, width = own.shape
     rows = 2 * share
     cols = contexts[0].shape[-1]
     f32, bf16 = jnp.float32, jnp.bfloat16
-    w = (4, width, cols)
     if student:
         outs = (
-            shaped(w, bf16),
+            shaped((4, width, 2 * cols), bf16),
             shaped((rows, width), f32),
             shaped((rows, 1), f32),
             shaped((rows, width), bf16),
             shaped((3, width), f32),
+            shaped(TOKEN, f32),
         )
-        scratch = ()
     else:
-        outs = (shaped((rows, width), f32), shaped((rows, width), bf16))
-        scratch = (pltpu.VMEM(w, bf16),)
+        outs = (shaped((rows, width), f32), shaped((rows + share, width), bf16))
     return call_kernel(
-        functools.partial(out_norm_kernel, student, 0 if student else 1),
+        functools.partial(out_norm_kernel, student),
         place,
-        (*contexts, *pieces, own, other, valid, params),
+        (*contexts, *(weights if student else (weights,)), own, other, valid, params, *cot),
         outs,
-        scratch,
         flops=2 * rows * width * cols * 4,
         moved=12 * rows * width,
     )
@@ -439,27 +596,35 @@
 def hidden_kernel(student, assemble, far, place_ref, h_ref, *refs):
     refs = list(refs)
     pieces = [refs.pop(0) for _ in range(8 if assemble else 1)]
-    bias_ref = refs.pop(0)
-    clip_ref = refs.pop(0) if student else None
+    with_terms = student and assemble
+    terms_ref = None if with_terms else refs.pop(0)
     w_ref = refs.pop(0) if assemble else pieces[0]
+    if with_terms:
+        terms_ref = refs.pop(0)
     if student:
         hid_ref, slope_ref = refs.pop(0), refs.pop(0)
-    part_ref = refs.pop(0)
+    part_ref, token_ref = refs
+    token_ref[...] = jnp.zeros_like(token_ref)
     bf16 = jnp.bfloat16
     total = None
-    inputs = h_ref[...]
+    inputs = h_ref[0 : part_ref.shape[0], :]
     for r in range(4):
         if assemble:
-            group = pieces[:4] if r < 2 else pieces[4:]
+            group = pieces[:4] if r % 2 == 0 else pieces[4:]
+            size = w_ref.shape[2] // 4
             for mat in range(2):
                 for distance, piece in zip((0, 2, 1, 3), group):
-                    size = piece.shape[2]
                     start = pl.multiple_of((place_ref[0] ^ distance) * size, 64)
-                    w_ref[r, mat, pl.ds(start, size), :] = piece[r & 1, mat]
-        upper = dot_nn(inputs, w_ref[r, 0]) + bias_ref[r : r + 1, :]
+                    w_ref[r, mat, pl.ds(start, size), :] = piece[r >> 1, mat * size : (mat + 1) * size, :]
+        if with_terms:
+            terms_ref[r] = group[0][r >> 1, 3 * size : 3 * size + 16, :]
+        terms = terms_ref[r].astype(jnp.float32)
+        base = 0 if student else 6
+        bias = terms[base : base + 1] + terms[base + 1 : base + 2] + terms[base + 2 : base + 3]
+        upper = dot_nn(inputs, w_ref[r, 0]) + bias
         active, cdf = gelu_parts(upper)
         if student:
-            clip = clip_ref[r : r + 1, :]
+            clip = terms[3:4] + terms[4:5] + terms[5:6]
             ratio = jnp.tanh(active / clip)
             pdf = jnp.exp(-0.5 * upper * upper) * ((2.0 * math.pi) ** -0.5)
             slope_ref[r] = ((1.0 - ratio * ratio) * (cdf + upper * pdf)).astype(bf16)
@@ -472,18 +637,20 @@
     part_ref[...] = total.astype(part_ref.dtype)
 
 
-def hidden_layer(student, far, place, h, weights, bias, clip):
-    rows, width = h.shape
-    half = bias.shape[-1]
+def hidden_layer(student, far, place, h, rows, weights, terms=None):
+    width = h.shape[-1]
+    half = weights[0].shape[-1] if isinstance(weights, tuple) else weights.shape[-1]
     f32, bf16 = jnp.float32, jnp.bfloat16
     assemble = isinstance(weights, tuple)
     outs = []
     if assemble:
         outs.append(shaped((4, 2, width, half), bf16))
+        if student:
+            outs.append(shaped((4, 16, half), bf16))
     if student:
         outs += [shaped((4, rows, half), bf16)] * 2
-    outs.append(shaped((rows, width), bf16 if far else f32))
-    inputs = (h, *(weights if assemble else (weights,)), bias) + ((clip,) if student else ())
+    outs += [shaped((rows, width), bf16 if far else f32), shaped(TOKEN, f32)]
+    inputs = (h, *(weights if assemble else (weights,))) + (() if terms is None else (terms,))
     return call_kernel(
         functools.partial(hidden_kernel, student, assemble, far),
         place,
@@ -497,9 +664,10 @@
 
 def loss_kernel(
     place_ref, unit_ref, ffn_ref, got_ref, ht_ref, ffnt_ref, gott_ref, cot_ref, cot_other_ref, valid_ref, params_ref, t_ref,
-    layer_ref, layer_other_ref, dz_ref, low_ref, sums_ref,
+    layer_ref, dz_ref, low_ref, sums_ref,
 ):
     share = cot_ref.shape[0]
+    rows = 2 * share
     f32, bf16 = jnp.float32, jnp.bfloat16
     h_one = unit_ref[...] * params_ref[2:3, :] + params_ref[3:4, :]
     ffn = ffn_ref[...] + got_ref[...].astype(f32) + params_ref[1:2, :]
@@ -507,12 +675,12 @@
     out = unit * params_ref[4:5, :] + params_ref[5:6, :]
     low = out.astype(bf16)
     layer_ref[...] = low[:share]
-    layer_other_ref[...] = low[share:]
+    low_ref[rows:, :] = low[share:]
     t_unit, _ = unit_of(ht_ref[...] + ffnt_ref[...] + gott_ref[...].astype(f32) + t_ref[1:2, :])
     difference = out - (t_unit * t_ref[4:5, :] + t_ref[5:6, :])
     valid = valid_ref[...]
     gap = valid * difference
-    arriving = jnp.concatenate([cot_ref[...], cot_other_ref[...]], axis=0).astype(f32)
+    arriving = jnp.concatenate([cot_ref[...], cot_other_ref[rows:, :]], axis=0).astype(f32)
     grad = arriving + gap
     inner = grad * params_ref[4:5, :]
     dz = scale * (
@@ -522,7 +690,7 @@
     )
     dz_ref[...] = dz
     dz_low = dz.astype(bf16)
-    low_ref[...] = dz_low
+    low_ref[0:rows, :] = dz_low
     sums_ref[0:1, :] = column_sum(dz_low.astype(f32))
     sums_ref[1:2, :] = column_sum(grad * unit)
     sums_ref[2:3, :] = column_sum(grad)
@@ -540,9 +708,8 @@
         (unit, ffn, got, ht, ffnt, gott, cot, cot_other, valid, params, t_rows),
         (
             shaped((share, width), bf16),
-            shaped((share, width), bf16),
             shaped((rows, width), f32),
-            shaped((rows, width), bf16),
+            shaped((rows + share, width), bf16),
             shaped((5, width), f32),
         ),
         flops=60 * rows * width,
@@ -551,7 +718,7 @@
 
 
 def hidden_pull_kernel(place_ref, grad_ref, w_ref, slope_ref, du_ref, part_ref, sums_ref):
-    grad = grad_ref[...]
+    grad = grad_ref[0 : part_ref.shape[0], :]
     total = None
     for r in range(4):
         upper = (dot_nn(grad, w_ref[r, 1]) * slope_ref[r].astype(jnp.float32)).astype(jnp.bfloat16)
@@ -563,7 +730,8 @@
 
 
 def hidden_pull(far, place, grad, weights, slope):
-    rows, width = grad.shape
+    width = grad.shape[-1]
+    rows = slope.shape[1]
     half = slope.shape[-1]
     f32, bf16 = jnp.float32, jnp.bfloat16
     return call_kernel(
@@ -576,40 +744,35 @@
     )
 
 
-def keep_and_send(place_ref, full_ref, keep_ref, send_ref, index):
+def hidden_grads_kernel(mat, place_ref, l0, l1, r0, r1, keep_ref, send_ref, full_ref):
+    rows = r0.shape[1]
+    left = jnp.transpose(jnp.concatenate([l0[0:rows, :], l1[0:rows, :]], axis=0))
     size = full_ref.shape[0] // 4
-    for slot in range(2):
-        for target, distance in ((keep_ref, 2 * slot), (send_ref, 2 * slot + 1)):
-            start = pl.multiple_of((place_ref[0] ^ distance) * size, 64)
-            target[(slot, *index)] = full_ref[pl.ds(start, size), :].astype(jnp.bfloat16)
-
-
-def hidden_grads_kernel(place_ref, f0, f1, hid0, hid1, h0, h1, du0, du1, keep_ref, send_ref, full_ref):
-    for mat, (left0, left1, right0, right1) in enumerate(((h0, h1, du0, du1), (f0, f1, hid0, hid1))):
-        left = jnp.concatenate([left0[...], left1[...]], axis=0)
-        for r in range(4):
-            right = jnp.concatenate([right0[r], right1[r]], axis=0)
-            full_ref[...] = dot_tn(left, right)
-            keep_and_send(place_ref, full_ref, keep_ref, send_ref, (mat, r))
-
-
-def hidden_grads(place, grads, hidden, inputs, d_upper):
-    rows, width = grads[0].shape
-    half = hidden[0].shape[-1]
-    bf16 = jnp.bfloat16
-    out = shaped((2, 2, 4, width // 4, half), bf16)
+    for r in range(4):
+        right = jnp.concatenate([r0[r], r1[r]], axis=0)
+        full_ref[...] = dot_nn(left, right)
+        for slot in range(2):
+            for target, distance in ((keep_ref, 2 * slot), (send_ref, 2 * slot + 1)):
+                start = pl.multiple_of((place_ref[0] ^ distance) * size, 64)
+                target[slot, r] = full_ref[pl.ds(start, size), :].astype(jnp.bfloat16)
+
+
+def hidden_grads(place, left, right):
+    width = left[0].shape[-1]
+    rows, half = right[0].shape[1:]
+    out = shaped((2, 4, width // 4, half), jnp.bfloat16)
     return call_kernel(
-        hidden_grads_kernel,
+        functools.partial(hidden_grads_kernel, 0),
         place,
-        (*grads, *hidden, *inputs, *d_upper),
+        (*left, *right),
         (out, out),
         (pltpu.VMEM((width, half), jnp.float32),),
-        flops=4 * rows * width * half * 8,
-        moved=16 * width * half * 2,
-    )
-
-
-def first_pull_kernel(place_ref, dz_ref, part_ref, got_ref, unit_ref, scale_ref, params_ref, w_ref, first_ref, low_ref, sums_ref, ctx_ref):
+        flops=16 * rows * width * half * 4,
+        moved=8 * width * half * 2,
+    )
+
+
+def first_pull_kernel(place_ref, dz_ref, part_ref, got_ref, unit_ref, scale_ref, params_ref, w_ref, first_ref, low_ref, sums_ref, *ctx_refs):
     f32, bf16 = jnp.float32, jnp.bfloat16
     grad = dz_ref[...] + part_ref[...] + got_ref[...].astype(f32)
     unit = unit_ref[...]
@@ -625,16 +788,16 @@
     sums_ref[0:1, :] = column_sum(low.astype(f32))
     sums_ref[1:2, :] = column_sum(grad * unit)
     sums_ref[2:3, :] = column_sum(grad)
-    share = ctx_ref.shape[2]
+    share, cols = ctx_refs[0].shape[1:]
     for r in range(4):
-        back = dot_nn(low, w_ref[r]).astype(bf16)
-        ctx_ref[r, 0] = back[:share]
-        ctx_ref[r, 1] = back[share:]
+        back = dot_nn(low, w_ref[r, :, 0:cols]).astype(bf16)
+        ctx_refs[r][0] = back[:share]
+        ctx_refs[r][1] = back[share:]
 
 
 def first_pull(place, dz, part, got, unit, scale, params, weights):
     rows, width = dz.shape
-    cols = weights.shape[-1]
+    cols = weights.shape[-1] // 2
     f32, bf16 = jnp.float32, jnp.bfloat16
     return call_kernel(
         first_pull_kernel,
@@ -644,61 +807,59 @@
             shaped((rows, width), f32),
             shaped((rows, width), bf16),
             shaped((3, width), f32),
-            shaped((4, 2, rows // 2, cols), bf16),
+            *(shaped((2, rows // 2, cols), bf16),) * 4,
         ),
         flops=2 * rows * width * cols * 4,
         moved=20 * rows * width,
     )
 
 
-def out_grads_kernel(place_ref, low_ref, c0, c1, c2, c3, keep_ref, send_ref, full_ref):
-    for r, source in enumerate((c0, c1, c2, c3)):
-        context = jnp.concatenate([source[0], source[1]], axis=0)
-        full_ref[...] = dot_tn(low_ref[...], context)
-        keep_and_send(place_ref, full_ref, keep_ref, send_ref, (r,))
-
-
-def out_grads(place, low, contexts):
+def last_grads_kernel(place_ref, low_ref, c0, c1, c2, c3, a_ref, a_other_ref, d_ref, qv_ref, keep_ref, send_ref, full_ref):
+    size = full_ref.shape[0] // 4
+    half = a_ref.shape[0]
+    low = jnp.transpose(low_ref[...])
+    own, other = jnp.transpose(a_ref[...]), jnp.transpose(a_other_ref[...])
+    for entry in range(7):
+        if entry < 4:
+            source = (c0, c1, c2, c3)[entry]
+            full_ref[...] = dot_nn(low, jnp.concatenate([source[0], source[1]], axis=0))
+        else:
+            full_ref[...] = dot_nn(own, d_ref[entry - 4, 0:half, :]) + dot_nn(
+                other, d_ref[entry - 4, half:, :]
+            )
+        for slot in range(2):
+            for target, distance in ((keep_ref, 2 * slot), (send_ref, 2 * slot + 1)):
+                start = pl.multiple_of((place_ref[0] ^ distance) * size, 64)
+                target[slot, entry * size : (entry + 1) * size, :] = full_ref[
+                    pl.ds(start, size), :
+                ].astype(jnp.bfloat16)
+    sums = jnp.concatenate([qv_ref[...], jnp.zeros((14, qv_ref.shape[1]), jnp.float32)], axis=0)
+    for slot in range(2):
+        for target in (keep_ref, send_ref):
+            target[slot, 7 * size :, :] = sums.astype(jnp.bfloat16)
+
+
+def last_grads(place, low, contexts, a_in, d_proj, d_bias_qv):
     rows, width = low.shape
-    cols = contexts[0].shape[-1]
-    out = shaped((2, 4, width // 4, cols), jnp.bfloat16)
+    count = d_proj.shape[1]
+    cols = d_proj.shape[-1]
+    out = shaped((2, 7 * (width // 4) + 16, cols), jnp.bfloat16)
     return call_kernel(
-        out_grads_kernel,
+        last_grads_kernel,
         place,
-        (low, *contexts),
+        (low, *contexts, *a_in, d_proj, d_bias_qv),
         (out, out),
         (pltpu.VMEM((width, cols), jnp.float32),),
-        flops=2 * rows * width * cols * 4,
-        moved=20 * width * cols,
-    )
-
-
-def in_grads_kernel(place_ref, a_ref, d_ref, keep_ref, send_ref, full_ref):
-    for kind in range(3):
-        full_ref[...] = dot_tn(a_ref[...], d_ref[kind])
-        keep_and_send(place_ref, full_ref, keep_ref, send_ref, (kind,))
-
-
-def in_grads(place, a_in, d_proj):
-    count, width = a_in.shape
-    cols = d_proj.shape[-1]
-    out = shaped((2, 3, width // 4, cols), jnp.bfloat16)
-    return call_kernel(
-        in_grads_kernel,
-        place,
-        (a_in, d_proj),
-        (out, out),
-        (pltpu.VMEM((width, cols), jnp.float32),),
-        flops=2 * count * width * cols * 3,
+        flops=2 * (4 * rows + 3 * count) * width * cols,
         moved=4 * count * width,
     )
 
 
-def input_kernel(place_ref, first_ref, b0, b1, b2, b3, own_ref, other_ref, clip_ref, mine_ref, other_out_ref):
+def input_kernel(place_ref, first_ref, b0, b1, b2, own_ref, other_ref, clip_ref, mine_ref, other_out_ref):
     f32 = jnp.float32
     share = own_ref.shape[0]
     for part, (source, target) in enumerate(((own_ref, mine_ref), (other_ref, other_out_ref))):
-        through = b0[part].astype(f32) + b1[part].astype(f32) + b2[part].astype(f32) + b3[part].astype(f32)
+        through = b0[0, part].astype(f32) + b1[0, part].astype(f32) + b2[part].astype(f32)
         inside = jnp.abs(source[...].astype(f32)) < clip_ref[...]
         first = first_ref[part * share : (part + 1) * share, :]
         target[...] = (first + jnp.where(inside, through, 0.0)).astype(target.dtype)
@@ -716,6 +877,32 @@
     )
 
 
+def vector_kernel(place_ref, third_ref, second_ref, first_ref, own_ref, far_ref, out_ref):
+    half = own_ref.shape[1]
+    out_ref[...] = jnp.zeros_like(out_ref)
+    out_ref[0:3, :] = third_ref[...]
+    out_ref[3:8, :] = second_ref[...]
+    out_ref[8:11, :] = first_ref[...]
+    for r in range(4):
+        part = own_ref[r : r + 1, :] + far_ref[r : r + 1, :]
+        nothing = jnp.zeros_like(part)
+        left = jnp.where(place_ref[2] == 0, part, nothing)
+        right = jnp.where(place_ref[2] == 0, nothing, part)
+        out_ref[pl.ds(11 + (place_ref[1] ^ r), 1), :] = jnp.concatenate([left, right], axis=1)
+
+
+def vector_rows(place, third, second, first, own, far):
+    width = third.shape[1]
+    return call_kernel(
+        vector_kernel,
+        place,
+        (third, second, first, own, far),
+        shaped((16, width), jnp.float32),
+        flops=1,
+        moved=1,
+    )
+
+
 def swap_ctx(value):
     return lax.ppermute(value, "ctx", [(0, 1), (1, 0)])
 
@@ -737,12 +924,23 @@
     return (piece, far, swap_core(piece), swap_core(far))
 
 
-def tp_pieces(piece):
-    return [piece] + [swap_tp(piece, r) for r in (1, 2, 3)]
-
-
-def exchange_tp(stacked):
-    return [stacked[0]] + [swap_tp(stacked[r], r) for r in (1, 2, 3)]
+def exchange_tp(entries):
+    return [entries[0]] + [swap_tp(entries[r], r) for r in (1, 2, 3)]
+
+
+def three_terms(value):
+    high = lax.reduce_precision(value, 8, 7)
+    rest = value - high
+    middle = lax.reduce_precision(rest, 8, 7)
+    return [high.astype(jnp.bfloat16), middle.astype(jnp.bfloat16), (rest - middle).astype(jnp.bfloat16)]
+
+
+def tie(values, *others):
+    return lax.optimization_barrier((values, others))[0]
+
+
+def once(place, *arrays):
+    return (place, arrays)
 
 
 def paired_body(
@@ -797,157 +995,217 @@
         return lax.dynamic_index_in_dim(value, 1 - ctx_rank, axis, keepdims=False)
 
     def half_of(weight):
-        return mine(weight.reshape(row_width, 2, half_hidden), 1)
-
-    relative = by_distance(tokens.reshape(4, share, seq_count, width))
+        return jnp.where(ctx_rank == 0, weight[..., :half_hidden], weight[..., half_hidden:])
+
+    def add(left, right):
+        return left.astype(f32) + right.astype(f32)
+
+    rows = 2 * share
+    bin_up = binarize(latent_up, up_quant[0][None], up_quant[1][None])
+    bin_down = binarize(latent_down, down_quant[0][:, None], down_quant[1][:, None])
+    terms = [term for v in (bias_up, clip_hidden, t_bias_up) for term in three_terms(half_of(v))]
+    vectors = jnp.pad(jnp.stack(terms), ((0, 16 - len(terms)), (0, 0)))
+    bin_out = binarize(latent_out, out_quant[0][:, None], out_quant[1][:, None])
+    piece = jnp.concatenate(
+        [
+            half_of(bin_up),
+            half_of(bin_down),
+            jnp.concatenate([bin_out, t_out], axis=1),
+            vectors,
+        ],
+        axis=0,
+    )
+    piece_two = swap_tp(piece, 2)
+    rows = 2 * share
+    tokens_then, segment_then = tie((tokens, segment_ids), piece)
+    relative = by_distance(tokens_then.reshape(4, share, seq_count, width))
     own = mine(relative, 2).reshape(local_len, width)
-    other = swap_ctx(theirs(relative, 2).reshape(local_len, width))
     code = by_distance(
-        jnp.transpose(segment_ids * 2 + (valid_mask > 0).astype(jnp.int32)).reshape(
+        jnp.transpose(segment_then * 2 + (valid_mask > 0).astype(jnp.int32)).reshape(
             4, share, seq_count
         )
     )
+    code_sent = jnp.pad(theirs(code, 2).reshape(1, local_len), ((0, 15), (0, width - local_len)))
+    tokens_sent = jnp.concatenate(
+        [theirs(relative, 2).reshape(local_len, width), code_sent.astype(bf16)], axis=0
+    )
+    other = swap_ctx(tokens_sent)
+    latent_qkv_then, t_qkv = tie((latent_qkv, t_qkv), tokens_sent)
+    bin_qkv = jnp.transpose(
+        binarize(latent_qkv_then, qkv_quant[0][None], qkv_quant[1][None]), (1, 0, 2)
+    )
+    qkv_piece = jnp.concatenate([bin_qkv, jnp.transpose(t_qkv, (1, 0, 2))], axis=0)
+    qkv_pieces = fsdp_pieces(qkv_piece)
+    t_up, t_down = tie((t_up, t_down), qkv_piece)
+    teacher_piece = jnp.concatenate([half_of(t_up), half_of(t_down)], axis=0)
+    clip_in_row, clip_row = clip_in[None], clip_ctx[None]
+
+    full_qkv, a_own, qkv_own, token = project_own(place, own, qkv_pieces, bias_qv, clip_in_row)
+    other = tie(other, token)
     code_all = jnp.concatenate(
-        [mine(code, 2).reshape(local_len), swap_ctx(theirs(code, 2)).reshape(local_len)]
+        [mine(code, 2).reshape(local_len), other[local_len, :local_len].astype(jnp.int32)]
     )
     code_col, code_row = code_all[:, None], code_all[None, :]
     valid = (
         jnp.concatenate([code_all[:share], code_all[local_len : local_len + share]]) & 1
     ).astype(f32)[:, None]
-    bin_qkv = jnp.transpose(
-        binarize(latent_qkv, qkv_quant[0][None], qkv_quant[1][None]), (1, 0, 2)
-    )
-    student_qkv = fsdp_pieces(bin_qkv)
-    teacher_qkv = fsdp_pieces(jnp.transpose(t_qkv, (1, 0, 2)))
-    bin_out = binarize(latent_out, out_quant[0][:, None], out_quant[1][:, None])
-    bin_up = binarize(latent_up, up_quant[0][None], up_quant[1][None])
-    bin_down = binarize(latent_down, down_quant[0][:, None], down_quant[1][:, None])
-    out_pieces = fsdp_pieces(jnp.stack(tp_pieces(jnp.stack([bin_out, t_out]))))
-
-    def hidden_pieces(up, down):
-        parts = tp_pieces(jnp.stack([half_of(up), half_of(down)]))
-        return fsdp_pieces(jnp.stack(parts[:2])) + fsdp_pieces(jnp.stack(parts[2:]))
-
-    student_hidden = hidden_pieces(bin_up, bin_down)
-    teacher_hidden = hidden_pieces(t_up, t_down)
-    vectors = jnp.stack(
-        tp_pieces(
-            jnp.stack([mine(v.reshape(2, half_hidden), 0) for v in (bias_up, clip_hidden, t_bias_up)])
-        )
-    )
-    bias_up_all, clip_all, t_bias_up_all = vectors[:, 0], vectors[:, 1], vectors[:, 2]
-    clip_in_row, clip_row = clip_in[None], clip_ctx[None]
-
-    context, a_in, q, k, v, ratio, lse = attention_forward(
-        True, place, own, other, student_qkv, bias_qv, clip_in_row, clip_row, code_col, code_row
+    even = jnp.stack([piece, tie(piece_two, token)])
+    odd, even_row = swap_tp(even, 1), swap_row(even)
+    *context, a_other, other_rows, qkv, merged, lse = attention_forward(
+        True, once(place, even, token), other, full_qkv, qkv_own, bias_qv, clip_in_row,
+        clip_row, code_col, code_row,
     )
     contexts = exchange_tp(context)
-    (teacher_context,) = attention_forward(
-        False, place, own, other, teacher_qkv, t_bias_qv, clip_in_row, clip_row, code_col, code_row
-    )
+    odd, even_row = tie((odd, even_row), lse)
+    even_cores = (swap_core(even), swap_core(even_row))
+    odd_row = swap_row(odd)
+    *teacher_context, token = attention_forward(
+        False, once(place, lse, *even_cores), other, qkv_pieces, own,
+        t_bias_qv, clip_in_row, clip_row, code_col, code_row,
+    )
+    token = gate(place, token, *contexts[1:])
+    odd, odd_row, teacher_piece = tie((odd, odd_row, teacher_piece), token)
+    teacher_two = swap_tp(teacher_piece, 2)
+    pieces = (
+        even, even_row, *even_cores,
+        odd, odd_row, swap_core(odd), swap_core(odd_row),
+    )
+    own_rows = own[:share]
+    out_full, unit, scale, h_low, first_sums, token = out_norm(
+        True, once(place, token), contexts, pieces, own_rows, other_rows, valid, row_params
+    )
+    h_far = swap_ctx(h_low)
     teacher_contexts = exchange_tp(teacher_context)
-    own_rows, other_rows = own[:share], other[:share]
-    out_full, unit, scale, h_low, first_sums = out_norm(
-        True, place, contexts, out_pieces, own_rows, other_rows, valid, row_params
-    )
+    hidden_full, terms, hid_own, slope_own, part_own, _ = hidden_layer(
+        True, False, once(place, token), h_low, rows, pieces
+    )
+    teacher_even = jnp.stack([teacher_piece, tie(teacher_two, terms)])
+    teacher_odd, teacher_even_row = swap_tp(teacher_even, 1), swap_row(teacher_even)
+    cot_own = mine(cotangent, 1)
     h_teacher, ht_low = out_norm(
-        False, place, teacher_contexts, out_pieces, own_rows, other_rows, valid, t_rows
-    )
-    h_far = swap_ctx(h_low)
+        False, once(place, part_own), teacher_contexts, out_full, own_rows, other_rows, valid, t_rows,
+        (theirs(cotangent, 1),),
+    )
     ht_far = swap_ctx(ht_low)
-    hidden_full, hid_own, slope_own, part_own = hidden_layer(
-        True, False, place, h_low, student_hidden, bias_up_all, clip_all
-    )
-    hid_far, slope_far, part_far = hidden_layer(
-        True, True, place, h_far, hidden_full, bias_up_all, clip_all
+    hid_far, slope_far, part_far, token = hidden_layer(
+        True, True, once(place, ht_low), h_far, rows, hidden_full, terms
     )
     part_got = swap_ctx(part_far)
-    teacher_full, t_part_own = hidden_layer(
-        False, False, place, ht_low, teacher_hidden, t_bias_up_all, None
-    )
-    (t_part_far,) = hidden_layer(False, True, place, ht_far, teacher_full, t_bias_up_all, None)
+    teacher_even_row, teacher_odd = tie((teacher_even_row, teacher_odd), token)
+    teacher_odd_row = swap_row(teacher_odd)
+    teacher_hidden = (
+        teacher_even, teacher_even_row, swap_core(teacher_even), swap_core(teacher_even_row),
+        teacher_odd, teacher_odd_row, swap_core(teacher_odd), swap_core(teacher_odd_row),
+    )
+    teacher_full, t_part_far, _ = hidden_layer(
+        False, True, once(place, token), ht_far, rows, teacher_hidden, terms
+    )
     t_part_got = swap_ctx(t_part_far)
-    cot_own = mine(cotangent, 1)
-    cot_other = swap_ctx(theirs(cotangent, 1))
-    layer_own, layer_other, d_second, d_ffn, second_sums = loss_step(
+    t_part_own, _ = hidden_layer(
+        False, False, once(place, t_part_far), ht_low, rows, teacher_full, terms
+    )
+    layer_own, d_second, d_ffn, second_sums = loss_step(
         place, unit, part_own, part_got, h_teacher, t_part_own, t_part_got,
-        cot_own, cot_other, valid, row_params, t_rows,
+        cot_own, ht_far, valid, row_params, t_rows,
     )
 
     def home(own_part, other_part):
-        got = swap_ctx(other_part).astype(own_part.dtype)
+        got = other_part.astype(own_part.dtype)
         first = jnp.where(ctx_rank == 0, own_part, got)
         second = jnp.where(ctx_rank == 0, got, own_part)
         return jnp.stack([first, second], axis=1)
 
-    layer_out = home(layer_own, layer_other)
     d_ffn_far = swap_ctx(d_ffn)
+    layer_out = home(layer_own, d_ffn_far[rows:])
     du_own, d_part_own, du_sums_own = hidden_pull(False, place, d_ffn, hidden_full, slope_own)
     du_far, d_part_far, du_sums_far = hidden_pull(True, place, d_ffn_far, hidden_full, slope_far)
     d_part_got = swap_ctx(d_part_far)
-    keep_hidden, send_hidden = hidden_grads(
-        place, (d_ffn, d_ffn_far), (hid_own, hid_far), (h_low, h_far), (du_own, du_far)
-    )
-    d_first, d_attn, third_sums, d_context = first_pull(
-        place, d_second, d_part_own, d_part_got, unit, scale, row_params, out_full
+    keep_down, send_down = hidden_grads(
+        once(place, du_sums_far), (d_ffn, d_ffn_far), (hid_own, hid_far)
+    )
+    got_down = swap_core(send_down)
+    leave_down = add(keep_down[1], got_down[1]).astype(bf16)
+    d_first, d_attn, third_sums, *d_context = first_pull(
+        once(place, send_down), d_second, d_part_own, d_part_got, unit, scale, row_params, out_full
     )
     d_contexts = exchange_tp(d_context)
-    keep_out, send_out = out_grads(place, d_attn, contexts)
-    back, d_proj, d_bias_qv = attention_backward(
-        place, a_in, q, k, v, ratio, lse, code_col, code_row, d_contexts, student_qkv
-    )
-    backs = exchange_tp(back)
-    keep_in, send_in = in_grads(place, a_in, d_proj)
-    input_own, input_other = input_rows(place, d_first, backs, own_rows, other_rows, clip_in_row)
-    input_grad = home(input_own, input_other)
-
-    def over_fsdp(keep, send):
-        got = swap_core(send)
-        stay = keep[0].astype(f32) + got[0].astype(f32)
-        leave = (keep[1].astype(f32) + got[1].astype(f32)).astype(bf16)
-        return stay + swap_row(leave).astype(f32)
-
-    def over_tp(value, axis):
-        parts = [lax.index_in_dim(value, r, axis, keepdims=False) for r in range(4)]
-        return parts[0] + sum(swap_tp(parts[r].astype(bf16), r).astype(f32) for r in (1, 2, 3))
-
-    low_hidden = over_tp(over_fsdp(keep_hidden, send_hidden), 1).astype(bf16)
-    low_far = swap_ctx(low_hidden)
-    hidden_halves = [
-        jnp.where(ctx_rank == 0, low_hidden, low_far),
-        jnp.where(ctx_rank == 0, low_far, low_hidden),
-    ]
-    grad_hidden = jnp.concatenate(hidden_halves, axis=-1).astype(f32)
-    low_out = over_tp(over_fsdp(keep_out, send_out), 0).astype(bf16)
-    sum_out = low_out.astype(f32) + swap_ctx(low_out).astype(f32)
-    low_in = over_fsdp(keep_in, send_in).astype(bf16)
-    sum_in = low_in.astype(f32) + swap_ctx(low_in).astype(f32)
+    keep_up, send_up = hidden_grads(once(place, third_sums), (h_low, h_far), (du_own, du_far))
+    got_up = swap_core(send_up)
+    leave_up = add(keep_up[1], got_up[1]).astype(bf16)
+    vector = vector_rows(place, third_sums, second_sums, first_sums, du_sums_own, du_sums_far)
+    keep_back, send_back, d_proj, d_bias_qv = attention_backward(
+        once(place, leave_down, leave_up, vector),
+        qkv, clip_row, merged, lse, code_col, code_row, d_contexts, full_qkv,
+    )
+    got_back = swap_tp(send_back, 1)
+    got_down_row, got_up_row = tie((swap_row(leave_down), swap_row(leave_up)), d_bias_qv)
+    row_down = add(add(keep_down[0], got_down[0]), got_down_row)
+    row_up = add(add(keep_up[0], got_up[0]), got_up_row)
+    keep_last, send_last = last_grads(
+        once(place, send_back, got_down_row, got_up_row),
+        d_attn, contexts, (a_own, a_other), d_proj, d_bias_qv,
+    )
+    got_last, vector_got = swap_core(send_last), swap_core(tie(vector, send_last))
+    got_back = tie(got_back, send_last)
+    leave_back = add(keep_back[1], got_back[1]).astype(bf16)
+    got_back_two = swap_tp(leave_back, 2)
+    vector = tie(vector + vector_got, leave_back)
+    vector_got = swap_ctx(vector)
+    send_both = tie(jnp.stack([row_down[1::2], row_up[1::2]]).astype(bf16), leave_back)
+    got_both = swap_tp(send_both, 1)
+    leave_last = tie(add(keep_last[1], got_last[1]).astype(bf16), leave_back)
+    got_last_row = swap_row(leave_last)
+    vector = tie(vector + vector_got, leave_last)
+    vector_got = swap_row(vector)
+    entry = row_width
+    row_last = add(add(keep_last[0], got_last[0]), got_last_row)
+    send_one = jnp.stack([row_last[entry : 2 * entry], row_last[3 * entry : 4 * entry]]).astype(bf16)
+    got_one = swap_tp(send_one, 1)
+    leave_both = tie(
+        jnp.stack([add(row_down[2], got_both[0, 1]), add(row_up[2], got_both[1, 1])]).astype(bf16), send_one
+    )
+    got_both_two = swap_tp(leave_both, 2)
+    vector = tie(vector + vector_got, leave_both)
+    vector_got = swap_tp(vector, 1)
+    input_own, input_other = input_rows(
+        once(place, leave_both), d_first, (keep_back, got_back, got_back_two), own_rows, other_rows, clip_in_row
+    )
+    input_grad = home(input_own, swap_ctx(input_other))
+    leave_two = add(row_last[2 * entry : 3 * entry], got_one[1]).astype(bf16)
+    got_two = swap_tp(leave_two, 2)
+    low_both = add(
+        jnp.stack([add(row_down[0], got_both[0, 0]), add(row_up[0], got_both[1, 0])]), got_both_two
+    ).astype(bf16)
+    low_out = add(add(row_last[0:entry], got_one[0]), got_two)
+    low_last = jnp.concatenate([low_out, row_last[4 * entry :]], axis=0).astype(bf16)
+    sum_last = add(low_last, swap_ctx(low_last))
+    vector = tie(vector + vector_got, low_both)
+    vector = vector + swap_tp(vector, 2)
+
+    both_far = swap_ctx(low_both)
+    grad_both = jnp.concatenate(
+        [
+            jnp.where(ctx_rank == 0, low_both, both_far),
+            jnp.where(ctx_rank == 0, both_far, low_both),
+        ],
+        axis=-1,
+    ).astype(f32)
+    grad_up = straight(grad_both[1], latent_up, up_quant[0][None], up_quant[1][None])
+    grad_down = straight(
+        grad_both[0], latent_down, down_quant[0][:, None], down_quant[1][:, None]
+    )
     grad_qkv = straight(
-        jnp.transpose(sum_in, (1, 0, 2)), latent_qkv, qkv_quant[0][None], qkv_quant[1][None]
-    )
-    grad_out = straight(sum_out, latent_out, out_quant[0][:, None], out_quant[1][:, None])
-    grad_up = straight(grad_hidden[0], latent_up, up_quant[0][None], up_quant[1][None])
-    grad_down = straight(
-        grad_hidden[1], latent_down, down_quant[0][:, None], down_quant[1][:, None]
-    )
-    placed_up = by_distance(du_sums_own + du_sums_far)
-    placed_up = jnp.where(
-        jnp.arange(2)[None, :, None] == ctx_rank, placed_up[:, None], 0.0
-    ).reshape(hidden_width * 4 // width, width)
-    vector = jnp.concatenate([third_sums, second_sums, first_sums, placed_up], axis=0)
-    vector = vector + swap_core(vector)
-    vector = vector + swap_row(vector)
-    vector = vector + swap_ctx(vector)
-    vector = vector + swap_tp(vector, 1)
-    vector = vector + swap_tp(vector, 2)
-    qv_sums = d_bias_qv + swap_core(d_bias_qv)
-    qv_sums = qv_sums + swap_row(qv_sums)
-    grad_qv = qv_sums + swap_ctx(qv_sums)
+        jnp.transpose(sum_last[entry : 4 * entry].reshape(3, row_width, col_width), (1, 0, 2)),
+        latent_qkv,
+        qkv_quant[0][None],
+        qkv_quant[1][None],
+    )
+    grad_out = straight(sum_last[0:entry], latent_out, out_quant[0][:, None], out_quant[1][:, None])
+    grad_qv = sum_last[4 * entry : 4 * entry + 2]
     vector_sums = jnp.concatenate([vector[0:1], vector[3:4], vector[1:3], vector[4:6]], axis=0)
     stat_sums = jnp.sum(vector[6:11], axis=-1)
-    up_sums = vector[11:].reshape(4 * hidden_width)
     grad_rows = lax.dynamic_slice_in_dim(vector_sums, fsdp_rank * row_width, row_width, 1)
-    grad_bias_up = lax.dynamic_slice_in_dim(up_sums, tp_rank * hidden_width, hidden_width, 0)
+    grad_bias_up = lax.dynamic_index_in_dim(vector, 11 + tp_rank, 0, keepdims=False)
     denom = stat_sums[2]
     statistics = jnp.stack(
         [

time: 449 us -> 326 us (0.73)
  the two profiles are of different devices: /device:TPU:8 before, /device:TPU:0 now
where the time goes in v2:
time: 326 us; the launch traced here: 322 us
  waiting for transfers between devices  104 us (32%)
  Pallas kernels  73.8 us (23%)
  starting transfers between devices  60.8 us (19%)
  local copies, waits for them, and re-layouts  43.2 us (13%)
  other arithmetic  31.6 us (10%)
  between operations  7.88 us (2%)
    pallas_call x20, Pallas kernels, call_kernel(): pl.pallas_call(body, out_shape=outs, in_specs=[pl.BlockSpec(memory_space=...  73.8 us
    ppermute x11, waiting for transfers between devices, swap_ctx(): return lax.ppermute(value, 'ctx', [(0, 1), (1, 0)])  39.3 us
    ppermute x21, waiting for transfers between devices, swap_tp(): return lax.ppermute(value, 'tp', [(i, i ^ distance) for i in range(4)])  36.9 us
    ppermute x21, starting transfers between devices, swap_tp(): return lax.ppermute(value, 'tp', [(i, i ^ distance) for i in range(4)])  27.9 us
    ppermute x9, waiting for transfers between devices, swap_row(): return lax.ppermute(value, 'fsdp', [(i, i ^ 2) for i in range(4)])  27.3 us
    unnamed x205, local copies, waits for them, and re-layouts  26.5 us
    ppermute x9, starting transfers between devices, swap_row(): return lax.ppermute(value, 'fsdp', [(i, i ^ 2) for i in range(4)])  16 us
    ppermute x11, starting transfers between devices, swap_ctx(): return lax.ppermute(value, 'ctx', [(0, 1), (1, 0)])  15.2 us
  transfers between devices with their start and end apart: 55, of which 24 were waited for; matrix products, arithmetic and copies ran while one was open for 14% of the time, Pallas kernels for 22%

profile of v2, /device:TPU:0, one launch (start us, length us, event | category | flops | bytes accessed | tf_op | source)
XLA Modules:
  0.0 321.6 jit_solution(16138110177488757723)
XLA Ops:
  12.3 3.0 collective-permute-start.1
  15.3 1.5 collective-permute-start.4
  16.8 2.6 collective-permute-start
  19.4 9.2 %collective-permute-done.1.refs_2_.refs_10_ = bf16[6,192,192]{2,1,0:T(8,128)(2,1)S(1)} collective-permute-done((bf16[6,192,192]{2,1,0:T(8,128)(2,1)S(1)}, bf16[6,192,192]{2,1,0:T(8,128)(2,1)S(1)}, u32[]{:S(2)}, u32[]{:S(2)}) %collective-permute-start.1) | collective-permute-done | bytes 442400 | tf_op jit(solution)/shard_map/ppermute | solution.py:915
  32.6 1.5 shard_map.312
  36.0 3.4 %collective-permute-done = bf16[592,384]{1,0:T(8,128)(2,1)} collective-permute-done((bf16[592,384]{1,0:T(8,128)(2,1)}, bf16[592,384]{1,0:T(8,128)(2,1)}, u32[]{:S(2)}, u32[]{:S(2)}) %collective-permute-start) | collective-permute-done | bytes 454688 | tf_op jit(solution)/shard_map/ppermute | solution.py:919
  47.1 9.8 %shard_map.313 = (bf16[2,128,192]{2,1,0:T(8,128)(2,1)S(1)}, bf16[2,128,192]{2,1,0:T(8,128)(2,1)S(1)}, bf16[2,128,192]{2,1,0:T(8,128)(2,1)S(1)}, bf16[2,128,192]{...) custom-call(s32[3]{0:T(128)S(1)} %pad_add_fusion.2.place_ref, ...), custom_call_target="tpu_custom_call" | custom-call | flops 5033164800 | bytes 4718592 | tf_op jit(solution)/shard_map/pallas_call | solution.py:98
  58.5 3.2 collective-permute-done.7.refs_6_.refs_3_
  62.0 1.5 collective-permute-start.12
  64.3 1.7 collective-permute-start.9
  66.0 3.4 %collective-permute-start.10 = (bf16[2,128,192]{2,1,0:T(8,128)(2,1)S(1)}, bf16[2,128,192]{2,1,0:T(8,128)(2,1)S(1)}, u32[]{:S(2)}, u32[]{:S(2)}) collective-permute-start(bf16[2,128,192]{2,1,0:T(8,128)(2,1)S(1)} %get-tuple-element.117), channel_id=1, source_target_pairs={{0,2},{1,3},{2,0},{3,1},{4,6},{5,7},{6,4},{7,5},{8,10},{9,11},{10,... | collective-permute-start | bytes 294920 | tf_op jit(solution)/shard_map/ppermute | solution.py:919
  69.5 9.7 %shard_map.314 = (bf16[2,128,192]{2,1,0:T(8,128)(2,1)S(1)}, bf16[2,128,192]{2,1,0:T(8,128)(2,1)S(1)}, bf16[2,128,192]{2,1,0:T(8,128)(2,1)S(1)}, bf16[2,128,192]{2,1,0:T(8,128)(2,1)S(1)}, f32[8,128]{1,0:T(8,128)S(1)}) custom-call(s32[3]{0:T(128)S(1)} %pad_add_fusion.2.place_ref, f32[8,1024]{1,0:T(8,128)S(1)} %get-tuple-element.113.refs_0_.refs_6_, ...), custom_call_target="tpu_custom_call" | custom-call | flops 5033164800 | bytes 4718592 | tf_op jit(solution)/shard_map/pallas_call | solution.py:98
  81.8 3.1 collective-permute-done.12.refs_10_.refs_7_
  87.9 1.8 collective-permute-start.15
  89.7 3.4 %collective-permute-start.16 = (bf16[2,128,192]{2,1,0:T(8,128)(2,1)S(1)}, bf16[2,128,192]{2,1,0:T(8,128)(2,1)S(1)}, u32[]{:S(2)}, u32[]{:S(2)}) collective-permute-start(bf16[2,128,192]{2,1,0:T(8,128)(2,1)S(1)} %copy-done.47), channel_id=1, source_target_pairs={{0,2},{1,3},{2,0},{3,1},{4,6},{5,7},{6,4},{7,5},{8,10},{9,11},{10,... | collective-permute-start | bytes 294920 | tf_op jit(solution)/shard_map/ppermute | solution.py:919
  93.1 1.7 collective-permute-start.21
  97.8 3.5 %shard_map.316 = (bf16[4,768,384]{2,1,0:T(8,128)(2,1)S(1)}, f32[256,768]{1,0:T(8,128)S(1)}, f32[256,1]{1,0:T(8,128)S(1)}, bf16[256,768]{1,0:T(8,128)(2,1)S(1)}, ...) custom-call(s32[3]{0:T(128)S(1)} %pad_add_fusion.2.place_ref, f32[8,128]{1,0:T(8,128)S(1)} %shard_map.315.refs_0_, ...), custom_call_target="tpu_custom_call" | custom-call | flops 1207959552 | bytes 2359296 | tf_op jit(solution)/shard_map/pallas_call | solution.py:98
  101.9 5.5 %shard_map.317 = (bf16[4,2,768,384]{3,2,1,0:T(8,128)(2,1)S(1)}, bf16[4,16,384]{2,1,0:T(8,128)(2,1)S(1)}, bf16[4,256,384]{2,1,0:T(8,128)(2,1)S(1)}, bf16[4,256,38...) custom-call(s32[3]{0:T(128)S(1)} %pad_add_fusion.2.place_ref, ...), custom_call_target="tpu_custom_call" | custom-call | flops 4831838208 | bytes 6291456 | tf_op jit(solution)/shard_map/pallas_call | solution.py:98
  107.4 10.1 %collective-permute-done.21 = bf16[384,384]{1,0:T(8,128)(2,1)S(1)} collective-permute-done((bf16[384,384]{1,0:T(8,128)(2,1)}, bf16[384,384]{1,0:T(8,128)(2,1)S(1)}, u32[]{:S(2)}, u32[]{:S(2)}) %collective-permute-start.21) | collective-permute-done | bytes 294944 | tf_op jit(solution)/shard_map/ppermute | solution.py:919
  118.7 1.6 collective-permute-start.22
  121.1 1.5 shard_map.318
  122.6 2.9 shard_map.319
  125.5 7.5 %collective-permute-done.23.refs_6_ = bf16[2,384,384]{2,1,0:T(8,128)(2,1)S(1)} collective-permute-done((bf16[2,384,384]{2,1,0:T(8,128)(2,1)S(1)}, bf16[2,384,384]{2,1,0:T(8,128)(2,1)S(1)}, u32[]{:S(2)}, u32[]{:S(2)}) %collective-permute-start.23) | collective-permute-done | bytes 589856 | tf_op jit(solution)/shard_map/ppermute | solution.py:919
  133.1 1.5 collective-permute-start.26
  135.7 10.9 %collective-permute-done.26.refs_7_ = bf16[2,384,384]{2,1,0:T(8,128)(2,1)S(1)} collective-permute-done((bf16[2,384,384]{2,1,0:T(8,128)(2,1)S(1)}, bf16[2,384,384]{2,1,0:T(8,128)(2,1)S(1)}, u32[]{:S(2)}, u32[]{:S(2)}) %collective-permute-start.26) | collective-permute-done | bytes 589856 | tf_op jit(solution)/shard_map/ppermute | solution.py:915
  147.2 3.5 %collective-permute-done.20.refs_1_.refs_7_ = bf16[384,768]{1,0:T(8,128)(2,1)S(1)} collective-permute-done((bf16[384,768]{1,0:T(8,128)(2,1)S(1)}, bf16[384,768]{1,0:T(8,128)(2,1)S(1)}, u32[]{:S(2)}, u32[]{:S(2)}) %collective-permute-start.20) | collective-permute-done | bytes 589856 | tf_op jit(solution)/shard_map/ppermute | solution.py:907
  150.8 3.3 %shard_map.320 = (bf16[4,2,768,384]{3,2,1,0:T(8,128)(2,1)S(1)}, bf16[256,768]{1,0:T(8,128)(2,1)S(1)}, f32[8,128]{1,0:T(8,128)}) custom-call(s32[3]{0:T(128)S(1)} %pad_add_fusion.2.place_ref, f32[8,128]{1,0:T(8,128)S(1)} %get-tuple-element.140.refs_0_, bf16[384,768]{1,0:T(8,128)(2,1)S(1)} %collective-permute-done.20.refs_1_.refs_7_, ...), custom_call_target="tpu_custom_call" | custom-call | flops 4831838208 | bytes 6291456 | tf_op jit(solution)/shard_map/pallas_call | solution.py:98
  154.6 3.2 shard_map.321
  159.2 8.0 %collective-permute-done.29.refs_5_ = bf16[256,768]{1,0:T(8,128)(2,1)S(1)} collective-permute-done((bf16[256,768]{1,0:T(8,128)(2,1)S(1)}, bf16[256,768]{1,0:T(8,128)(2,1)S(1)}, u32[]{:S(2)}, u32[]{:S(2)}) %collective-permute-start.29) | collective-permute-done | bytes 393248 | tf_op jit(solution)/shard_map/ppermute | solution.py:907
  167.2 2.0 shard_map.322
  169.8 2.4 shard_map.325
  172.2 12.0 %collective-permute-done.30.refs_0_.refs_2_ = bf16[384,768]{1,0:T(8,128)(2,1)S(1)} collective-permute-done((bf16[384,768]{1,0:T(8,128)(2,1)S(1)}, bf16[384,768]{1,0:T(8,128)(2,1)S(1)}, u32[]{:S(2)}, u32[]{:S(2)}) %collective-permute-start.30) | collective-permute-done | bytes 589856 | tf_op jit(solution)/shard_map/ppermute | solution.py:907
  184.2 2.4 shard_map.323
  187.3 2.5 shard_map.324
  189.8 6.7 %collective-permute-done.33.refs_3_ = bf16[256,768]{1,0:T(8,128)(2,1)S(1)} collective-permute-done((bf16[256,768]{1,0:T(8,128)(2,1)S(1)}, bf16[256,768]{1,0:T(8,128)(2,1)S(1)}, u32[]{:S(2)}, u32[]{:S(2)}) %collective-permute-start.33) | collective-permute-done | bytes 393248 | tf_op jit(solution)/shard_map/ppermute | solution.py:907
  196.6 1.6 shard_map.326
  199.1 2.5 shard_map.327
  201.7 1.7 collective-permute-start.36
  204.7 1.5 collective-permute-start.38
  209.8 6.5 %collective-permute-done.37.refs_11_ = bf16[2,128,192]{2,1,0:T(8,128)(2,1)S(1)} collective-permute-done((bf16[2,128,192]{2,1,0:T(8,128)(2,1)S(1)}, bf16[2,128,192]{2,1,0:T(8,128)(2,1)S(1)}, u32[]{:S(2)}, u32[]{:S(2)}) %collective-permute-start.37) | collective-permute-done | bytes 98336 | tf_op jit(solution)/shard_map/ppermute | solution.py:919
  216.4 14.6 %shard_map.329 = (bf16[2,2,128,768]{3,2,1,0:T(8,128)(2,1)S(1)}, bf16[2,2,128,768]{3,2,1,0:T(8,128)(2,1)}, bf16[3,1024,192]{2,1,0:T(8,128)(2,1)S(1)}, f32[2,192]{1,0:T(2,128)S(1)}) custom-call(s32[3]{0:T(128)S(1)} %pad_add_fusion.2.place_ref, bf16[4,192,384]{2,1,0:T(8,128)(2,1)S(1)} %fusion.4.refs_0_, bf16[4,192,384]{2,1,0:T(8,128)(2,1)S(1)} %fusion.5.refs_1_, ...), custom_call_target="tpu_custom_call" | custom-call | flops 11676942336 | bytes 6291456 | tf_op jit(solution)/shard_map/pallas_call | solution.py:98
  231.0 2.6 collective-permute-start.39
  234.5 2.6 shard_map.330
  238.3 1.6 copy.63
  240.0 2.8 fusion.35
  245.5 2.5 collective-permute-done.39.refs_3_
  248.9 1.7 collective-permute-start.40
  251.8 2.2 copy.75
  254.0 2.1 fusion.3
  256.1 2.2 copy.66
  259.5 1.8 select_bitcast_fusion.1
  264.2 2.4 slice_add_fusion.1
  266.5 2.2 copy.74
  268.7 4.6 %collective-permute-start.52 = (f32[16,768]{1,0:T(8,128)}, f32[16,768]{1,0:T(8,128)}, u32[]{:S(2)}, u32[]{:S(2)}) collective-permute-start(f32[16,768]{1,0:T(8,128)} %add.145), channel_id=1, source_target_pairs={{0,16},{8,24},{16,0},{24,8},{1,17},{9,25},{17,1},{25,9},{2,18},{10... | collective-permute-start | bytes 147464 | tf_op jit(solution)/shard_map/ppermute | solution.py:915
  273.2 2.2 copy.67
  275.4 1.6 fusion.34
  278.6 1.5 collective-permute-start.53
  283.6 8.0 %collective-permute-start.44 = (bf16[128,768]{1,0:T(8,128)(2,1)S(1)}, bf16[128,768]{1,0:T(8,128)(2,1)S(1)}, u32[]{:S(2)}, u32[]{:S(2)}) collective-permute-start(bf16[128,768]{1,0:T(8,128)(2,1)S(1)} %get-tuple-element.192), channel_id=1, source_target_pairs={{0,4},{4,0},{1,5},{5,1},{2,6},{6,2},{3,7},{7,3},{8,12},{12,8},{9,1... | collective-permute-start | bytes 589832 | tf_op jit(solution)/shard_map/ppermute | solution.py:907
  291.7 4.9 %collective-permute-done.44 = bf16[128,768]{1,0:T(8,128)(2,1)S(1)} collective-permute-done((bf16[128,768]{1,0:T(8,128)(2,1)S(1)}, bf16[128,768]{1,0:T(8,128)(2,1)S(1)}, u32[]{:S(2)}, u32[]{:S(2)}) %collective-permute-start.44) | collective-permute-done | bytes 196640 | tf_op jit(solution)/shard_map/ppermute | solution.py:907
  296.8 1.5 copy.69
  298.2 3.2 collective-permute-done.46
  301.8 2.0 collective-permute-start.49
  303.8 2.8 collective-permute-done.54
  317.2 1.5 collective-permute-done.49
  (373 shorter events, 73.2 us)
Async XLA Ops:
  12.2 19.3 %copy-start.37 = (f32[2,192]{1,0:T(2,128)S(1)}, f32[2,192]{1,0:T(2,128)}, u32[]{:S(2)}) copy-start(f32[2,192]{1,0:T(2,128)} %refs_3_.1) | copy-start | bytes 4612
  12.3 16.4 %collective-permute-start.1 = (bf16[6,192,192]{2,1,0:T(8,128)(2,1)S(1)}, bf16[6,192,192]{2,1,0:T(8,128)(2,1)S(1)}, u32[]{:S(2)}, u32[]{:S(2)}) collective-permute-start(bf16[6,192,192]{2,1,0:T(8,128)(2,1)S(1)} %pad_maximum_fusion.2.refs_1_.refs_9_), channel_id=1, source_target_pairs={{0,16},{8,24},{16,0},{24,8},{1,17},{9,25},{17,1},{25,9},{2,18},{10... | collective-permute-start | bytes 1327112 | tf_op jit(solution)/shard_map/ppermute | solution.py:915
  15.3 26.4 %collective-permute-start.4 = (bf16[528,768]{1,0:T(8,128)(2,1)}, bf16[528,768]{1,0:T(8,128)(2,1)}, u32[]{:S(2)}, u32[]{:S(2)}) collective-permute-start(bf16[528,768]{1,0:T(8,128)(2,1)} %fusion.2), channel_id=1, source_target_pairs={{0,4},{4,0},{1,5},{5,1},{2,6},{6,2},{3,7},{7,3},{8,12},{12,8},{9,1... | collective-permute-start | bytes 2433032 | tf_op jit(solution)/shard_map/ppermute | solution.py:907
  16.8 22.6 %collective-permute-start = (bf16[592,384]{1,0:T(8,128)(2,1)}, bf16[592,384]{1,0:T(8,128)(2,1)}, u32[]{:S(2)}, u32[]{:S(2)}) collective-permute-start(bf16[592,384]{1,0:T(8,128)(2,1)} %fusion.11), channel_id=1, source_target_pairs={{0,2},{1,3},{2,0},{3,1},{4,6},{5,7},{6,4},{7,5},{8,10},{9,11},{10,... | collective-permute-start | bytes 1363976 | tf_op jit(solution)/shard_map/ppermute | solution.py:919
  19.4 10.5 %collective-permute-start.2 = (bf16[6,192,192]{2,1,0:T(8,128)(2,1)S(1)}, bf16[6,192,192]{2,1,0:T(8,128)(2,1)S(1)}, u32[]{:S(2)}, u32[]{:S(2)}) collective-permute-start(bf16[6,192,192]{2,1,0:T(8,128)(2,1)S(1)} %pad_maximum_fusion.2.refs_1_.refs_9_), channel_id=1, source_target_pairs={{0,8},{8,0},{16,24},{24,16},{1,9},{9,1},{17,25},{25,17},{2,10},{10... | collective-permute-start | bytes 1327112 | tf_op jit(solution)/shard_map/ppermute | solution.py:911
  28.7 2.0 collective-permute-start.3
  40.5 21.1 %collective-permute-start.7 = (bf16[2,592,384]{2,1,0:T(8,128)(2,1)S(1)}, bf16[2,592,384]{2,1,0:T(8,128)(2,1)S(1)}, u32[]{:S(2)}, u32[]{:S(2)}) collective-permute-start(bf16[2,592,384]{2,1,0:T(8,128)(2,1)S(1)} %pad_maximum_fusion.refs_0_.refs_5_.refs_2_), channel_id=1, source_target_pairs={{0,16},{8,24},{16,0},{24,8},{1,17},{9,25},{17,1},{25,9},{2,18},{10... | collective-permute-start | bytes 2727944 | tf_op jit(solution)/shard_map/ppermute | solution.py:915
  41.1 20.9 %collective-permute-start.6 = (bf16[2,592,384]{2,1,0:T(8,128)(2,1)S(1)}, bf16[2,592,384]{2,1,0:T(8,128)(2,1)}, u32[]{:S(2)}, u32[]{:S(2)}) collective-permute-start(bf16[2,592,384]{2,1,0:T(8,128)(2,1)S(1)} %pad_maximum_fusion.refs_0_.refs_5_.refs_2_), channel_id=1, source_target_pairs={{0,1},{1,0},{2,3},{3,2},{4,5},{5,4},{6,7},{7,6},{8,9},{9,8},{10,11... | collective-permute-start | bytes 2727944 | tf_op jit(solution)/shard_map/ppermute | solution.py:919
  41.8 27.6 %collective-permute-start.5 = (bf16[2,592,384]{2,1,0:T(8,128)(2,1)S(1)}, bf16[2,592,384]{2,1,0:T(8,128)(2,1)}, u32[]{:S(2)}, u32[]{:S(2)}) collective-permute-start(bf16[2,592,384]{2,1,0:T(8,128)(2,1)S(1)} %pad_maximum_fusion.refs_0_.refs_5_.refs_2_), channel_id=1, source_target_pairs={{0,8},{8,0},{16,24},{24,16},{1,9},{9,1},{17,25},{25,17},{2,10},{10... | collective-permute-start | bytes 2727944 | tf_op jit(solution)/shard_map/ppermute | solution.py:911
  47.1 22.3 %copy-start.16 = (bf16[6,192,192]{2,1,0:T(8,128)(2,1)S(1)}, bf16[6,192,192]{2,1,0:T(8,128)(2,1)}, u32[]{:S(2)}) copy-start(bf16[6,192,192]{2,1,0:T(8,128)(2,1)} %copy-done.14) | copy-start | bytes 1327108
  58.4 20.8 %copy-start.56 = (bf16[512,768]{1,0:T(8,128)(2,1)}, bf16[512,768]{1,0:T(8,128)(2,1)S(1)}, u32[]{:S(2)}) copy-start(bf16[512,768]{1,0:T(8,128)(2,1)S(1)} %get-tuple-element.182.refs_9_) | copy-start | bytes 2359300
  58.4 20.8 %copy-start.58 = (f32[192,1024]{1,0:T(8,128)}, f32[192,1024]{1,0:T(8,128)S(1)}, u32[]{:S(2)}) copy-start(f32[192,1024]{1,0:T(8,128)S(1)} %get-tuple-element.170.refs_5_) | copy-start | bytes 2359300
  58.4 20.8 %copy-start.60 = (f32[8,1024]{1,0:T(8,128)}, f32[8,1024]{1,0:T(8,128)S(1)}, u32[]{:S(2)}) copy-start(f32[8,1024]{1,0:T(8,128)S(1)} %get-tuple-element.113.refs_0_.refs_6_) | copy-start | bytes 98308
  62.0 7.5 %collective-permute-start.8 = (bf16[2,592,384]{2,1,0:T(8,128)(2,1)S(1)}, bf16[2,592,384]{2,1,0:T(8,128)(2,1)S(1)}, u32[]{:S(2)}, u32[]{:S(2)}) collective-permute-start(bf16[2,592,384]{2,1,0:T(8,128)(2,1)S(1)} %collective-permute-done.7.refs_6_.refs_3_), channel_id=1, source_target_pairs={{0,8},{8,0},{16,24},{24,16},{1,9},{9,1},{17,25},{25,17},{2,10},{10... | collective-permute-start | bytes 2727944 | tf_op jit(solution)/shard_map/ppermute | solution.py:911
  62.0 22.9 %collective-permute-start.12 = (bf16[2,592,384]{2,1,0:T(8,128)(2,1)}, bf16[2,592,384]{2,1,0:T(8,128)(2,1)}, u32[]{:S(2)}, u32[]{:S(2)}) collective-permute-start(bf16[2,592,384]{2,1,0:T(8,128)(2,1)} %collective-permute-done.6.refs_9_.refs_6_), channel_id=1, source_target_pairs={{0,16},{8,24},{16,0},{24,8},{1,17},{9,25},{17,1},{25,9},{2,18},{10... | collective-permute-start | bytes 2727944 | tf_op jit(solution)/shard_map/ppermute | solution.py:915
  64.3 16.9 %collective-permute-start.9 = (bf16[2,128,192]{2,1,0:T(8,128)(2,1)S(1)}, bf16[2,128,192]{2,1,0:T(8,128)(2,1)S(1)}, u32[]{:S(2)}, u32[]{:S(2)}) collective-permute-start(bf16[2,128,192]{2,1,0:T(8,128)(2,1)S(1)} %get-tuple-element.116), channel_id=1, source_target_pairs={{0,1},{1,0},{2,3},{3,2},{4,5},{5,4},{6,7},{7,6},{8,9},{9,8},{10,11... | collective-permute-start | bytes 294920 | tf_op jit(solution)/shard_map/ppermute | solution.py:919
  66.0 15.2 %collective-permute-start.10 = (bf16[2,128,192]{2,1,0:T(8,128)(2,1)S(1)}, bf16[2,128,192]{2,1,0:T(8,128)(2,1)S(1)}, u32[]{:S(2)}, u32[]{:S(2)}) collective-permute-start(bf16[2,128,192]{2,1,0:T(8,128)(2,1)S(1)} %get-tuple-element.117), channel_id=1, source_target_pairs={{0,2},{1,3},{2,0},{3,1},{4,6},{5,7},{6,4},{7,5},{8,10},{9,11},{10,... | collective-permute-start | bytes 294920 | tf_op jit(solution)/shard_map/ppermute | solution.py:919
  69.4 11.8 %collective-permute-start.11 = (bf16[2,128,192]{2,1,0:T(8,128)(2,1)S(1)}, bf16[2,128,192]{2,1,0:T(8,128)(2,1)S(1)}, u32[]{:S(2)}, u32[]{:S(2)}) collective-permute-start(bf16[2,128,192]{2,1,0:T(8,128)(2,1)S(1)} %get-tuple-element.118), channel_id=1, source_target_pairs={{0,3},{1,2},{2,1},{3,0},{4,7},{5,6},{6,5},{7,4},{8,11},{9,10},{10,... | collective-permute-start | bytes 294920 | tf_op jit(solution)/shard_map/ppermute | solution.py:919
  84.9 8.2 %collective-permute-start.13 = (bf16[2,592,384]{2,1,0:T(8,128)(2,1)}, bf16[2,592,384]{2,1,0:T(8,128)(2,1)}, u32[]{:S(2)}, u32[]{:S(2)}) collective-permute-start(bf16[2,592,384]{2,1,0:T(8,128)(2,1)} %collective-permute-done.6.refs_9_.refs_6_), channel_id=1, source_target_pairs={{0,8},{8,0},{16,24},{24,16},{1,9},{9,1},{17,25},{25,17},{2,10},{10... | collective-permute-start | bytes 2727944 | tf_op jit(solution)/shard_map/ppermute | solution.py:911
  84.9 9.9 %collective-permute-start.14 = (bf16[2,592,384]{2,1,0:T(8,128)(2,1)}, bf16[2,592,384]{2,1,0:T(8,128)(2,1)}, u32[]{:S(2)}, u32[]{:S(2)}) collective-permute-start(bf16[2,592,384]{2,1,0:T(8,128)(2,1)} %collective-permute-done.12.refs_10_.refs_7_), channel_id=1, source_target_pairs={{0,8},{8,0},{16,24},{24,16},{1,9},{9,1},{17,25},{25,17},{2,10},{10... | collective-permute-start | bytes 2727944 | tf_op jit(solution)/shard_map/ppermute | solution.py:911
  87.9 30.8 %collective-permute-start.15 = (bf16[2,128,192]{2,1,0:T(8,128)(2,1)S(1)}, bf16[2,128,192]{2,1,0:T(8,128)(2,1)S(1)}, u32[]{:S(2)}, u32[]{:S(2)}) collective-permute-start(bf16[2,128,192]{2,1,0:T(8,128)(2,1)S(1)} %copy-done.49), channel_id=1, source_target_pairs={{0,1},{1,0},{2,3},{3,2},{4,5},{5,4},{6,7},{7,6},{8,9},{9,8},{10,11... | collective-permute-start | bytes 294920 | tf_op jit(solution)/shard_map/ppermute | solution.py:919
  89.7 31.4 %collective-permute-start.16 = (bf16[2,128,192]{2,1,0:T(8,128)(2,1)S(1)}, bf16[2,128,192]{2,1,0:T(8,128)(2,1)S(1)}, u32[]{:S(2)}, u32[]{:S(2)}) collective-permute-start(bf16[2,128,192]{2,1,0:T(8,128)(2,1)S(1)} %copy-done.47), channel_id=1, source_target_pairs={{0,2},{1,3},{2,0},{3,1},{4,6},{5,7},{6,4},{7,5},{8,10},{9,11},{10,... | collective-permute-start | bytes 294920 | tf_op jit(solution)/shard_map/ppermute | solution.py:919
  93.1 28.0 %collective-permute-start.17 = (bf16[2,128,192]{2,1,0:T(8,128)(2,1)}, bf16[2,128,192]{2,1,0:T(8,128)(2,1)S(1)}, u32[]{:S(2)}, u32[]{:S(2)}) collective-permute-start(bf16[2,128,192]{2,1,0:T(8,128)(2,1)} %copy-done.45), channel_id=1, source_target_pairs={{0,3},{1,2},{2,1},{3,0},{4,7},{5,6},{6,5},{7,4},{8,11},{9,10},{10,... | collective-permute-start | bytes 294920 | tf_op jit(solution)/shard_map/ppermute | solution.py:919
  93.1 24.4 %collective-permute-start.21 = (bf16[384,384]{1,0:T(8,128)(2,1)}, bf16[384,384]{1,0:T(8,128)(2,1)S(1)}, u32[]{:S(2)}, u32[]{:S(2)}) collective-permute-start(bf16[384,384]{1,0:T(8,128)(2,1)} %pad_maximum_fusion.7), channel_id=1, source_target_pairs={{0,2},{1,3},{2,0},{3,1},{4,6},{5,7},{6,4},{7,5},{8,10},{9,11},{10,... | collective-permute-start | bytes 884744 | tf_op jit(solution)/shard_map/ppermute | solution.py:919
  101.3 21.3 %collective-permute-start.18 = (bf16[256,768]{1,0:T(8,128)(2,1)S(1)}, bf16[256,768]{1,0:T(8,128)(2,1)S(1)}, u32[]{:S(2)}, u32[]{:S(2)}) collective-permute-start(bf16[256,768]{1,0:T(8,128)(2,1)S(1)} %get-tuple-element.128.refs_1_), channel_id=1, source_target_pairs={{0,4},{4,0},{1,5},{5,1},{2,6},{6,2},{3,7},{7,3},{8,12},{12,8},{9,1... | collective-permute-start | bytes 1179656 | tf_op jit(solution)/shard_map/ppermute | solution.py:907
  118.6 14.4 %collective-permute-start.23 = (bf16[2,384,384]{2,1,0:T(8,128)(2,1)S(1)}, bf16[2,384,384]{2,1,0:T(8,128)(2,1)S(1)}, u32[]{:S(2)}, u32[]{:S(2)}) collective-permute-start(bf16[2,384,384]{2,1,0:T(8,128)(2,1)S(1)} %pad_maximum_fusion.3.refs_2_), channel_id=1, source_target_pairs={{0,1},{1,0},{2,3},{3,2},{4,5},{5,4},{6,7},{7,6},{8,9},{9,8},{10,11... | collective-permute-start | bytes 1769480 | tf_op jit(solution)/shard_map/ppermute | solution.py:919
  118.7 14.4 %collective-permute-start.22 = (bf16[2,384,384]{2,1,0:T(8,128)(2,1)S(1)}, bf16[2,384,384]{2,1,0:T(8,128)(2,1)S(1)}, u32[]{:S(2)}, u32[]{:S(2)}) collective-permute-start(bf16[2,384,384]{2,1,0:T(8,128)(2,1)S(1)} %pad_maximum_fusion.3.refs_2_), channel_id=1, source_target_pairs={{0,16},{8,24},{16,0},{24,8},{1,17},{9,25},{17,1},{25,9},{2,18},{10... | collective-permute-start | bytes 1769480 | tf_op jit(solution)/shard_map/ppermute | solution.py:915
  133.1 13.5 %collective-permute-start.26 = (bf16[2,384,384]{2,1,0:T(8,128)(2,1)S(1)}, bf16[2,384,384]{2,1,0:T(8,128)(2,1)S(1)}, u32[]{:S(2)}, u32[]{:S(2)}) collective-permute-start(bf16[2,384,384]{2,1,0:T(8,128)(2,1)S(1)} %collective-permute-done.23.refs_6_), channel_id=1, source_target_pairs={{0,16},{8,24},{16,0},{24,8},{1,17},{9,25},{17,1},{25,9},{2,18},{10... | collective-permute-start | bytes 1769480 | tf_op jit(solution)/shard_map/ppermute | solution.py:915
  134.6 12.0 %collective-permute-start.24 = (bf16[2,384,384]{2,1,0:T(8,128)(2,1)S(1)}, bf16[2,384,384]{2,1,0:T(8,128)(2,1)S(1)}, u32[]{:S(2)}, u32[]{:S(2)}) collective-permute-start(bf16[2,384,384]{2,1,0:T(8,128)(2,1)S(1)} %pad_maximum_fusion.3.refs_2_), channel_id=1, source_target_pairs={{0,8},{8,0},{16,24},{24,16},{1,9},{9,1},{17,25},{25,17},{2,10},{10... | collective-permute-start | bytes 1769480 | tf_op jit(solution)/shard_map/ppermute | solution.py:911
  134.6 16.1 %collective-permute-start.20 = (bf16[384,768]{1,0:T(8,128)(2,1)S(1)}, bf16[384,768]{1,0:T(8,128)(2,1)S(1)}, u32[]{:S(2)}, u32[]{:S(2)}) collective-permute-start(bf16[384,768]{1,0:T(8,128)(2,1)S(1)} %get-tuple-element.135.refs_0_.refs_1_), channel_id=1, source_target_pairs={{0,4},{4,0},{1,5},{5,1},{2,6},{6,2},{3,7},{7,3},{8,12},{12,8},{9,1... | collective-permute-start | bytes 1769480 | tf_op jit(solution)/shard_map/ppermute | solution.py:907
  135.2 15.6 %collective-permute-start.27 = (bf16[2,384,384]{2,1,0:T(8,128)(2,1)S(1)}, bf16[2,384,384]{2,1,0:T(8,128)(2,1)S(1)}, u32[]{:S(2)}, u32[]{:S(2)}) collective-permute-start(bf16[2,384,384]{2,1,0:T(8,128)(2,1)S(1)} %collective-permute-done.23.refs_6_), channel_id=1, source_target_pairs={{0,8},{8,0},{16,24},{24,16},{1,9},{9,1},{17,25},{25,17},{2,10},{10... | collective-permute-start | bytes 1769480 | tf_op jit(solution)/shard_map/ppermute | solution.py:911
  135.4 15.4 %collective-permute-start.25 = (bf16[2,384,384]{2,1,0:T(8,128)(2,1)S(1)}, bf16[2,384,384]{2,1,0:T(8,128)(2,1)S(1)}, u32[]{:S(2)}, u32[]{:S(2)}) collective-permute-start(bf16[2,384,384]{2,1,0:T(8,128)(2,1)S(1)} %collective-permute-done.22.refs_3_), channel_id=1, source_target_pairs={{0,8},{8,0},{16,24},{24,16},{1,9},{9,1},{17,25},{25,17},{2,10},{10... | collective-permute-start | bytes 1769480 | tf_op jit(solution)/shard_map/ppermute | solution.py:911
  146.6 4.2 %collective-permute-start.28 = (bf16[2,384,384]{2,1,0:T(8,128)(2,1)S(1)}, bf16[2,384,384]{2,1,0:T(8,128)(2,1)S(1)}, u32[]{:S(2)}, u32[]{:S(2)}) collective-permute-start(bf16[2,384,384]{2,1,0:T(8,128)(2,1)S(1)} %collective-permute-done.26.refs_7_), channel_id=1, source_target_pairs={{0,8},{8,0},{16,24},{24,16},{1,9},{9,1},{17,25},{25,17},{2,10},{10... | collective-permute-start | bytes 1769480 | tf_op jit(solution)/shard_map/ppermute | solution.py:911
  146.6 12.6 %collective-permute-start.19 = (bf16[256,768]{1,0:T(8,128)(2,1)S(1)}, bf16[256,768]{1,0:T(8,128)(2,1)S(1)}, u32[]{:S(2)}, u32[]{:S(2)}) collective-permute-start(bf16[256,768]{1,0:T(8,128)(2,1)S(1)} %get-tuple-element.138), channel_id=1, source_target_pairs={{0,4},{4,0},{1,5},{5,1},{2,6},{6,2},{3,7},{7,3},{8,12},{12,8},{9,1... | collective-permute-start | bytes 1179656 | tf_op jit(solution)/shard_map/ppermute | solution.py:907
  154.1 13.2 %collective-permute-start.29 = (bf16[256,768]{1,0:T(8,128)(2,1)S(1)}, bf16[256,768]{1,0:T(8,128)(2,1)S(1)}, u32[]{:S(2)}, u32[]{:S(2)}) collective-permute-start(bf16[256,768]{1,0:T(8,128)(2,1)S(1)} %get-tuple-element.145.refs_0_), channel_id=1, source_target_pairs={{0,4},{4,0},{1,5},{5,1},{2,6},{6,2},{3,7},{7,3},{8,12},{12,8},{9,1... | collective-permute-start | bytes 1179656 | tf_op jit(solution)/shard_map/ppermute | solution.py:907
  169.2 15.0 %collective-permute-start.30 = (bf16[384,768]{1,0:T(8,128)(2,1)S(1)}, bf16[384,768]{1,0:T(8,128)(2,1)S(1)}, u32[]{:S(2)}, u32[]{:S(2)}) collective-permute-start(bf16[384,768]{1,0:T(8,128)(2,1)S(1)} %get-tuple-element.149.refs_1_.refs_0_), channel_id=1, source_target_pairs={{0,4},{4,0},{1,5},{5,1},{2,6},{6,2},{3,7},{7,3},{8,12},{12,8},{9,1... | collective-permute-start | bytes 1769480 | tf_op jit(solution)/shard_map/ppermute | solution.py:907
  186.7 9.9 %collective-permute-start.33 = (bf16[256,768]{1,0:T(8,128)(2,1)S(1)}, bf16[256,768]{1,0:T(8,128)(2,1)S(1)}, u32[]{:S(2)}, u32[]{:S(2)}) collective-permute-start(bf16[256,768]{1,0:T(8,128)(2,1)S(1)} %get-tuple-element.159), channel_id=1, source_target_pairs={{0,4},{4,0},{1,5},{5,1},{2,6},{6,2},{3,7},{7,3},{8,12},{12,8},{9,1... | collective-permute-start | bytes 1179656 | tf_op jit(solution)/shard_map/ppermute | solution.py:907
  189.8 17.0 %collective-permute-start.31 = (bf16[2,4,192,384]{3,2,1,0:T(8,128)(2,1)S(1)}, bf16[2,4,192,384]{3,2,1,0:T(8,128)(2,1)S(1)}, u32[]{:S(2)}, u32[]{:S(2)}) collective-permute-start(bf16[2,4,192,384]{3,2,1,0:T(8,128)(2,1)S(1)} %get-tuple-element.155.refs_0_), channel_id=1, source_target_pairs={{0,8},{8,0},{16,24},{24,16},{1,9},{9,1},{17,25},{25,17},{2,10},{10... | collective-permute-start | bytes 3538952 | tf_op jit(solution)/shard_map/ppermute | solution.py:911
  201.6 6.3 %collective-permute-start.34 = (bf16[2,4,192,384]{3,2,1,0:T(8,128)(2,1)S(1)}, bf16[2,4,192,384]{3,2,1,0:T(8,128)(2,1)S(1)}, u32[]{:S(2)}, u32[]{:S(2)}) collective-permute-start(bf16[2,4,192,384]{3,2,1,0:T(8,128)(2,1)S(1)} %get-tuple-element.165), channel_id=1, source_target_pairs={{0,8},{8,0},{16,24},{24,16},{1,9},{9,1},{17,25},{25,17},{2,10},{10... | collective-permute-start | bytes 3538952 | tf_op jit(solution)/shard_map/ppermute | solution.py:911
  201.7 8.1 %collective-permute-start.36 = (bf16[2,128,192]{2,1,0:T(8,128)(2,1)S(1)}, bf16[2,128,192]{2,1,0:T(8,128)(2,1)S(1)}, u32[]{:S(2)}, u32[]{:S(2)}) collective-permute-start(bf16[2,128,192]{2,1,0:T(8,128)(2,1)S(1)} %get-tuple-element.172), channel_id=1, source_target_pairs={{0,1},{1,0},{2,3},{3,2},{4,5},{5,4},{6,7},{7,6},{8,9},{9,8},{10,11... | collective-permute-start | bytes 294920 | tf_op jit(solution)/shard_map/ppermute | solution.py:919
  203.4 12.9 %collective-permute-start.37 = (bf16[2,128,192]{2,1,0:T(8,128)(2,1)S(1)}, bf16[2,128,192]{2,1,0:T(8,128)(2,1)S(1)}, u32[]{:S(2)}, u32[]{:S(2)}) collective-permute-start(bf16[2,128,192]{2,1,0:T(8,128)(2,1)S(1)} %get-tuple-element.173), channel_id=1, source_target_pairs={{0,2},{1,3},{2,0},{3,1},{4,6},{5,7},{6,4},{7,5},{8,10},{9,11},{10,... | collective-permute-start | bytes 294920 | tf_op jit(solution)/shard_map/ppermute | solution.py:919
  204.7 11.7 %collective-permute-start.38 = (bf16[2,128,192]{2,1,0:T(8,128)(2,1)S(1)}, bf16[2,128,192]{2,1,0:T(8,128)(2,1)S(1)}, u32[]{:S(2)}, u32[]{:S(2)}) collective-permute-start(bf16[2,128,192]{2,1,0:T(8,128)(2,1)S(1)} %get-tuple-element.174), channel_id=1, source_target_pairs={{0,3},{1,2},{2,1},{3,0},{4,7},{5,6},{6,5},{7,4},{8,11},{9,10},{10,... | collective-permute-start | bytes 294920 | tf_op jit(solution)/shard_map/ppermute | solution.py:919
  207.0 26.7 %collective-permute-start.32 = (bf16[4,192,384]{2,1,0:T(8,128)(2,1)S(1)}, bf16[4,192,384]{2,1,0:T(8,128)(2,1)S(1)}, u32[]{:S(2)}, u32[]{:S(2)}) collective-permute-start(bf16[4,192,384]{2,1,0:T(8,128)(2,1)S(1)} %fusion.4.refs_0_), channel_id=1, source_target_pairs={{0,16},{8,24},{16,0},{24,8},{1,17},{9,25},{17,1},{25,9},{2,18},{10... | collective-permute-start | bytes 1769480 | tf_op jit(solution)/shard_map/ppermute | solution.py:915
  208.1 26.4 %collective-permute-start.35 = (bf16[4,192,384]{2,1,0:T(8,128)(2,1)S(1)}, bf16[4,192,384]{2,1,0:T(8,128)(2,1)S(1)}, u32[]{:S(2)}, u32[]{:S(2)}) collective-permute-start(bf16[4,192,384]{2,1,0:T(8,128)(2,1)S(1)} %fusion.5.refs_1_), channel_id=1, source_target_pairs={{0,16},{8,24},{16,0},{24,8},{1,17},{9,25},{17,1},{25,9},{2,18},{10... | collective-permute-start | bytes 1769480 | tf_op jit(solution)/shard_map/ppermute | solution.py:915
  216.4 18.1 %copy-start.22 = (bf16[2,128,192]{2,1,0:T(8,128)(2,1)S(1)}, bf16[2,128,192]{2,1,0:T(8,128)(2,1)}, u32[]{:S(2)}) copy-start(bf16[2,128,192]{2,1,0:T(8,128)(2,1)} %copy-done.20) | copy-start | bytes 294916
  216.4 18.1 %copy-start.25 = (bf16[2,128,192]{2,1,0:T(8,128)(2,1)S(1)}, bf16[2,128,192]{2,1,0:T(8,128)(2,1)}, u32[]{:S(2)}) copy-start(bf16[2,128,192]{2,1,0:T(8,128)(2,1)} %copy-done.23) | copy-start | bytes 294916
  216.4 18.1 %copy-start.34 = (bf16[2,128,192]{2,1,0:T(8,128)(2,1)S(1)}, bf16[2,128,192]{2,1,0:T(8,128)(2,1)}, u32[]{:S(2)}) copy-start(bf16[2,128,192]{2,1,0:T(8,128)(2,1)} %copy-done.32) | copy-start | bytes 294916
  216.4 18.1 %copy-start.44 = (bf16[512,768]{1,0:T(8,128)(2,1)S(1)}, bf16[512,768]{1,0:T(8,128)(2,1)}, u32[]{:S(2)}) copy-start(bf16[512,768]{1,0:T(8,128)(2,1)} %copy-done.43) | copy-start | bytes 2359300
  231.0 17.0 %collective-permute-start.39 = (bf16[2,2,128,768]{3,2,1,0:T(8,128)(2,1)}, bf16[2,2,128,768]{3,2,1,0:T(8,128)(2,1)S(1)}, u32[]{:S(2)}, u32[]{:S(2)}) collective-permute-start(bf16[2,2,128,768]{3,2,1,0:T(8,128)(2,1)} %get-tuple-element.179.refs_0_), channel_id=1, source_target_pairs={{0,1},{1,0},{2,3},{3,2},{4,5},{5,4},{6,7},{7,6},{8,9},{9,8},{10,11... | collective-permute-start | bytes 2359304 | tf_op jit(solution)/shard_map/ppermute | solution.py:919
  239.9 10.8 %collective-permute-start.41 = (bf16[2,1360,192]{1,2,0:T(8,128)(2,1)}, bf16[2,1360,192]{1,2,0:T(8,128)(2,1)S(1)}, u32[]{:S(2)}, u32[]{:S(2)}) collective-permute-start(bf16[2,1360,192]{1,2,0:T(8,128)(2,1)} %copy.63), channel_id=1, source_target_pairs={{0,8},{8,0},{16,24},{24,16},{1,9},{9,1},{17,25},{25,17},{2,10},{10... | collective-permute-start | bytes 3133448 | tf_op jit(solution)/shard_map/ppermute | solution.py:911
  242.9 16.5 %collective-permute-start.50 = (f32[16,768]{1,0:T(8,128)S(1)}, f32[16,768]{1,0:T(8,128)S(1)}, u32[]{:S(2)}, u32[]{:S(2)}) collective-permute-start(f32[16,768]{1,0:T(8,128)S(1)} %copy-done.30), channel_id=1, source_target_pairs={{0,8},{8,0},{16,24},{24,16},{1,9},{9,1},{17,25},{25,17},{2,10},{10... | collective-permute-start | bytes 147464 | tf_op jit(solution)/shard_map/ppermute | solution.py:911
  248.9 15.2 %collective-permute-start.40 = (bf16[2,2,192,384]{3,2,1,0:T(8,128)(2,1)}, bf16[2,2,192,384]{3,2,1,0:T(8,128)(2,1)}, u32[]{:S(2)}, u32[]{:S(2)}) collective-permute-start(bf16[2,2,192,384]{3,2,1,0:T(8,128)(2,1)} %pad_maximum_fusion.4), channel_id=1, source_target_pairs={{0,1},{1,0},{2,3},{3,2},{4,5},{5,4},{6,7},{7,6},{8,9},{9,8},{10,11... | collective-permute-start | bytes 1769480 | tf_op jit(solution)/shard_map/ppermute | solution.py:919
  258.3 15.0 %collective-permute-start.42 = (bf16[1360,192]{0,1:T(8,128)(2,1)}, bf16[1360,192]{0,1:T(8,128)(2,1)}, u32[]{:S(2)}, u32[]{:S(2)}) collective-permute-start(bf16[1360,192]{0,1:T(8,128)(2,1)} %copy.66), channel_id=1, source_target_pairs={{0,16},{8,24},{16,0},{24,8},{1,17},{9,25},{17,1},{25,9},{2,18},{10... | collective-permute-start | bytes 1566728 | tf_op jit(solution)/shard_map/ppermute | solution.py:915
  259.4 4.2 %collective-permute-start.51 = (f32[16,768]{1,0:T(8,128)S(1)}, f32[16,768]{1,0:T(8,128)S(1)}, u32[]{:S(2)}, u32[]{:S(2)}) collective-permute-start(f32[16,768]{1,0:T(8,128)S(1)} %add.144), channel_id=1, source_target_pairs={{0,4},{4,0},{1,5},{5,1},{2,6},{6,2},{3,7},{7,3},{8,12},{12,8},{9,1... | collective-permute-start | bytes 147464 | tf_op jit(solution)/shard_map/ppermute | solution.py:907
  261.3 21.0 %collective-permute-start.43 = (bf16[2,128,768]{2,1,0:T(8,128)(2,1)}, bf16[2,128,768]{2,1,0:T(8,128)(2,1)}, u32[]{:S(2)}, u32[]{:S(2)}) collective-permute-start(bf16[2,128,768]{2,1,0:T(8,128)(2,1)} %fusion.14), channel_id=1, source_target_pairs={{0,2},{1,3},{2,0},{3,1},{4,6},{5,7},{6,4},{7,5},{8,10},{9,11},{10,... | collective-permute-start | bytes 1179656 | tf_op jit(solution)/shard_map/ppermute | solution.py:919
  268.7 8.6 %collective-permute-start.52 = (f32[16,768]{1,0:T(8,128)}, f32[16,768]{1,0:T(8,128)}, u32[]{:S(2)}, u32[]{:S(2)}) collective-permute-start(f32[16,768]{1,0:T(8,128)} %add.145), channel_id=1, source_target_pairs={{0,16},{8,24},{16,0},{24,8},{1,17},{9,25},{17,1},{25,9},{2,18},{10... | collective-permute-start | bytes 147464 | tf_op jit(solution)/shard_map/ppermute | solution.py:915
  277.1 14.5 %collective-permute-start.45 = (bf16[2,192,192]{2,1,0:T(8,128)(2,1)S(1)}, bf16[2,192,192]{2,1,0:T(8,128)(2,1)S(1)}, u32[]{:S(2)}, u32[]{:S(2)}) collective-permute-start(bf16[2,192,192]{2,1,0:T(8,128)(2,1)S(1)} %pad_maximum_fusion.9), channel_id=1, source_target_pairs={{0,1},{1,0},{2,3},{3,2},{4,5},{5,4},{6,7},{7,6},{8,9},{9,8},{10,11... | collective-permute-start | bytes 442376 | tf_op jit(solution)/shard_map/ppermute | solution.py:919
  278.6 12.9 %collective-permute-start.53 = (f32[16,768]{1,0:T(8,128)S(1)}, f32[16,768]{1,0:T(8,128)S(1)}, u32[]{:S(2)}, u32[]{:S(2)}) collective-permute-start(f32[16,768]{1,0:T(8,128)S(1)} %add.146), channel_id=1, source_target_pairs={{0,1},{1,0},{2,3},{3,2},{4,5},{5,4},{6,7},{7,6},{8,9},{9,8},{10,11... | collective-permute-start | bytes 147464 | tf_op jit(solution)/shard_map/ppermute | solution.py:919
  281.4 20.1 %collective-permute-start.48 = (bf16[2,192,384]{2,1,0:T(8,128)(2,1)S(1)}, bf16[2,192,384]{2,1,0:T(8,128)(2,1)S(1)}, u32[]{:S(2)}, u32[]{:S(2)}) collective-permute-start(bf16[2,192,384]{2,1,0:T(8,128)(2,1)S(1)} %pad_maximum_fusion.8.refs_0_), channel_id=1, source_target_pairs={{0,2},{1,3},{2,0},{3,1},{4,6},{5,7},{6,4},{7,5},{8,10},{9,11},{10,... | collective-permute-start | bytes 884744 | tf_op jit(solution)/shard_map/ppermute | solution.py:919
  283.6 13.0 %collective-permute-start.44 = (bf16[128,768]{1,0:T(8,128)(2,1)S(1)}, bf16[128,768]{1,0:T(8,128)(2,1)S(1)}, u32[]{:S(2)}, u32[]{:S(2)}) collective-permute-start(bf16[128,768]{1,0:T(8,128)(2,1)S(1)} %get-tuple-element.192), channel_id=1, source_target_pairs={{0,4},{4,0},{1,5},{5,1},{2,6},{6,2},{3,7},{7,3},{8,12},{12,8},{9,1... | collective-permute-start | bytes 589832 | tf_op jit(solution)/shard_map/ppermute | solution.py:907
  291.6 9.8 %collective-permute-start.46 = (bf16[192,192]{1,0:T(8,128)(2,1)S(1)}, bf16[192,192]{1,0:T(8,128)(2,1)S(1)}, u32[]{:S(2)}, u32[]{:S(2)}) collective-permute-start(bf16[192,192]{1,0:T(8,128)(2,1)S(1)} %fusion.19), channel_id=1, source_target_pairs={{0,2},{1,3},{2,0},{3,1},{4,6},{5,7},{6,4},{7,5},{8,10},{9,11},{10,... | collective-permute-start | bytes 221192 | tf_op jit(solution)/shard_map/ppermute | solution.py:919
  301.6 5.1 %collective-permute-start.54 = (f32[16,768]{1,0:T(8,128)S(1)}, f32[16,768]{1,0:T(8,128)S(1)}, u32[]{:S(2)}, u32[]{:S(2)}) collective-permute-start(f32[16,768]{1,0:T(8,128)S(1)} %add.147), channel_id=1, source_target_pairs={{0,2},{1,3},{2,0},{3,1},{4,6},{5,7},{6,4},{7,5},{8,10},{9,11},{10,... | collective-permute-start | bytes 147464 | tf_op jit(solution)/shard_map/ppermute | solution.py:919
  301.7 13.0 %collective-permute-start.47 = (bf16[784,192]{1,0:T(8,128)(2,1)S(1)}, bf16[784,192]{1,0:T(8,128)(2,1)S(1)}, u32[]{:S(2)}, u32[]{:S(2)}) collective-permute-start(bf16[784,192]{1,0:T(8,128)(2,1)S(1)} %pad_maximum_fusion.5), channel_id=1, source_target_pairs={{0,4},{4,0},{1,5},{5,1},{2,6},{6,2},{3,7},{7,3},{8,12},{12,8},{9,1... | collective-permute-start | bytes 903176 | tf_op jit(solution)/shard_map/ppermute | solution.py:907
  301.8 16.9 %collective-permute-start.49 = (bf16[2,192,384]{2,1,0:T(8,128)(2,1)S(1)}, bf16[2,192,384]{2,1,0:T(8,128)(2,1)S(1)}, u32[]{:S(2)}, u32[]{:S(2)}) collective-permute-start(bf16[2,192,384]{2,1,0:T(8,128)(2,1)S(1)} %fusion.10), channel_id=1, source_target_pairs={{0,4},{4,0},{1,5},{5,1},{2,6},{6,2},{3,7},{7,3},{8,12},{12,8},{9,1... | collective-permute-start | bytes 884744 | tf_op jit(solution)/shard_map/ppermute | solution.py:907
  (90 other events, 490.3 us)

commit v3 on v2

--- a/solution.py
+++ b/solution.py
@@ -82,6 +82,8 @@
 def vmem_room(inputs, outs, scratch):
     total = 0
     for array in (*inputs, *jax.tree.leaves(outs), *scratch):
+        if not jnp.issubdtype(array.dtype, jnp.number):
+            continue
         *lead, rows, lanes = (1, 1, *array.shape)
         size = jnp.dtype(array.dtype).itemsize
         tile = 8 * (4 // size)
@@ -89,7 +91,7 @@
     return min(total + ROOM, 60 * 2**20)
 
 
-def call_kernel(kernel, place, inputs, outs, scratch=(), flops=0, moved=0, exps=0):
+def call_kernel(kernel, place, inputs, outs, scratch=(), flops=0, moved=0, exps=0, from_hbm=False):
     place, after = place if isinstance(place, tuple) else (place, ())
 
     def body(place_ref, *refs):
@@ -100,7 +102,7 @@
         out_shape=outs,
         in_specs=[pl.BlockSpec(memory_space=pltpu.SMEM)]
         + [pl.BlockSpec(memory_space=pl.ANY)] * len(after)
-        + vmem_specs(len(inputs)),
+        + ([pl.BlockSpec(memory_space=pltpu.HBM)] * len(inputs) if from_hbm else vmem_specs(len(inputs))),
         out_specs=jax.tree.map(lambda _: pl.BlockSpec(memory_space=pltpu.VMEM), outs),
         scratch_shapes=list(scratch),
         compiler_params=pltpu.CompilerParams(vmem_limit_bytes=vmem_room(inputs, outs, scratch)),
@@ -137,11 +139,11 @@
 
 
 def place_projections(place_ref, pieces, target, first):
-    size = pieces[0].shape[1]
+    size, cols = pieces[0].shape[1], target.shape[2]
     for kind in range(3):
         for distance, piece in zip((0, 2, 1, 3), pieces):
             start = pl.multiple_of((place_ref[0] ^ distance) * size, 64)
-            target[kind, pl.ds(start, size), :] = piece[kind + first]
+            target[kind, pl.ds(start, size), :] = piece[kind, :, first : first + cols]
 
 
 def project_kernel(place_ref, own_ref, w0, w2, w1, w3, bias_ref, clip_in_ref, full_ref, a_ref, q_ref, token_ref):
@@ -168,7 +170,7 @@
 
 def project_own(place, own, pieces, bias, clip_in):
     half, width = own.shape
-    cols = pieces[0].shape[-1]
+    cols = pieces[0].shape[-1] // 2
     heads = cols // HEAD_DIM
     bf16 = jnp.bfloat16
     return call_kernel(
@@ -267,7 +269,7 @@
         a_ref[...] = inputs
         rows_ref[...] = other_ref[0 : half // 4, :]
     else:
-        place_projections(place_ref, pieces, w_ref, 3)
+        place_projections(place_ref, pieces, w_ref, w_ref.shape[2])
         write_heads(own_ref[...], w_ref, bias_ref, qkv_ref, 0)
     write_heads(inputs, w_ref, bias_ref, qkv_ref, half)
     eye = unit_matrix()
@@ -313,14 +315,14 @@
         if student:
             merged = clip_ref[...] * jnp.tanh(merged / clip_ref[...])
         merged = merged.astype(bf16)
-        part = query >> 1
         share = size // 2
-        for pair in range(2):
-
-            @pl.when((query & 1) == pair)
+        for at in range(blocks):
+
+            @pl.when(query == at)
             def _():
-                c_refs[2 * pair][part] = merged[:share]
-                c_refs[2 * pair + 1][part] = merged[share:]
+                lanes = slice((at >> 1) * cols, ((at >> 1) + 1) * cols)
+                c_refs[2 * (at & 1)][:, lanes] = merged[:share]
+                c_refs[2 * (at & 1) + 1][:, lanes] = merged[share:]
 
         return carry
 
@@ -330,12 +332,12 @@
 def attention_forward(student, place, other, weights, parts, bias, clip_in, clip, code_col, code_row):
     width = other.shape[1]
     half = parts.shape[2] if student else parts.shape[0]
-    cols = weights[0].shape[-1]
+    cols = clip.shape[-1]
     heads = cols // HEAD_DIM
     count = 2 * half
     bf16, f32 = jnp.bfloat16, jnp.float32
     qkv = (3, heads, count, HEAD_DIM)
-    c_shape = (shaped((2, half // 4, cols), bf16),) * 4
+    c_shape = (shaped((half // 4, 2 * cols), bf16),) * 4
     scratch = (
         pltpu.VMEM((heads, HEAD_DIM, count), bf16),
         pltpu.VMEM((count // QUERY_BLOCK, QUERY_BLOCK, QUERY_BLOCK), f32),
@@ -408,7 +410,7 @@
             merged = merged_ref[:, at : at + share]
             wide = jnp.concatenate([merged, jnp.zeros((256 - cols, share), f32)], axis=0)
             ratio = jnp.tanh(jnp.transpose(wide)[:, :cols] / clip_ref[...])
-            grad = (source[part].astype(f32) * (1.0 - ratio * ratio)).astype(bf16)
+            grad = (source[:, part * cols : (part + 1) * cols].astype(f32) * (1.0 - ratio * ratio)).astype(bf16)
             for head in range(heads):
                 grad_ref[head, at : at + share, :] = grad[:, head * HEAD_DIM : (head + 1) * HEAD_DIM]
             wide = jnp.concatenate(
@@ -522,15 +524,16 @@
 def out_norm_kernel(student, place_ref, *refs):
     if student:
         c_refs, pieces = refs[:4], refs[4:12]
-        own_ref, other_ref, valid_ref, params_ref = refs[12:16]
-        w_ref, unit_ref, scale_ref, low_ref, sums_ref, token_ref = refs[16:]
+        own_ref, other_ref, valid_ref, params_ref, cot_ref = refs[12:17]
+        w_ref, unit_ref, scale_ref, low_ref, sums_ref, token_ref = refs[17:]
         token_ref[...] = jnp.zeros_like(token_ref)
     else:
         c_refs, w_ref = refs[:4], refs[4]
-        own_ref, other_ref, valid_ref, params_ref, cot_ref = refs[5:10]
-        wide_ref, low_ref = refs[10:]
+        own_ref, other_ref, valid_ref, params_ref = refs[5:9]
+        wide_ref, low_ref, token_ref = refs[9:]
+        token_ref[...] = jnp.zeros_like(token_ref)
     share = own_ref.shape[0]
-    cols = c_refs[0].shape[2]
+    cols = c_refs[0].shape[1] // 2
     size = w_ref.shape[1] // 4
     total = None
     for r, source in enumerate(c_refs):
@@ -542,7 +545,7 @@
             weights = w_ref[r, :, 0:cols]
         else:
             weights = w_ref[r, :, cols : 2 * cols]
-        context = jnp.concatenate([source[0], source[1]], axis=0)
+        context = jnp.concatenate([source[:, 0:cols], source[:, cols:]], axis=0)
         term = dot_nt(context, weights)
         total = term if total is None else total + term
     attn = total + params_ref[0:1, :]
@@ -551,6 +554,7 @@
     wide = unit * params_ref[2:3, :] + params_ref[3:4, :]
     low_ref[0 : 2 * share, :] = wide.astype(jnp.bfloat16)
     if student:
+        low_ref[2 * share :, :] = cot_ref[...]
         unit_ref[...] = unit
         scale_ref[...] = scale
         valid = valid_ref[...]
@@ -559,25 +563,24 @@
         sums_ref[2:3, :] = column_sum(valid * attn * attn)
     else:
         wide_ref[...] = wide
-        low_ref[2 * share :, :] = cot_ref[...]
 
 
 def out_norm(student, place, contexts, weights, own, other, valid, params, cot=()):
     share, width = own.shape
     rows = 2 * share
-    cols = contexts[0].shape[-1]
+    cols = contexts[0].shape[-1] // 2
     f32, bf16 = jnp.float32, jnp.bfloat16
     if student:
         outs = (
             shaped((4, width, 2 * cols), bf16),
             shaped((rows, width), f32),
             shaped((rows, 1), f32),
-            shaped((rows, width), bf16),
+            shaped((rows + share, width), bf16),
             shaped((3, width), f32),
             shaped(TOKEN, f32),
         )
     else:
-        outs = (shaped((rows, width), f32), shaped((rows + share, width), bf16))
+        outs = (shaped((rows, width), f32), shaped((rows, width), bf16), shaped(TOKEN, f32))
     return call_kernel(
         functools.partial(out_norm_kernel, student),
         place,
@@ -664,7 +667,7 @@
 
 def loss_kernel(
     place_ref, unit_ref, ffn_ref, got_ref, ht_ref, ffnt_ref, gott_ref, cot_ref, cot_other_ref, valid_ref, params_ref, t_ref,
-    layer_ref, dz_ref, low_ref, sums_ref,
+    layer_ref, layer_other_ref, dz_ref, low_ref, sums_ref,
 ):
     share = cot_ref.shape[0]
     rows = 2 * share
@@ -675,7 +678,7 @@
     out = unit * params_ref[4:5, :] + params_ref[5:6, :]
     low = out.astype(bf16)
     layer_ref[...] = low[:share]
-    low_ref[rows:, :] = low[share:]
+    layer_other_ref[...] = low[share:]
     t_unit, _ = unit_of(ht_ref[...] + ffnt_ref[...] + gott_ref[...].astype(f32) + t_ref[1:2, :])
     difference = out - (t_unit * t_ref[4:5, :] + t_ref[5:6, :])
     valid = valid_ref[...]
@@ -690,7 +693,7 @@
     )
     dz_ref[...] = dz
     dz_low = dz.astype(bf16)
-    low_ref[0:rows, :] = dz_low
+    low_ref[...] = dz_low
     sums_ref[0:1, :] = column_sum(dz_low.astype(f32))
     sums_ref[1:2, :] = column_sum(grad * unit)
     sums_ref[2:3, :] = column_sum(grad)
@@ -708,8 +711,9 @@
         (unit, ffn, got, ht, ffnt, gott, cot, cot_other, valid, params, t_rows),
         (
             shaped((share, width), bf16),
+            shaped((share, width), bf16),
             shaped((rows, width), f32),
-            shaped((rows + share, width), bf16),
+            shaped((rows, width), bf16),
             shaped((5, width), f32),
         ),
         flops=60 * rows * width,
@@ -788,11 +792,11 @@
     sums_ref[0:1, :] = column_sum(low.astype(f32))
     sums_ref[1:2, :] = column_sum(grad * unit)
     sums_ref[2:3, :] = column_sum(grad)
-    share, cols = ctx_refs[0].shape[1:]
+    share, cols = ctx_refs[0].shape[0], ctx_refs[0].shape[1] // 2
     for r in range(4):
         back = dot_nn(low, w_ref[r, :, 0:cols]).astype(bf16)
-        ctx_refs[r][0] = back[:share]
-        ctx_refs[r][1] = back[share:]
+        ctx_refs[r][:, 0:cols] = back[:share]
+        ctx_refs[r][:, cols:] = back[share:]
 
 
 def first_pull(place, dz, part, got, unit, scale, params, weights):
@@ -807,7 +811,7 @@
             shaped((rows, width), f32),
             shaped((rows, width), bf16),
             shaped((3, width), f32),
-            *(shaped((2, rows // 2, cols), bf16),) * 4,
+            *(shaped((rows // 2, 2 * cols), bf16),) * 4,
         ),
         flops=2 * rows * width * cols * 4,
         moved=20 * rows * width,
@@ -815,14 +819,16 @@
 
 
 def last_grads_kernel(place_ref, low_ref, c0, c1, c2, c3, a_ref, a_other_ref, d_ref, qv_ref, keep_ref, send_ref, full_ref):
-    size = full_ref.shape[0] // 4
+    size, cols = full_ref.shape[0] // 4, full_ref.shape[1]
     half = a_ref.shape[0]
     low = jnp.transpose(low_ref[...])
     own, other = jnp.transpose(a_ref[...]), jnp.transpose(a_other_ref[...])
-    for entry in range(7):
+    spots = ((0, 0), (1, 0), (0, 1), (1, 1), (2, 0), (2, 1), (3, 0))
+    for entry, (block, side) in enumerate(spots):
         if entry < 4:
             source = (c0, c1, c2, c3)[entry]
-            full_ref[...] = dot_nn(low, jnp.concatenate([source[0], source[1]], axis=0))
+            context = jnp.concatenate([source[:, 0:cols], source[:, cols:]], axis=0)
+            full_ref[...] = dot_nn(low, context)
         else:
             full_ref[...] = dot_nn(own, d_ref[entry - 4, 0:half, :]) + dot_nn(
                 other, d_ref[entry - 4, half:, :]
@@ -830,20 +836,23 @@
         for slot in range(2):
             for target, distance in ((keep_ref, 2 * slot), (send_ref, 2 * slot + 1)):
                 start = pl.multiple_of((place_ref[0] ^ distance) * size, 64)
-                target[slot, entry * size : (entry + 1) * size, :] = full_ref[
-                    pl.ds(start, size), :
-                ].astype(jnp.bfloat16)
-    sums = jnp.concatenate([qv_ref[...], jnp.zeros((14, qv_ref.shape[1]), jnp.float32)], axis=0)
+                target[slot, block * size : (block + 1) * size, side * cols : (side + 1) * cols] = (
+                    full_ref[pl.ds(start, size), :].astype(jnp.bfloat16)
+                )
+    sums = jnp.concatenate([qv_ref[...], jnp.zeros((14, cols), jnp.float32)], axis=0)
+    sums = jnp.concatenate([sums, jnp.zeros((16, cols), jnp.float32)], axis=1)
+    nothing = jnp.zeros((size, cols), jnp.bfloat16)
     for slot in range(2):
         for target in (keep_ref, send_ref):
-            target[slot, 7 * size :, :] = sums.astype(jnp.bfloat16)
+            target[slot, 3 * size : 4 * size, cols:] = nothing
+            target[slot, 4 * size :, :] = sums.astype(jnp.bfloat16)
 
 
 def last_grads(place, low, contexts, a_in, d_proj, d_bias_qv):
     rows, width = low.shape
     count = d_proj.shape[1]
     cols = d_proj.shape[-1]
-    out = shaped((2, 7 * (width // 4) + 16, cols), jnp.bfloat16)
+    out = shaped((2, 4 * (width // 4) + 16, 2 * cols), jnp.bfloat16)
     return call_kernel(
         last_grads_kernel,
         place,
@@ -900,6 +909,61 @@
         shaped((16, width), jnp.float32),
         flops=1,
         moved=1,
+    )
+
+
+def sign_of(value):
+    return jnp.where(value > 0.0, 1.0, jnp.where(value < 0.0, -1.0, 0.0))
+
+
+def piece_kernel(place_ref, *refs):
+    sources, (piece_ref, teacher_ref), copies, sems = refs[:11], refs[11:13], refs[13:24], refs[24]
+    moves = [
+        pltpu.make_async_copy(source, target, sems.at[at])
+        for at, (source, target) in enumerate(zip(sources, copies))
+    ]
+    for move in moves:
+        move.start()
+    for move in moves:
+        move.wait()
+    up_ref, down_ref, out_ref, t_out_ref, t_up_ref, t_down_ref, quant_ref, columns_ref, *rows = copies
+    bf16, f32 = jnp.bfloat16, jnp.float32
+    size, half = up_ref.shape[0], piece_ref.shape[1]
+    lanes = pl.ds(pl.multiple_of(place_ref[2] * half, 128), half)
+    quant = quant_ref[:, lanes]
+    up = quant[1:2] * sign_of(up_ref[:, lanes] - quant[0:1])
+    piece_ref[0:size, :] = up.astype(bf16)
+    columns = columns_ref[...]
+    down = columns[:, 3:4] * sign_of(down_ref[:, lanes] - columns[:, 2:3])
+    piece_ref[size : 2 * size, :] = down.astype(bf16)
+    out = columns[:, 1:2] * sign_of(out_ref[...] - columns[:, 0:1])
+    piece_ref[2 * size : 3 * size, :] = jnp.concatenate([out.astype(bf16), t_out_ref[...]], axis=1)
+    terms = []
+    for row in rows:
+        rest = row[:, lanes]
+        for _ in range(3):
+            term = rest.astype(bf16).astype(f32)
+            terms.append(term)
+            rest = rest - term
+    terms = jnp.concatenate(terms + [jnp.zeros((7, half), f32)], axis=0)
+    piece_ref[3 * size :, :] = terms.astype(bf16)
+    teacher_ref[0:size, :] = t_up_ref[:, lanes]
+    teacher_ref[size:, :] = t_down_ref[:, lanes]
+
+
+def own_pieces(place, *sources):
+    size, wide = sources[0].shape
+    bf16 = jnp.bfloat16
+    return call_kernel(
+        piece_kernel,
+        place,
+        sources,
+        (shaped((3 * size + 16, wide // 2), bf16), shaped((2 * size, wide // 2), bf16)),
+        tuple(pltpu.VMEM(source.shape, source.dtype) for source in sources)
+        + (pltpu.SemaphoreType.DMA((len(sources),)),),
+        flops=1,
+        moved=1,
+        from_hbm=True,
     )
 
 
@@ -1034,13 +1098,15 @@
     bin_qkv = jnp.transpose(
         binarize(latent_qkv_then, qkv_quant[0][None], qkv_quant[1][None]), (1, 0, 2)
     )
-    qkv_piece = jnp.concatenate([bin_qkv, jnp.transpose(t_qkv, (1, 0, 2))], axis=0)
+    qkv_piece = jnp.concatenate([bin_qkv, jnp.transpose(t_qkv, (1, 0, 2))], axis=2)
     qkv_pieces = fsdp_pieces(qkv_piece)
     t_up, t_down = tie((t_up, t_down), qkv_piece)
     teacher_piece = jnp.concatenate([half_of(t_up), half_of(t_down)], axis=0)
     clip_in_row, clip_row = clip_in[None], clip_ctx[None]
 
-    full_qkv, a_own, qkv_own, token = project_own(place, own, qkv_pieces, bias_qv, clip_in_row)
+    own_rows = own[:share]
+    cot_own, cot_sent = mine(cotangent, 1), theirs(cotangent, 1)
+    full_qkv, a_own, qkv_own, token = project_own(once(place, own_rows, cot_own, cot_sent), own, qkv_pieces, bias_qv, clip_in_row)
     other = tie(other, token)
     code_all = jnp.concatenate(
         [mine(code, 2).reshape(local_len), other[local_len, :local_len].astype(jnp.int32)]
@@ -1070,28 +1136,27 @@
         even, even_row, *even_cores,
         odd, odd_row, swap_core(odd), swap_core(odd_row),
     )
-    own_rows = own[:share]
     out_full, unit, scale, h_low, first_sums, token = out_norm(
-        True, once(place, token), contexts, pieces, own_rows, other_rows, valid, row_params
+        True, once(place, token), contexts, pieces, own_rows, other_rows, valid, row_params,
+        (cot_sent,),
     )
     h_far = swap_ctx(h_low)
-    teacher_contexts = exchange_tp(teacher_context)
+    teacher_contexts = exchange_tp([teacher_context[0], *tie(teacher_context[1:], token)])
     hidden_full, terms, hid_own, slope_own, part_own, _ = hidden_layer(
         True, False, once(place, token), h_low, rows, pieces
     )
-    teacher_even = jnp.stack([teacher_piece, tie(teacher_two, terms)])
+    teacher_even = jnp.stack([teacher_piece, tie(teacher_two, terms, *teacher_contexts[1:])])
     teacher_odd, teacher_even_row = swap_tp(teacher_even, 1), swap_row(teacher_even)
-    cot_own = mine(cotangent, 1)
-    h_teacher, ht_low = out_norm(
+    h_teacher, ht_low, token = out_norm(
         False, once(place, part_own), teacher_contexts, out_full, own_rows, other_rows, valid, t_rows,
-        (theirs(cotangent, 1),),
     )
     ht_far = swap_ctx(ht_low)
     hid_far, slope_far, part_far, token = hidden_layer(
-        True, True, once(place, ht_low), h_far, rows, hidden_full, terms
+        True, True, once(place, token), h_far, rows, hidden_full, terms
     )
     part_got = swap_ctx(part_far)
-    teacher_even_row, teacher_odd = tie((teacher_even_row, teacher_odd), token)
+    teacher_odd = tie(teacher_odd, token)
+    teacher_even_row = tie(teacher_even_row, token, ht_far)
     teacher_odd_row = swap_row(teacher_odd)
     teacher_hidden = (
         teacher_even, teacher_even_row, swap_core(teacher_even), swap_core(teacher_even_row),
@@ -1104,9 +1169,9 @@
     t_part_own, _ = hidden_layer(
         False, False, once(place, t_part_far), ht_low, rows, teacher_full, terms
     )
-    layer_own, d_second, d_ffn, second_sums = loss_step(
+    layer_own, layer_other, d_second, d_ffn, second_sums = loss_step(
         place, unit, part_own, part_got, h_teacher, t_part_own, t_part_got,
-        cot_own, ht_far, valid, row_params, t_rows,
+        cot_own, h_far, valid, row_params, t_rows,
     )
 
     def home(own_part, other_part):
@@ -1116,7 +1181,6 @@
         return jnp.stack([first, second], axis=1)
 
     d_ffn_far = swap_ctx(d_ffn)
-    layer_out = home(layer_own, d_ffn_far[rows:])
     du_own, d_part_own, du_sums_own = hidden_pull(False, place, d_ffn, hidden_full, slope_own)
     du_far, d_part_far, du_sums_far = hidden_pull(True, place, d_ffn_far, hidden_full, slope_far)
     d_part_got = swap_ctx(d_part_far)
@@ -1138,6 +1202,7 @@
         qkv, clip_row, merged, lse, code_col, code_row, d_contexts, full_qkv,
     )
     got_back = swap_tp(send_back, 1)
+    layer_out = home(layer_own, swap_ctx(tie(layer_other, d_bias_qv)))
     got_down_row, got_up_row = tie((swap_row(leave_down), swap_row(leave_up)), d_bias_qv)
     row_down = add(add(keep_down[0], got_down[0]), got_down_row)
     row_up = add(add(keep_up[0], got_up[0]), got_up_row)
@@ -1159,10 +1224,10 @@
     vector_got = swap_row(vector)
     entry = row_width
     row_last = add(add(keep_last[0], got_last[0]), got_last_row)
-    send_one = jnp.stack([row_last[entry : 2 * entry], row_last[3 * entry : 4 * entry]]).astype(bf16)
+    send_one = row_last[entry : 2 * entry].astype(bf16)
     got_one = swap_tp(send_one, 1)
     leave_both = tie(
-        jnp.stack([add(row_down[2], got_both[0, 1]), add(row_up[2], got_both[1, 1])]).astype(bf16), send_one
+        jnp.stack([add(row_down[2], got_both[0, 1]), add(row_up[2], got_both[1, 1])]).astype(bf16), send_one, got_back_two
     )
     got_both_two = swap_tp(leave_both, 2)
     vector = tie(vector + vector_got, leave_both)
@@ -1171,13 +1236,21 @@
         once(place, leave_both), d_first, (keep_back, got_back, got_back_two), own_rows, other_rows, clip_in_row
     )
     input_grad = home(input_own, swap_ctx(input_other))
-    leave_two = add(row_last[2 * entry : 3 * entry], got_one[1]).astype(bf16)
+    out_two = add(row_last[0:entry], got_one)
+    leave_two = out_two[:, col_width:].astype(bf16)
     got_two = swap_tp(leave_two, 2)
     low_both = add(
         jnp.stack([add(row_down[0], got_both[0, 0]), add(row_up[0], got_both[1, 0])]), got_both_two
     ).astype(bf16)
-    low_out = add(add(row_last[0:entry], got_one[0]), got_two)
-    low_last = jnp.concatenate([low_out, row_last[4 * entry :]], axis=0).astype(bf16)
+    low_out = add(out_two[:, :col_width], got_two)
+    low_last = jnp.concatenate(
+        [
+            row_last[2 * entry : 3 * entry],
+            jnp.concatenate([row_last[3 * entry : 4 * entry, :col_width], low_out], axis=1),
+            row_last[4 * entry :],
+        ],
+        axis=0,
+    ).astype(bf16)
     sum_last = add(low_last, swap_ctx(low_last))
     vector = tie(vector + vector_got, low_both)
     vector = vector + swap_tp(vector, 2)
@@ -1195,13 +1268,20 @@
         grad_both[0], latent_down, down_quant[0][:, None], down_quant[1][:, None]
     )
     grad_qkv = straight(
-        jnp.transpose(sum_last[entry : 4 * entry].reshape(3, row_width, col_width), (1, 0, 2)),
+        jnp.stack(
+            [
+                sum_last[:entry, :col_width],
+                sum_last[:entry, col_width:],
+                sum_last[entry : 2 * entry, :col_width],
+            ],
+            axis=1,
+        ),
         latent_qkv,
         qkv_quant[0][None],
         qkv_quant[1][None],
     )
-    grad_out = straight(sum_last[0:entry], latent_out, out_quant[0][:, None], out_quant[1][:, None])
-    grad_qv = sum_last[4 * entry : 4 * entry + 2]
+    grad_out = straight(sum_last[entry : 2 * entry, col_width:], latent_out, out_quant[0][:, None], out_quant[1][:, None])
+    grad_qv = sum_last[2 * entry : 2 * entry + 2, :col_width]
     vector_sums = jnp.concatenate([vector[0:1], vector[3:4], vector[1:3], vector[4:6]], axis=0)
     stat_sums = jnp.sum(vector[6:11], axis=-1)
     grad_rows = lax.dynamic_slice_in_dim(vector_sums, fsdp_rank * row_width, row_width, 1)

time: 326 us -> 312 us (0.957)
  local copies, waits for them, and re-layouts: 43.2 us -> 21.6 us
  starting transfers between devices: 60.8 us -> 79.3 us
  other arithmetic: 31.6 us -> 23.9 us
  waiting for transfers between devices: 104 us -> 99.9 us
    ppermute x9, starting transfers between devices: 16 us -> 30 us  [swap_row(): return lax.ppermute(value, 'fsdp', [(i, i ^ 2) for i in range(4)])]
    unnamed x205 -> x139, local copies, waits for them, and re-layouts: 26.5 us -> 13.1 us
    ppermute x9, waiting for transfers between devices: 27.3 us -> 21.6 us  [swap_row(): return lax.ppermute(value, 'fsdp', [(i, i ^ 2) for i in range(4)])]
    ppermute x21, starting transfers between devices: 27.9 us -> 33.5 us  [swap_tp(): return lax.ppermute(value, 'tp', [(i, i ^ distance) for i in range(4)])]
    ppermute x11 -> x12, waiting for transfers between devices: 39.3 us -> 35 us  [swap_ctx(): return lax.ppermute(value, 'ctx', [(0, 1), (1, 0)])]
    ppermute x21, waiting for transfers between devices: 36.9 us -> 40.7 us  [swap_tp(): return lax.ppermute(value, 'tp', [(i, i ^ distance) for i in range(4)])]
    another operation x6 -> x5, other arithmetic: 6.85 us -> 3.93 us
    ppermute x11 -> x12, starting transfers between devices: 15.2 us -> 14.5 us  [swap_ctx(): return lax.ppermute(value, 'ctx', [(0, 1), (1, 0)])]
  transfers between devices with their start and end apart: 55 -> 56, of which waited for: 24 -> 28; matrix products, arithmetic and copies ran while one was open for 14% -> 8% of each run, Pallas kernels for 22% -> 23%
where the time goes in v3:
time: 312 us; the launch traced here: 307 us
  waiting for transfers between devices  99.9 us (32%)
  starting transfers between devices  79.3 us (25%)
  Pallas kernels  75 us (24%)
  other arithmetic  23.9 us (8%)
  local copies, waits for them, and re-layouts  21.6 us (7%)
  between operations  7.46 us (2%)
    pallas_call x20, Pallas kernels, call_kernel(): pl.pallas_call(body, out_shape=outs, in_specs=[pl.BlockSpec(memory_space=...  75 us
    ppermute x21, waiting for transfers between devices, swap_tp(): return lax.ppermute(value, 'tp', [(i, i ^ distance) for i in range(4)])  40.7 us
    ppermute x12, waiting for transfers between devices, swap_ctx(): return lax.ppermute(value, 'ctx', [(0, 1), (1, 0)])  35 us
    ppermute x21, starting transfers between devices, swap_tp(): return lax.ppermute(value, 'tp', [(i, i ^ distance) for i in range(4)])  33.5 us
    ppermute x9, starting transfers between devices, swap_row(): return lax.ppermute(value, 'fsdp', [(i, i ^ 2) for i in range(4)])  30 us
    ppermute x9, waiting for transfers between devices, swap_row(): return lax.ppermute(value, 'fsdp', [(i, i ^ 2) for i in range(4)])  21.6 us
    ppermute x12, starting transfers between devices, swap_ctx(): return lax.ppermute(value, 'ctx', [(0, 1), (1, 0)])  14.5 us
    unnamed x139, local copies, waits for them, and re-layouts  13.1 us
  transfers between devices with their start and end apart: 56, of which 28 were waited for; matrix products, arithmetic and copies ran while one was open for 8% of the time, Pallas kernels for 23%

profile of v3, /device:TPU:0, one launch (start us, length us, event | category | flops | bytes accessed | tf_op | source)
XLA Modules:
  0.0 307.1 jit_solution(8808735580249003473)
XLA Ops:
  12.3 3.0 collective-permute-start.1
  15.3 2.6 collective-permute-start
  17.9 1.5 collective-permute-start.4
  20.4 5.0 %collective-permute-done.1.refs_5_.refs_10_ = bf16[3,192,384]{2,1,0:T(8,128)(2,1)S(1)} collective-permute-done((bf16[3,192,384]{2,1,0:T(8,128)(2,1)S(1)}, bf16[3,192,384]{2,1,0:T(8,128)(2,1)S(1)}, u32[]{:S(2)}, u32[]{:S(2)}) %collective-permute-start.1) | collective-permute-done | bytes 442400 | tf_op jit(solution)/shard_map/ppermute | solution.py:979
  27.3 1.5 shard_map.312
  30.8 7.4 %collective-permute-done = bf16[592,384]{1,0:T(8,128)(2,1)} collective-permute-done((bf16[592,384]{1,0:T(8,128)(2,1)}, bf16[592,384]{1,0:T(8,128)(2,1)}, u32[]{:S(2)}, u32[]{:S(2)}) %collective-permute-start) | collective-permute-done | bytes 454688 | tf_op jit(solution)/shard_map/ppermute | solution.py:983
  45.9 9.9 %shard_map.313 = (bf16[128,384]{1,0:T(8,128)(2,1)S(1)}, bf16[128,384]{1,0:T(8,128)(2,1)S(1)}, bf16[128,384]{1,0:T(8,128)(2,1)S(1)}, bf16[128,384]{1,0:T(8,128)(2...) custom-call(s32[3]{0:T(128)S(1)} %pad_add_fusion.2.place_ref, ...), custom_call_target="tpu_custom_call" | custom-call | flops 5033164800 | bytes 4718592 | tf_op jit(solution)/shard_map/pallas_call | solution.py:100
  55.9 4.6 %collective-permute-done.7.refs_6_.refs_3_ = bf16[2,592,384]{2,1,0:T(8,128)(2,1)} collective-permute-done((bf16[2,592,384]{2,1,0:T(8,128)(2,1)S(1)}, bf16[2,592,384]{2,1,0:T(8,128)(2,1)}, u32[]{:S(2)}, u32[]{:S(2)}) %collective-permute-start.7) | collective-permute-done | bytes 909344 | tf_op jit(solution)/shard_map/ppermute | solution.py:979
  60.7 1.5 collective-permute-start.12
  63.0 1.7 collective-permute-start.9
  64.8 3.4 %collective-permute-start.10 = (bf16[128,384]{1,0:T(8,128)(2,1)S(1)}, bf16[128,384]{1,0:T(8,128)(2,1)S(1)}, u32[]{:S(2)}, u32[]{:S(2)}) collective-permute-start(bf16[128,384]{1,0:T(8,128)(2,1)S(1)} %get-tuple-element.123), channel_id=1, source_target_pairs={{0,2},{1,3},{2,0},{3,1},{4,6},{5,7},{6,4},{7,5},{8,10},{9,11},{10,... | collective-permute-start | bytes 294920 | tf_op jit(solution)/shard_map/ppermute | solution.py:983
  68.2 10.2 %shard_map.314 = (bf16[128,384]{1,0:T(8,128)(2,1)S(1)}, bf16[128,384]{1,0:T(8,128)(2,1)S(1)}, bf16[128,384]{1,0:T(8,128)(2,1)S(1)}, bf16[128,384]{1,0:T(8,128)(2,1)S(1)}, f32[8,128]{1,0:T(8,128)S(1)}) custom-call(s32[3]{0:T(128)S(1)} %pad_add_fusion.2.place_ref, f32[8,1024]{1,0:T(8,128)S(1)} %get-tuple-element.119.refs_0_.refs_6_, ...), custom_call_target="tpu_custom_call" | custom-call | flops 5033164800 | bytes 4718592 | tf_op jit(solution)/shard_map/pallas_call | solution.py:100
  79.7 3.9 %collective-permute-done.12.refs_10_.refs_7_ = bf16[2,592,384]{2,1,0:T(8,128)(2,1)} collective-permute-done((bf16[2,592,384]{2,1,0:T(8,128)(2,1)}, bf16[2,592,384]{2,1,0:T(8,128)(2,1)}, u32[]{:S(2)}, u32[]{:S(2)}) %collective-permute-start.12) | collective-permute-done | bytes 909344 | tf_op jit(solution)/shard_map/ppermute | solution.py:979
  84.3 3.4 %collective-permute-start.21 = (bf16[384,384]{1,0:T(8,128)(2,1)}, bf16[384,384]{1,0:T(8,128)(2,1)S(1)}, u32[]{:S(2)}, u32[]{:S(2)}) collective-permute-start(bf16[384,384]{1,0:T(8,128)(2,1)} %pad_maximum_fusion.7), channel_id=1, source_target_pairs={{0,2},{1,3},{2,0},{3,1},{4,6},{5,7},{6,4},{7,5},{8,10},{9,11},{10,... | collective-permute-start | bytes 884744 | tf_op jit(solution)/shard_map/ppermute | solution.py:983
  89.0 3.8 %shard_map.316 = (bf16[4,768,384]{2,1,0:T(8,128)(2,1)S(1)}, f32[256,768]{1,0:T(8,128)S(1)}, f32[256,1]{1,0:T(8,128)S(1)}, bf16[384,768]{1,0:T(8,128)(2,1)S(1)}, ...) custom-call(s32[3]{0:T(128)S(1)} %pad_add_fusion.2.place_ref, f32[8,128]{1,0:T(8,128)S(1)} %shard_map.315.refs_0_, ...), custom_call_target="tpu_custom_call" | custom-call | flops 1207959552 | bytes 2359296 | tf_op jit(solution)/shard_map/pallas_call | solution.py:100
  92.8 1.8 collective-permute-start.15
  94.6 3.3 %collective-permute-start.16 = (bf16[128,384]{1,0:T(8,128)(2,1)S(1)}, bf16[128,384]{1,0:T(8,128)(2,1)S(1)}, u32[]{:S(2)}, u32[]{:S(2)}) collective-permute-start(bf16[128,384]{1,0:T(8,128)(2,1)S(1)} %copy-done.33), channel_id=1, source_target_pairs={{0,2},{1,3},{2,0},{3,1},{4,6},{5,7},{6,4},{7,5},{8,10},{9,11},{10,... | collective-permute-start | bytes 294920 | tf_op jit(solution)/shard_map/ppermute | solution.py:983
  97.9 1.6 collective-permute-start.18
  99.5 5.7 %shard_map.317 = (bf16[4,2,768,384]{3,2,1,0:T(8,128)(2,1)S(1)}, bf16[4,16,384]{2,1,0:T(8,128)(2,1)S(1)}, bf16[4,256,384]{2,1,0:T(8,128)(2,1)S(1)}, bf16[4,256,38...) custom-call(s32[3]{0:T(128)S(1)} %pad_add_fusion.2.place_ref, ...), custom_call_target="tpu_custom_call" | custom-call | flops 4831838208 | bytes 6291456 | tf_op jit(solution)/shard_map/pallas_call | solution.py:100
  106.3 2.1 collective-permute-done.16.refs_3_
  108.5 2.3 collective-permute-start.25
  110.8 1.5 collective-permute-start.22
  112.3 1.5 shard_map.318
  113.9 2.9 shard_map.319
  116.8 7.5 %collective-permute-done.25.refs_6_ = bf16[2,384,384]{2,1,0:T(8,128)(2,1)S(1)} collective-permute-done((bf16[2,384,384]{2,1,0:T(8,128)(2,1)S(1)}, bf16[2,384,384]{2,1,0:T(8,128)(2,1)S(1)}, u32[]{:S(2)}, u32[]{:S(2)}) %collective-permute-start.25) | collective-permute-done | bytes 589856 | tf_op jit(solution)/shard_map/ppermute | solution.py:983
  124.3 1.5 collective-permute-start.26
  125.8 1.5 collective-permute-start.20
  127.8 8.2 %collective-permute-done.20.refs_1_ = bf16[256,768]{1,0:T(8,128)(2,1)S(1)} collective-permute-done((bf16[256,768]{1,0:T(8,128)(2,1)S(1)}, bf16[256,768]{1,0:T(8,128)(2,1)S(1)}, u32[]{:S(2)}, u32[]{:S(2)}) %collective-permute-start.20) | collective-permute-done | bytes 393248 | tf_op jit(solution)/shard_map/ppermute | solution.py:971
  136.1 3.0 collective-permute-done.26.refs_7_
  139.0 1.5 collective-permute-start.19
  141.0 3.3 %shard_map.320 = (bf16[4,2,768,384]{3,2,1,0:T(8,128)(2,1)S(1)}, bf16[256,768]{1,0:T(8,128)(2,1)S(1)}, f32[8,128]{1,0:T(8,128)}) custom-call(s32[3]{0:T(128)S(1)} %pad_add_fusion.2.place_ref, f32[8,128]{1,0:T(8,128)S(1)} %get-tuple-element.149.refs_0_, bf16[256,768]{1,0:T(8,128)(2,1)S(1)} %collective-permute-done.20.refs_1_, ...), custom_call_target="tpu_custom_call" | custom-call | flops 4831838208 | bytes 6291456 | tf_op jit(solution)/shard_map/pallas_call | solution.py:100
  144.3 1.5 collective-permute-start.29
  145.8 2.9 shard_map.321
  148.8 2.2 collective-permute-done.19.refs_2_
  151.0 8.0 %collective-permute-done.29.refs_5_ = bf16[256,768]{1,0:T(8,128)(2,1)S(1)} collective-permute-done((bf16[256,768]{1,0:T(8,128)(2,1)S(1)}, bf16[256,768]{1,0:T(8,128)(2,1)S(1)}, u32[]{:S(2)}, u32[]{:S(2)}) %collective-permute-start.29) | collective-permute-done | bytes 393248 | tf_op jit(solution)/shard_map/ppermute | solution.py:971
  159.0 2.6 shard_map.322
  161.6 1.5 collective-permute-start.30
  163.1 2.4 shard_map.325
  165.5 6.8 %collective-permute-done.30.refs_0_.refs_2_ = bf16[256,768]{1,0:T(8,128)(2,1)S(1)} collective-permute-done((bf16[256,768]{1,0:T(8,128)(2,1)S(1)}, bf16[256,768]{1,0:T(8,128)(2,1)S(1)}, u32[]{:S(2)}, u32[]{:S(2)}) %collective-permute-start.30) | collective-permute-done | bytes 393248 | tf_op jit(solution)/shard_map/ppermute | solution.py:971
  172.3 2.4 shard_map.323
  174.8 1.6 collective-permute-start.32
  176.3 2.5 shard_map.324
  178.9 5.8 %collective-permute-done.32.refs_3_ = bf16[256,768]{1,0:T(8,128)(2,1)S(1)} collective-permute-done((bf16[256,768]{1,0:T(8,128)(2,1)S(1)}, bf16[256,768]{1,0:T(8,128)(2,1)S(1)}, u32[]{:S(2)}, u32[]{:S(2)}) %collective-permute-start.32) | collective-permute-done | bytes 393248 | tf_op jit(solution)/shard_map/ppermute | solution.py:971
  184.7 1.6 shard_map.326
  186.4 2.5 shard_map.327
  189.0 1.5 collective-permute-start.34
  190.5 2.5 collective-permute-start.35
  194.6 1.6 collective-permute-start.38
  196.9 4.3 %collective-permute-done.36.refs_12_ = bf16[128,384]{1,0:T(8,128)(2,1)S(1)} collective-permute-done((bf16[128,384]{1,0:T(8,128)(2,1)S(1)}, bf16[128,384]{1,0:T(8,128)(2,1)S(1)}, u32[]{:S(2)}, u32[]{:S(2)}) %collective-permute-start.36) | collective-permute-done | bytes 98336 | tf_op jit(solution)/shard_map/ppermute | solution.py:983
  201.3 14.4 %shard_map.329 = (bf16[2,2,128,768]{3,2,1,0:T(8,128)(2,1)S(1)}, bf16[2,2,128,768]{3,2,1,0:T(8,128)(2,1)S(1)}, bf16[3,1024,192]{2,1,0:T(8,128)(2,1)S(1)}, f32[2,192]{1,0:T(2,128)S(1)}) custom-call(s32[3]{0:T(128)S(1)} %pad_add_fusion.2.place_ref, bf16[4,192,384]{2,1,0:T(8,128)(2,1)S(1)} %fusion.4.refs_0_, bf16[4,192,384]{2,1,0:T(8,128)(2,1)S(1)} %fusion.5.refs_1_, ...), custom_call_target="tpu_custom_call" | custom-call | flops 11676942336 | bytes 6291456 | tf_op jit(solution)/shard_map/pallas_call | solution.py:100
  215.8 2.0 collective-permute-start.40
  217.8 4.6 %collective-permute-done.39.refs_2_ = bf16[4,192,384]{2,1,0:T(8,128)(2,1)S(1)} collective-permute-done((bf16[4,192,384]{2,1,0:T(8,128)(2,1)S(1)}, bf16[4,192,384]{2,1,0:T(8,128)(2,1)S(1)}, u32[]{:S(2)}, u32[]{:S(2)}) %collective-permute-start.39) | collective-permute-done | bytes 589856 | tf_op jit(solution)/shard_map/ppermute | solution.py:979
  222.5 2.8 shard_map.330
  228.8 4.9 %collective-permute-done.40.refs_3_ = bf16[2,2,128,768]{3,2,1,0:T(8,128)(2,1)S(1)} collective-permute-done((bf16[2,2,128,768]{3,2,1,0:T(8,128)(2,1)S(1)}, bf16[2,2,128,768]{3,2,1,0:T(8,128)(2,1)S(1)}, u32[]{:S(2)}, u32[]{:S(2)}) %collective-permute-start.40) | collective-permute-done | bytes 786464 | tf_op jit(solution)/shard_map/ppermute | solution.py:983
  234.5 1.7 collective-permute-start.41
  237.5 4.3 %collective-permute-start.43 = (bf16[784,384]{1,0:T(8,128)(2,1)}, bf16[784,384]{1,0:T(8,128)(2,1)}, u32[]{:S(2)}, u32[]{:S(2)}) collective-permute-start(bf16[784,384]{1,0:T(8,128)(2,1)} %fusion.3), channel_id=1, source_target_pairs={{0,16},{8,24},{16,0},{24,8},{1,17},{9,25},{17,1},{25,9},{2,18},{10... | collective-permute-start | bytes 1806344 | tf_op jit(solution)/shard_map/ppermute | solution.py:979
  244.6 2.2 collective-permute-start.44
  247.5 1.7 slice_add_fusion.1
  249.2 15.4 %collective-permute-start.53 = (f32[16,768]{1,0:T(8,128)S(1)}, f32[16,768]{1,0:T(8,128)S(1)}, u32[]{:S(2)}, u32[]{:S(2)}) collective-permute-start(f32[16,768]{1,0:T(8,128)S(1)} %add.141), channel_id=1, source_target_pairs={{0,16},{8,24},{16,0},{24,8},{1,17},{9,25},{17,1},{25,9},{2,18},{10... | collective-permute-start | bytes 147464 | tf_op jit(solution)/shard_map/ppermute | solution.py:979
  266.7 1.5 collective-permute-start.54
  273.6 3.6 %collective-permute-done.45 = bf16[128,768]{1,0:T(8,128)(2,1)S(1)} collective-permute-done((bf16[128,768]{1,0:T(8,128)(2,1)S(1)}, bf16[128,768]{1,0:T(8,128)(2,1)S(1)}, u32[]{:S(2)}, u32[]{:S(2)}) %collective-permute-start.45) | collective-permute-done | bytes 196640 | tf_op jit(solution)/shard_map/ppermute | solution.py:971
  278.8 9.7 %collective-permute-done.47 = bf16[192,192]{1,0:T(8,128)(2,1)S(1)} collective-permute-done((bf16[192,192]{1,0:T(8,128)(2,1)S(1)}, bf16[192,192]{1,0:T(8,128)(2,1)S(1)}, u32[]{:S(2)}, u32[]{:S(2)}) %collective-permute-start.47) | collective-permute-done | bytes 73760 | tf_op jit(solution)/shard_map/ppermute | solution.py:983
  288.8 2.0 collective-permute-start.50
  290.8 2.8 collective-permute-done.55
  (306 shorter events, 59.1 us)
Async XLA Ops:
  12.3 13.2 %collective-permute-start.1 = (bf16[3,192,384]{2,1,0:T(8,128)(2,1)S(1)}, bf16[3,192,384]{2,1,0:T(8,128)(2,1)S(1)}, u32[]{:S(2)}, u32[]{:S(2)}) collective-permute-start(bf16[3,192,384]{2,1,0:T(8,128)(2,1)S(1)} %pad_maximum_fusion.4.refs_4_.refs_9_), channel_id=1, source_target_pairs={{0,16},{8,24},{16,0},{24,8},{1,17},{9,25},{17,1},{25,9},{2,18},{10... | collective-permute-start | bytes 1327112 | tf_op jit(solution)/shard_map/ppermute | solution.py:979
  15.3 22.8 %collective-permute-start = (bf16[592,384]{1,0:T(8,128)(2,1)}, bf16[592,384]{1,0:T(8,128)(2,1)}, u32[]{:S(2)}, u32[]{:S(2)}) collective-permute-start(bf16[592,384]{1,0:T(8,128)(2,1)} %fusion.12), channel_id=1, source_target_pairs={{0,2},{1,3},{2,0},{3,1},{4,6},{5,7},{6,4},{7,5},{8,10},{9,11},{10,... | collective-permute-start | bytes 1363976 | tf_op jit(solution)/shard_map/ppermute | solution.py:983
  17.9 8.5 %collective-permute-start.2 = (bf16[3,192,384]{2,1,0:T(8,128)(2,1)S(1)}, bf16[3,192,384]{2,1,0:T(8,128)(2,1)S(1)}, u32[]{:S(2)}, u32[]{:S(2)}) collective-permute-start(bf16[3,192,384]{2,1,0:T(8,128)(2,1)S(1)} %pad_maximum_fusion.4.refs_4_.refs_9_), channel_id=1, source_target_pairs={{0,8},{8,0},{16,24},{24,16},{1,9},{9,1},{17,25},{25,17},{2,10},{10... | collective-permute-start | bytes 1327112 | tf_op jit(solution)/shard_map/ppermute | solution.py:975
  17.9 22.6 %collective-permute-start.4 = (bf16[528,768]{1,0:T(8,128)(2,1)}, bf16[528,768]{1,0:T(8,128)(2,1)}, u32[]{:S(2)}, u32[]{:S(2)}) collective-permute-start(bf16[528,768]{1,0:T(8,128)(2,1)} %fusion.2), channel_id=1, source_target_pairs={{0,4},{4,0},{1,5},{5,1},{2,6},{6,2},{3,7},{7,3},{8,12},{12,8},{9,1... | collective-permute-start | bytes 2433032 | tf_op jit(solution)/shard_map/ppermute | solution.py:971
  25.5 1.8 collective-permute-start.3
  39.3 21.2 %collective-permute-start.7 = (bf16[2,592,384]{2,1,0:T(8,128)(2,1)S(1)}, bf16[2,592,384]{2,1,0:T(8,128)(2,1)}, u32[]{:S(2)}, u32[]{:S(2)}) collective-permute-start(bf16[2,592,384]{2,1,0:T(8,128)(2,1)S(1)} %pad_maximum_fusion.refs_0_.refs_5_.refs_2_), channel_id=1, source_target_pairs={{0,16},{8,24},{16,0},{24,8},{1,17},{9,25},{17,1},{25,9},{2,18},{10... | collective-permute-start | bytes 2727944 | tf_op jit(solution)/shard_map/ppermute | solution.py:979
  39.8 20.9 %collective-permute-start.6 = (bf16[2,592,384]{2,1,0:T(8,128)(2,1)S(1)}, bf16[2,592,384]{2,1,0:T(8,128)(2,1)}, u32[]{:S(2)}, u32[]{:S(2)}) collective-permute-start(bf16[2,592,384]{2,1,0:T(8,128)(2,1)S(1)} %pad_maximum_fusion.refs_0_.refs_5_.refs_2_), channel_id=1, source_target_pairs={{0,1},{1,0},{2,3},{3,2},{4,5},{5,4},{6,7},{7,6},{8,9},{9,8},{10,11... | collective-permute-start | bytes 2727944 | tf_op jit(solution)/shard_map/ppermute | solution.py:983
  40.5 27.6 %collective-permute-start.5 = (bf16[2,592,384]{2,1,0:T(8,128)(2,1)S(1)}, bf16[2,592,384]{2,1,0:T(8,128)(2,1)}, u32[]{:S(2)}, u32[]{:S(2)}) collective-permute-start(bf16[2,592,384]{2,1,0:T(8,128)(2,1)S(1)} %pad_maximum_fusion.refs_0_.refs_5_.refs_2_), channel_id=1, source_target_pairs={{0,8},{8,0},{16,24},{24,16},{1,9},{9,1},{17,25},{25,17},{2,10},{10... | collective-permute-start | bytes 2727944 | tf_op jit(solution)/shard_map/ppermute | solution.py:975
  45.9 22.3 %copy-start.13 = (bf16[3,192,384]{2,1,0:T(8,128)(2,1)S(1)}, bf16[3,192,384]{2,1,0:T(8,128)(2,1)}, u32[]{:S(2)}) copy-start(bf16[3,192,384]{2,1,0:T(8,128)(2,1)} %copy-done.12) | copy-start | bytes 1327108
  55.8 22.6 %copy-start.40 = (bf16[3,3,1024,64]{3,2,1,0:T(8,128)(2,1)}, bf16[3,3,1024,64]{3,2,1,0:T(8,128)(2,1)S(1)}, u32[]{:S(2)}) copy-start(bf16[3,3,1024,64]{3,2,1,0:T(8,128)(2,1)S(1)} %get-tuple-element.180.refs_3_) | copy-start | bytes 3538948
  55.8 22.6 %copy-start.42 = (bf16[512,768]{1,0:T(8,128)(2,1)}, bf16[512,768]{1,0:T(8,128)(2,1)S(1)}, u32[]{:S(2)}) copy-start(bf16[512,768]{1,0:T(8,128)(2,1)S(1)} %get-tuple-element.194.refs_9_) | copy-start | bytes 2359300
  55.8 22.6 %copy-start.44 = (f32[192,1024]{1,0:T(8,128)}, f32[192,1024]{1,0:T(8,128)S(1)}, u32[]{:S(2)}) copy-start(f32[192,1024]{1,0:T(8,128)S(1)} %get-tuple-element.181.refs_5_) | copy-start | bytes 2359300
  55.8 22.6 %copy-start.46 = (f32[8,1024]{1,0:T(8,128)}, f32[8,1024]{1,0:T(8,128)S(1)}, u32[]{:S(2)}) copy-start(f32[8,1024]{1,0:T(8,128)S(1)} %get-tuple-element.119.refs_0_.refs_6_) | copy-start | bytes 98308
  55.8 31.9 %copy-start.19 = (bf16[128,384]{1,0:T(8,128)(2,1)}, bf16[128,384]{1,0:T(8,128)(2,1)S(1)}, u32[]{:S(2)}) copy-start(bf16[128,384]{1,0:T(8,128)(2,1)S(1)} %get-tuple-element.125.refs_1_.refs_4_) | copy-start | bytes 294916
  60.7 7.5 %collective-permute-start.8 = (bf16[2,592,384]{2,1,0:T(8,128)(2,1)}, bf16[2,592,384]{2,1,0:T(8,128)(2,1)S(1)}, u32[]{:S(2)}, u32[]{:S(2)}) collective-permute-start(bf16[2,592,384]{2,1,0:T(8,128)(2,1)} %collective-permute-done.7.refs_6_.refs_3_), channel_id=1, source_target_pairs={{0,8},{8,0},{16,24},{24,16},{1,9},{9,1},{17,25},{25,17},{2,10},{10... | collective-permute-start | bytes 2727944 | tf_op jit(solution)/shard_map/ppermute | solution.py:975
  60.7 22.9 %collective-permute-start.12 = (bf16[2,592,384]{2,1,0:T(8,128)(2,1)}, bf16[2,592,384]{2,1,0:T(8,128)(2,1)}, u32[]{:S(2)}, u32[]{:S(2)}) collective-permute-start(bf16[2,592,384]{2,1,0:T(8,128)(2,1)} %collective-permute-done.6.refs_9_.refs_6_), channel_id=1, source_target_pairs={{0,16},{8,24},{16,0},{24,8},{1,17},{9,25},{17,1},{25,9},{2,18},{10... | collective-permute-start | bytes 2727944 | tf_op jit(solution)/shard_map/ppermute | solution.py:979
  63.0 16.1 %collective-permute-start.9 = (bf16[128,384]{1,0:T(8,128)(2,1)S(1)}, bf16[128,384]{1,0:T(8,128)(2,1)S(1)}, u32[]{:S(2)}, u32[]{:S(2)}) collective-permute-start(bf16[128,384]{1,0:T(8,128)(2,1)S(1)} %get-tuple-element.122), channel_id=1, source_target_pairs={{0,1},{1,0},{2,3},{3,2},{4,5},{5,4},{6,7},{7,6},{8,9},{9,8},{10,11... | collective-permute-start | bytes 294920 | tf_op jit(solution)/shard_map/ppermute | solution.py:983
  64.8 14.3 %collective-permute-start.10 = (bf16[128,384]{1,0:T(8,128)(2,1)S(1)}, bf16[128,384]{1,0:T(8,128)(2,1)S(1)}, u32[]{:S(2)}, u32[]{:S(2)}) collective-permute-start(bf16[128,384]{1,0:T(8,128)(2,1)S(1)} %get-tuple-element.123), channel_id=1, source_target_pairs={{0,2},{1,3},{2,0},{3,1},{4,6},{5,7},{6,4},{7,5},{8,10},{9,11},{10,... | collective-permute-start | bytes 294920 | tf_op jit(solution)/shard_map/ppermute | solution.py:983
  68.2 11.0 %collective-permute-start.11 = (bf16[128,384]{1,0:T(8,128)(2,1)S(1)}, bf16[128,384]{1,0:T(8,128)(2,1)S(1)}, u32[]{:S(2)}, u32[]{:S(2)}) collective-permute-start(bf16[128,384]{1,0:T(8,128)(2,1)S(1)} %get-tuple-element.124), channel_id=1, source_target_pairs={{0,3},{1,2},{2,1},{3,0},{4,7},{5,6},{6,5},{7,4},{8,11},{9,10},{10,... | collective-permute-start | bytes 294920 | tf_op jit(solution)/shard_map/ppermute | solution.py:983
  83.6 4.1 %collective-permute-start.13 = (bf16[2,592,384]{2,1,0:T(8,128)(2,1)}, bf16[2,592,384]{2,1,0:T(8,128)(2,1)}, u32[]{:S(2)}, u32[]{:S(2)}) collective-permute-start(bf16[2,592,384]{2,1,0:T(8,128)(2,1)} %collective-permute-done.6.refs_9_.refs_6_), channel_id=1, source_target_pairs={{0,8},{8,0},{16,24},{24,16},{1,9},{9,1},{17,25},{25,17},{2,10},{10... | collective-permute-start | bytes 2727944 | tf_op jit(solution)/shard_map/ppermute | solution.py:975
  83.6 4.1 %collective-permute-start.14 = (bf16[2,592,384]{2,1,0:T(8,128)(2,1)}, bf16[2,592,384]{2,1,0:T(8,128)(2,1)}, u32[]{:S(2)}, u32[]{:S(2)}) collective-permute-start(bf16[2,592,384]{2,1,0:T(8,128)(2,1)} %collective-permute-done.12.refs_10_.refs_7_), channel_id=1, source_target_pairs={{0,8},{8,0},{16,24},{24,16},{1,9},{9,1},{17,25},{25,17},{2,10},{10... | collective-permute-start | bytes 2727944 | tf_op jit(solution)/shard_map/ppermute | solution.py:975
  84.3 22.0 %collective-permute-start.21 = (bf16[384,384]{1,0:T(8,128)(2,1)}, bf16[384,384]{1,0:T(8,128)(2,1)S(1)}, u32[]{:S(2)}, u32[]{:S(2)}) collective-permute-start(bf16[384,384]{1,0:T(8,128)(2,1)} %pad_maximum_fusion.7), channel_id=1, source_target_pairs={{0,2},{1,3},{2,0},{3,1},{4,6},{5,7},{6,4},{7,5},{8,10},{9,11},{10,... | collective-permute-start | bytes 884744 | tf_op jit(solution)/shard_map/ppermute | solution.py:983
  92.8 13.6 %collective-permute-start.15 = (bf16[128,384]{1,0:T(8,128)(2,1)S(1)}, bf16[128,384]{1,0:T(8,128)(2,1)S(1)}, u32[]{:S(2)}, u32[]{:S(2)}) collective-permute-start(bf16[128,384]{1,0:T(8,128)(2,1)S(1)} %copy-done.35), channel_id=1, source_target_pairs={{0,1},{1,0},{2,3},{3,2},{4,5},{5,4},{6,7},{7,6},{8,9},{9,8},{10,11... | collective-permute-start | bytes 294920 | tf_op jit(solution)/shard_map/ppermute | solution.py:983
  94.6 13.9 %collective-permute-start.16 = (bf16[128,384]{1,0:T(8,128)(2,1)S(1)}, bf16[128,384]{1,0:T(8,128)(2,1)S(1)}, u32[]{:S(2)}, u32[]{:S(2)}) collective-permute-start(bf16[128,384]{1,0:T(8,128)(2,1)S(1)} %copy-done.33), channel_id=1, source_target_pairs={{0,2},{1,3},{2,0},{3,1},{4,6},{5,7},{6,4},{7,5},{8,10},{9,11},{10,... | collective-permute-start | bytes 294920 | tf_op jit(solution)/shard_map/ppermute | solution.py:983
  97.9 10.6 %collective-permute-start.17 = (bf16[128,384]{1,0:T(8,128)(2,1)S(1)}, bf16[128,384]{1,0:T(8,128)(2,1)S(1)}, u32[]{:S(2)}, u32[]{:S(2)}) collective-permute-start(bf16[128,384]{1,0:T(8,128)(2,1)S(1)} %copy-done.31), channel_id=1, source_target_pairs={{0,3},{1,2},{2,1},{3,0},{4,7},{5,6},{6,5},{7,4},{8,11},{9,10},{10,... | collective-permute-start | bytes 294920 | tf_op jit(solution)/shard_map/ppermute | solution.py:983
  97.9 16.0 %collective-permute-start.18 = (bf16[384,768]{1,0:T(8,128)(2,1)S(1)}, bf16[384,768]{1,0:T(8,128)(2,1)S(1)}, u32[]{:S(2)}, u32[]{:S(2)}) collective-permute-start(bf16[384,768]{1,0:T(8,128)(2,1)S(1)} %get-tuple-element.134.refs_1_), channel_id=1, source_target_pairs={{0,4},{4,0},{1,5},{5,1},{2,6},{6,2},{3,7},{7,3},{8,12},{12,8},{9,1... | collective-permute-start | bytes 1769480 | tf_op jit(solution)/shard_map/ppermute | solution.py:971
  108.5 15.8 %collective-permute-start.25 = (bf16[2,384,384]{2,1,0:T(8,128)(2,1)S(1)}, bf16[2,384,384]{2,1,0:T(8,128)(2,1)S(1)}, u32[]{:S(2)}, u32[]{:S(2)}) collective-permute-start(bf16[2,384,384]{2,1,0:T(8,128)(2,1)S(1)} %pad_maximum_fusion.2.refs_2_), channel_id=1, source_target_pairs={{0,1},{1,0},{2,3},{3,2},{4,5},{5,4},{6,7},{7,6},{8,9},{9,8},{10,11... | collective-permute-start | bytes 1769480 | tf_op jit(solution)/shard_map/ppermute | solution.py:983
  110.8 25.3 %collective-permute-start.22 = (bf16[2,384,384]{2,1,0:T(8,128)(2,1)S(1)}, bf16[2,384,384]{2,1,0:T(8,128)(2,1)S(1)}, u32[]{:S(2)}, u32[]{:S(2)}) collective-permute-start(bf16[2,384,384]{2,1,0:T(8,128)(2,1)S(1)} %pad_maximum_fusion.2.refs_2_), channel_id=1, source_target_pairs={{0,16},{8,24},{16,0},{24,8},{1,17},{9,25},{17,1},{25,9},{2,18},{10... | collective-permute-start | bytes 1769480 | tf_op jit(solution)/shard_map/ppermute | solution.py:979
  124.3 14.7 %collective-permute-start.26 = (bf16[2,384,384]{2,1,0:T(8,128)(2,1)S(1)}, bf16[2,384,384]{2,1,0:T(8,128)(2,1)S(1)}, u32[]{:S(2)}, u32[]{:S(2)}) collective-permute-start(bf16[2,384,384]{2,1,0:T(8,128)(2,1)S(1)} %collective-permute-done.25.refs_6_), channel_id=1, source_target_pairs={{0,16},{8,24},{16,0},{24,8},{1,17},{9,25},{17,1},{25,9},{2,18},{10... | collective-permute-start | bytes 1769480 | tf_op jit(solution)/shard_map/ppermute | solution.py:979
  125.8 10.2 %collective-permute-start.20 = (bf16[256,768]{1,0:T(8,128)(2,1)S(1)}, bf16[256,768]{1,0:T(8,128)(2,1)S(1)}, u32[]{:S(2)}, u32[]{:S(2)}) collective-permute-start(bf16[256,768]{1,0:T(8,128)(2,1)S(1)} %get-tuple-element.150.refs_1_), channel_id=1, source_target_pairs={{0,4},{4,0},{1,5},{5,1},{2,6},{6,2},{3,7},{7,3},{8,12},{12,8},{9,1... | collective-permute-start | bytes 1179656 | tf_op jit(solution)/shard_map/ppermute | solution.py:971
  127.3 13.2 %collective-permute-start.23 = (bf16[2,384,384]{2,1,0:T(8,128)(2,1)S(1)}, bf16[2,384,384]{2,1,0:T(8,128)(2,1)S(1)}, u32[]{:S(2)}, u32[]{:S(2)}) collective-permute-start(bf16[2,384,384]{2,1,0:T(8,128)(2,1)S(1)} %pad_maximum_fusion.2.refs_2_), channel_id=1, source_target_pairs={{0,8},{8,0},{16,24},{24,16},{1,9},{9,1},{17,25},{25,17},{2,10},{10... | collective-permute-start | bytes 1769480 | tf_op jit(solution)/shard_map/ppermute | solution.py:975
  127.3 13.2 %collective-permute-start.27 = (bf16[2,384,384]{2,1,0:T(8,128)(2,1)S(1)}, bf16[2,384,384]{2,1,0:T(8,128)(2,1)S(1)}, u32[]{:S(2)}, u32[]{:S(2)}) collective-permute-start(bf16[2,384,384]{2,1,0:T(8,128)(2,1)S(1)} %collective-permute-done.25.refs_6_), channel_id=1, source_target_pairs={{0,8},{8,0},{16,24},{24,16},{1,9},{9,1},{17,25},{25,17},{2,10},{10... | collective-permute-start | bytes 1769480 | tf_op jit(solution)/shard_map/ppermute | solution.py:975
  136.1 4.5 %collective-permute-start.24 = (bf16[2,384,384]{2,1,0:T(8,128)(2,1)S(1)}, bf16[2,384,384]{2,1,0:T(8,128)(2,1)S(1)}, u32[]{:S(2)}, u32[]{:S(2)}) collective-permute-start(bf16[2,384,384]{2,1,0:T(8,128)(2,1)S(1)} %collective-permute-done.22.refs_3_), channel_id=1, source_target_pairs={{0,8},{8,0},{16,24},{24,16},{1,9},{9,1},{17,25},{25,17},{2,10},{10... | collective-permute-start | bytes 1769480 | tf_op jit(solution)/shard_map/ppermute | solution.py:975
  139.0 2.0 collective-permute-start.28
  139.0 11.9 %collective-permute-start.19 = (bf16[256,768]{1,0:T(8,128)(2,1)S(1)}, bf16[256,768]{1,0:T(8,128)(2,1)S(1)}, u32[]{:S(2)}, u32[]{:S(2)}) collective-permute-start(bf16[256,768]{1,0:T(8,128)(2,1)S(1)} %get-tuple-element.147), channel_id=1, source_target_pairs={{0,4},{4,0},{1,5},{5,1},{2,6},{6,2},{3,7},{7,3},{8,12},{12,8},{9,1... | collective-permute-start | bytes 1179656 | tf_op jit(solution)/shard_map/ppermute | solution.py:971
  144.3 14.7 %collective-permute-start.29 = (bf16[256,768]{1,0:T(8,128)(2,1)S(1)}, bf16[256,768]{1,0:T(8,128)(2,1)S(1)}, u32[]{:S(2)}, u32[]{:S(2)}) collective-permute-start(bf16[256,768]{1,0:T(8,128)(2,1)S(1)} %get-tuple-element.155.refs_0_), channel_id=1, source_target_pairs={{0,4},{4,0},{1,5},{5,1},{2,6},{6,2},{3,7},{7,3},{8,12},{12,8},{9,1... | collective-permute-start | bytes 1179656 | tf_op jit(solution)/shard_map/ppermute | solution.py:971
  161.6 10.7 %collective-permute-start.30 = (bf16[256,768]{1,0:T(8,128)(2,1)S(1)}, bf16[256,768]{1,0:T(8,128)(2,1)S(1)}, u32[]{:S(2)}, u32[]{:S(2)}) collective-permute-start(bf16[256,768]{1,0:T(8,128)(2,1)S(1)} %get-tuple-element.160.refs_1_.refs_0_), channel_id=1, source_target_pairs={{0,4},{4,0},{1,5},{5,1},{2,6},{6,2},{3,7},{7,3},{8,12},{12,8},{9,1... | collective-permute-start | bytes 1179656 | tf_op jit(solution)/shard_map/ppermute | solution.py:971
  174.8 9.9 %collective-permute-start.32 = (bf16[256,768]{1,0:T(8,128)(2,1)S(1)}, bf16[256,768]{1,0:T(8,128)(2,1)S(1)}, u32[]{:S(2)}, u32[]{:S(2)}) collective-permute-start(bf16[256,768]{1,0:T(8,128)(2,1)S(1)} %get-tuple-element.170), channel_id=1, source_target_pairs={{0,4},{4,0},{1,5},{5,1},{2,6},{6,2},{3,7},{7,3},{8,12},{12,8},{9,1... | collective-permute-start | bytes 1179656 | tf_op jit(solution)/shard_map/ppermute | solution.py:971
  178.8 15.6 %collective-permute-start.31 = (bf16[2,4,192,384]{3,2,1,0:T(8,128)(2,1)S(1)}, bf16[2,4,192,384]{3,2,1,0:T(8,128)(2,1)S(1)}, u32[]{:S(2)}, u32[]{:S(2)}) collective-permute-start(bf16[2,4,192,384]{3,2,1,0:T(8,128)(2,1)S(1)} %get-tuple-element.166.refs_0_), channel_id=1, source_target_pairs={{0,8},{8,0},{16,24},{24,16},{1,9},{9,1},{17,25},{25,17},{2,10},{10... | collective-permute-start | bytes 3538952 | tf_op jit(solution)/shard_map/ppermute | solution.py:975
  188.9 7.3 %collective-permute-start.33 = (bf16[2,4,192,384]{3,2,1,0:T(8,128)(2,1)S(1)}, bf16[2,4,192,384]{3,2,1,0:T(8,128)(2,1)S(1)}, u32[]{:S(2)}, u32[]{:S(2)}) collective-permute-start(bf16[2,4,192,384]{3,2,1,0:T(8,128)(2,1)S(1)} %get-tuple-element.176), channel_id=1, source_target_pairs={{0,8},{8,0},{16,24},{24,16},{1,9},{9,1},{17,25},{25,17},{2,10},{10... | collective-permute-start | bytes 3538952 | tf_op jit(solution)/shard_map/ppermute | solution.py:975
  189.0 8.0 %collective-permute-start.34 = (bf16[128,384]{1,0:T(8,128)(2,1)S(1)}, bf16[128,384]{1,0:T(8,128)(2,1)S(1)}, u32[]{:S(2)}, u32[]{:S(2)}) collective-permute-start(bf16[128,384]{1,0:T(8,128)(2,1)S(1)} %get-tuple-element.183), channel_id=1, source_target_pairs={{0,1},{1,0},{2,3},{3,2},{4,5},{5,4},{6,7},{7,6},{8,9},{9,8},{10,11... | collective-permute-start | bytes 294920 | tf_op jit(solution)/shard_map/ppermute | solution.py:983
  190.5 6.5 %collective-permute-start.35 = (bf16[128,384]{1,0:T(8,128)(2,1)S(1)}, bf16[128,384]{1,0:T(8,128)(2,1)S(1)}, u32[]{:S(2)}, u32[]{:S(2)}) collective-permute-start(bf16[128,384]{1,0:T(8,128)(2,1)S(1)} %get-tuple-element.184), channel_id=1, source_target_pairs={{0,2},{1,3},{2,0},{3,1},{4,6},{5,7},{6,4},{7,5},{8,10},{9,11},{10,... | collective-permute-start | bytes 294920 | tf_op jit(solution)/shard_map/ppermute | solution.py:983
  193.0 8.3 %collective-permute-start.36 = (bf16[128,384]{1,0:T(8,128)(2,1)S(1)}, bf16[128,384]{1,0:T(8,128)(2,1)S(1)}, u32[]{:S(2)}, u32[]{:S(2)}) collective-permute-start(bf16[128,384]{1,0:T(8,128)(2,1)S(1)} %get-tuple-element.185), channel_id=1, source_target_pairs={{0,3},{1,2},{2,1},{3,0},{4,7},{5,6},{6,5},{7,4},{8,11},{9,10},{10,... | collective-permute-start | bytes 294920 | tf_op jit(solution)/shard_map/ppermute | solution.py:983
  194.6 23.2 %collective-permute-start.38 = (bf16[4,192,384]{2,1,0:T(8,128)(2,1)S(1)}, bf16[4,192,384]{2,1,0:T(8,128)(2,1)S(1)}, u32[]{:S(2)}, u32[]{:S(2)}) collective-permute-start(bf16[4,192,384]{2,1,0:T(8,128)(2,1)S(1)} %fusion.4.refs_0_), channel_id=1, source_target_pairs={{0,16},{8,24},{16,0},{24,8},{1,17},{9,25},{17,1},{25,9},{2,18},{10... | collective-permute-start | bytes 1769480 | tf_op jit(solution)/shard_map/ppermute | solution.py:979
  196.3 26.1 %collective-permute-start.39 = (bf16[4,192,384]{2,1,0:T(8,128)(2,1)S(1)}, bf16[4,192,384]{2,1,0:T(8,128)(2,1)S(1)}, u32[]{:S(2)}, u32[]{:S(2)}) collective-permute-start(bf16[4,192,384]{2,1,0:T(8,128)(2,1)S(1)} %fusion.5.refs_1_), channel_id=1, source_target_pairs={{0,16},{8,24},{16,0},{24,8},{1,17},{9,25},{17,1},{25,9},{2,18},{10... | collective-permute-start | bytes 1769480 | tf_op jit(solution)/shard_map/ppermute | solution.py:979
  201.3 21.1 %copy-start.15 = (bf16[128,384]{1,0:T(8,128)(2,1)S(1)}, bf16[128,384]{1,0:T(8,128)(2,1)}, u32[]{:S(2)}) copy-start(bf16[128,384]{1,0:T(8,128)(2,1)} %copy-done.14) | copy-start | bytes 294916
  201.3 21.1 %copy-start.20 = (bf16[128,384]{1,0:T(8,128)(2,1)S(1)}, bf16[128,384]{1,0:T(8,128)(2,1)}, u32[]{:S(2)}) copy-start(bf16[128,384]{1,0:T(8,128)(2,1)} %copy-done.19) | copy-start | bytes 294916
  215.7 27.9 %collective-permute-start.37 = (bf16[128,768]{1,0:T(8,128)(2,1)}, bf16[128,768]{1,0:T(8,128)(2,1)}, u32[]{:S(2)}, u32[]{:S(2)}) collective-permute-start(bf16[128,768]{1,0:T(8,128)(2,1)} %get-tuple-element.187), channel_id=1, source_target_pairs={{0,4},{4,0},{1,5},{5,1},{2,6},{6,2},{3,7},{7,3},{8,12},{12,8},{9,1... | collective-permute-start | bytes 589832 | tf_op jit(solution)/shard_map/ppermute | solution.py:971
  215.8 17.9 %collective-permute-start.40 = (bf16[2,2,128,768]{3,2,1,0:T(8,128)(2,1)S(1)}, bf16[2,2,128,768]{3,2,1,0:T(8,128)(2,1)S(1)}, u32[]{:S(2)}, u32[]{:S(2)}) collective-permute-start(bf16[2,2,128,768]{3,2,1,0:T(8,128)(2,1)S(1)} %get-tuple-element.191.refs_0_), channel_id=1, source_target_pairs={{0,1},{1,0},{2,3},{3,2},{4,5},{5,4},{6,7},{7,6},{8,9},{9,8},{10,11... | collective-permute-start | bytes 2359304 | tf_op jit(solution)/shard_map/ppermute | solution.py:983
  225.3 11.0 %collective-permute-start.42 = (bf16[2,784,384]{2,1,0:T(8,128)(2,1)S(1)}, bf16[2,784,384]{2,1,0:T(8,128)(2,1)S(1)}, u32[]{:S(2)}, u32[]{:S(2)}) collective-permute-start(bf16[2,784,384]{2,1,0:T(8,128)(2,1)S(1)} %get-tuple-element.196), channel_id=1, source_target_pairs={{0,8},{8,0},{16,24},{24,16},{1,9},{9,1},{17,25},{25,17},{2,10},{10... | collective-permute-start | bytes 3612680 | tf_op jit(solution)/shard_map/ppermute | solution.py:975
  234.5 13.0 %collective-permute-start.41 = (bf16[2,2,192,384]{3,2,1,0:T(8,128)(2,1)}, bf16[2,2,192,384]{3,2,1,0:T(8,128)(2,1)}, u32[]{:S(2)}, u32[]{:S(2)}) collective-permute-start(bf16[2,2,192,384]{3,2,1,0:T(8,128)(2,1)} %pad_maximum_fusion.3), channel_id=1, source_target_pairs={{0,1},{1,0},{2,3},{3,2},{4,5},{5,4},{6,7},{7,6},{8,9},{9,8},{10,11... | collective-permute-start | bytes 1769480 | tf_op jit(solution)/shard_map/ppermute | solution.py:983
  237.5 27.1 %collective-permute-start.43 = (bf16[784,384]{1,0:T(8,128)(2,1)}, bf16[784,384]{1,0:T(8,128)(2,1)}, u32[]{:S(2)}, u32[]{:S(2)}) collective-permute-start(bf16[784,384]{1,0:T(8,128)(2,1)} %fusion.3), channel_id=1, source_target_pairs={{0,16},{8,24},{16,0},{24,8},{1,17},{9,25},{17,1},{25,9},{2,18},{10... | collective-permute-start | bytes 1806344 | tf_op jit(solution)/shard_map/ppermute | solution.py:979
  241.8 1.2 collective-permute-start.51
  243.0 4.2 %collective-permute-start.52 = (f32[16,768]{1,0:T(8,128)S(1)}, f32[16,768]{1,0:T(8,128)S(1)}, u32[]{:S(2)}, u32[]{:S(2)}) collective-permute-start(f32[16,768]{1,0:T(8,128)S(1)} %add.140), channel_id=1, source_target_pairs={{0,4},{4,0},{1,5},{5,1},{2,6},{6,2},{3,7},{7,3},{8,12},{12,8},{9,1... | collective-permute-start | bytes 147464 | tf_op jit(solution)/shard_map/ppermute | solution.py:971
  244.6 22.1 %collective-permute-start.44 = (bf16[2,128,768]{2,1,0:T(8,128)(2,1)}, bf16[2,128,768]{2,1,0:T(8,128)(2,1)S(1)}, u32[]{:S(2)}, u32[]{:S(2)}) collective-permute-start(bf16[2,128,768]{2,1,0:T(8,128)(2,1)} %fusion.15), channel_id=1, source_target_pairs={{0,2},{1,3},{2,0},{3,1},{4,6},{5,7},{6,4},{7,5},{8,10},{9,11},{10,... | collective-permute-start | bytes 1179656 | tf_op jit(solution)/shard_map/ppermute | solution.py:983
  249.2 17.5 %collective-permute-start.53 = (f32[16,768]{1,0:T(8,128)S(1)}, f32[16,768]{1,0:T(8,128)S(1)}, u32[]{:S(2)}, u32[]{:S(2)}) collective-permute-start(f32[16,768]{1,0:T(8,128)S(1)} %add.141), channel_id=1, source_target_pairs={{0,16},{8,24},{16,0},{24,8},{1,17},{9,25},{17,1},{25,9},{2,18},{10... | collective-permute-start | bytes 147464 | tf_op jit(solution)/shard_map/ppermute | solution.py:979
  266.0 6.2 %collective-permute-start.46 = (bf16[192,384]{1,0:T(8,128)(2,1)S(1)}, bf16[192,384]{1,0:T(8,128)(2,1)S(1)}, u32[]{:S(2)}, u32[]{:S(2)}) collective-permute-start(bf16[192,384]{1,0:T(8,128)(2,1)S(1)} %get-tuple-element.267), channel_id=1, source_target_pairs={{0,1},{1,0},{2,3},{3,2},{4,5},{5,4},{6,7},{7,6},{8,9},{9,8},{10,11... | collective-permute-start | bytes 442376 | tf_op jit(solution)/shard_map/ppermute | solution.py:983
  266.7 5.5 %collective-permute-start.54 = (f32[16,768]{1,0:T(8,128)S(1)}, f32[16,768]{1,0:T(8,128)S(1)}, u32[]{:S(2)}, u32[]{:S(2)}) collective-permute-start(f32[16,768]{1,0:T(8,128)S(1)} %add.142), channel_id=1, source_target_pairs={{0,1},{1,0},{2,3},{3,2},{4,5},{5,4},{6,7},{7,6},{8,9},{9,8},{10,11... | collective-permute-start | bytes 147464 | tf_op jit(solution)/shard_map/ppermute | solution.py:983
  269.4 19.0 %collective-permute-start.49 = (bf16[2,192,384]{2,1,0:T(8,128)(2,1)S(1)}, bf16[2,192,384]{2,1,0:T(8,128)(2,1)S(1)}, u32[]{:S(2)}, u32[]{:S(2)}) collective-permute-start(bf16[2,192,384]{2,1,0:T(8,128)(2,1)S(1)} %pad_maximum_fusion.8.refs_0_), channel_id=1, source_target_pairs={{0,2},{1,3},{2,0},{3,1},{4,6},{5,7},{6,4},{7,5},{8,10},{9,11},{10,... | collective-permute-start | bytes 884744 | tf_op jit(solution)/shard_map/ppermute | solution.py:983
  270.8 6.3 %collective-permute-start.45 = (bf16[128,768]{1,0:T(8,128)(2,1)S(1)}, bf16[128,768]{1,0:T(8,128)(2,1)S(1)}, u32[]{:S(2)}, u32[]{:S(2)}) collective-permute-start(bf16[128,768]{1,0:T(8,128)(2,1)S(1)} %get-tuple-element.204), channel_id=1, source_target_pairs={{0,4},{4,0},{1,5},{5,1},{2,6},{6,2},{3,7},{7,3},{8,12},{12,8},{9,1... | collective-permute-start | bytes 589832 | tf_op jit(solution)/shard_map/ppermute | solution.py:971
  272.4 16.0 %collective-permute-start.47 = (bf16[192,192]{1,0:T(8,128)(2,1)S(1)}, bf16[192,192]{1,0:T(8,128)(2,1)S(1)}, u32[]{:S(2)}, u32[]{:S(2)}) collective-permute-start(bf16[192,192]{1,0:T(8,128)(2,1)S(1)} %slice.431), channel_id=1, source_target_pairs={{0,2},{1,3},{2,0},{3,1},{4,6},{5,7},{6,4},{7,5},{8,10},{9,11},{10,... | collective-permute-start | bytes 221192 | tf_op jit(solution)/shard_map/ppermute | solution.py:983
  288.6 5.1 %collective-permute-start.55 = (f32[16,768]{1,0:T(8,128)S(1)}, f32[16,768]{1,0:T(8,128)S(1)}, u32[]{:S(2)}, u32[]{:S(2)}) collective-permute-start(f32[16,768]{1,0:T(8,128)S(1)} %add.143), channel_id=1, source_target_pairs={{0,2},{1,3},{2,0},{3,1},{4,6},{5,7},{6,4},{7,5},{8,10},{9,11},{10,... | collective-permute-start | bytes 147464 | tf_op jit(solution)/shard_map/ppermute | solution.py:983
  288.7 13.0 %collective-permute-start.48 = (bf16[400,384]{1,0:T(8,128)(2,1)S(1)}, bf16[400,384]{1,0:T(8,128)(2,1)S(1)}, u32[]{:S(2)}, u32[]{:S(2)}) collective-permute-start(bf16[400,384]{1,0:T(8,128)(2,1)S(1)} %pad_maximum_fusion.6), channel_id=1, source_target_pairs={{0,4},{4,0},{1,5},{5,1},{2,6},{6,2},{3,7},{7,3},{8,12},{12,8},{9,1... | collective-permute-start | bytes 921608 | tf_op jit(solution)/shard_map/ppermute | solution.py:971
  288.8 15.5 %collective-permute-start.50 = (bf16[2,192,384]{2,1,0:T(8,128)(2,1)S(1)}, bf16[2,192,384]{2,1,0:T(8,128)(2,1)S(1)}, u32[]{:S(2)}, u32[]{:S(2)}) collective-permute-start(bf16[2,192,384]{2,1,0:T(8,128)(2,1)S(1)} %fusion.11), channel_id=1, source_target_pairs={{0,4},{4,0},{1,5},{5,1},{2,6},{6,2},{3,7},{7,3},{8,12},{12,8},{9,1... | collective-permute-start | bytes 884744 | tf_op jit(solution)/shard_map/ppermute | solution.py:971
  (60 other events, 399.7 us)
